TPU v7x, 32 devices: a whole 2x2x4 slice. The times are simulated.
32 devices in a mesh: row: 8 (over z, y), rep: 4 (over x, core).
Axes of the slice: x: 2, y: 2, z: 4, core: 2. Of those that a mesh axis runs over, the one named last changes fastest.
Arguments:
- params: float32 [59, 32768], P(None, 'row'), may hold values from -6 to 6, as said below
- first_moment: float32 [59, 32768], P(None, 'row'), may hold values from -6 to 6
- second_moment: float32 [59, 32768], P(None, 'row'), may hold values from 0.01 to 1
- camera: float32 [2, 4, 11], P(None, 'rep'), may hold values from -200 to 200, as said below
- tile_corner: float32 [2, 4, 32, 2], P(None, 'rep', 'row'), may hold values from 0 to 240
- tile_owner: int32 [2, 4, 32, 4], P(None, 'rep', 'row'), may hold values from 0 to 7, all different within a row; in each aligned block of 4 rows (0 to 3, 4 to 7, ..., all dimensions but the last counted through in order) at most 4 rows name the same one
- tile_block: int32 [2, 4, 32, 4], P(None, 'rep', 'row'), may hold values from 0 to 31
- depth_order: int32 [2, 4, 32, 512], P(None, 'rep', 'row'), may hold values from 0 to 511, each once within a row
- targets: float32 [2, 4, 32, 3, 256], P(None, 'rep', 'row'), may hold values from 0 to 1
- migration: int32 [8, 2, 2], P('row'), may hold values from 0 to 31, as said below
Outputs:
- new_params: float32 [59, 32768], P(None, 'row')
- new_first: float32 [59, 32768], P(None, 'row')
- new_second: float32 [59, 32768], P(None, 'row')
- rendered: float32 [2, 4, 32, 3, 256], P(None, 'rep', 'row')
Inputs may be any that keep to these rules, and one draw needn't show every extreme that they name: `tile_owner`: each tile names 4 different owners; among the tiles of one device no owner is named more than 4 times. `depth_order`: each tile's row is a permutation. `migration`: the (4) entries of one owner are different blocks. `params`: row 6 lies in [1, 2]; rows 3 to 5 in [-1.9, -0.7]; row 10 in [2, 4]. `camera`: entries 8 to 10 form a unit vector.
All inputs are finite; a program needn't handle non-finite values.
Results may differ from a plain program's by a relative error of at most 0.0003.
Values sent between devices are 32-bit elements; how exact they have to be, the bound alone decides.
No kernel may reach another device: no remote copies, remote signals or barrier semaphores. Data moves between devices by JAX's collectives and lax.ppermute only.
A program may use at most 64 MiB of HBM per device.

v0:
```python
import math

import jax
import jax.numpy as jnp
from jax import lax
from jax.sharding import PartitionSpec as P

P_SIZE = 59
BLOCK = 128
LISTB = 4
PIX = 256
ITERS = 2
MIGH = 2
DEPTH = 512


harm_zero = 0.28209479177387814
harm_one = 0.4886025119029199
harm_two = (
    1.0925484305920792,
    -1.0925484305920792,
    0.31539156525252005,
    -1.0925484305920792,
    0.5462742152960396,
)
harm_three = (
    -0.5900435899266435,
    2.890611442640554,
    -0.4570457994644658,
    0.3731763325901154,
    -0.4570457994644658,
    1.445305721320277,
    -0.5900435899266435,
)
learn_rate = 0.01
adam_epsilon = 1e-08


def extended(block, sides, width):
    for axis, dim in sides:
        count = lax.axis_size(axis)
        forward = [(i, i + 1) for i in range(count - 1)]
        forward.append((count - 1, 0))
        backward = [(target, source) for source, target in forward]
        low = lax.ppermute(
            lax.slice_in_dim(block, block.shape[dim] - width, None, axis=dim), axis, forward
        )
        high = lax.ppermute(lax.slice_in_dim(block, 0, width, axis=dim), axis, backward)
        block = jnp.concatenate([low, block, high], axis=dim)
    return block


def harmonics(facing):
    face_x, face_y, face_z = (facing[0], facing[1], facing[2])
    face_xx, face_yy, face_zz = (face_x * face_x, face_y * face_y, face_z * face_z)
    terms = [
        harm_zero + 0.0 * face_x,
        -harm_one * face_y,
        harm_one * face_z,
        -harm_one * face_x,
        harm_two[0] * face_x * face_y,
        harm_two[1] * face_y * face_z,
        harm_two[2] * (2.0 * face_zz - face_xx - face_yy),
        harm_two[3] * face_x * face_z,
        harm_two[4] * (face_xx - face_yy),
        harm_three[0] * face_y * (3.0 * face_xx - face_yy),
        harm_three[1] * face_x * face_y * face_z,
        harm_three[2] * face_y * (4.0 * face_zz - face_xx - face_yy),
        harm_three[3] * face_z * (2.0 * face_zz - 3.0 * face_xx - 3.0 * face_yy),
        harm_three[4] * face_x * (4.0 * face_zz - face_xx - face_yy),
        harm_three[5] * face_z * (face_xx - face_yy),
        harm_three[6] * face_x * (face_xx - 3.0 * face_yy),
    ]
    return jnp.stack(terms)


def project(params, camera_now):
    means = params[0:3]
    scales = jnp.exp(params[3:6])
    quats = params[6:10]
    quats = quats / jnp.sqrt(jnp.sum(quats * quats, axis=0, keepdims=True))
    quat_w, quat_x, quat_y, quat_z = (quats[0], quats[1], quats[2], quats[3])
    rotation = [
        [
            1.0 - 2.0 * (quat_y * quat_y + quat_z * quat_z),
            2.0 * (quat_x * quat_y - quat_w * quat_z),
            2.0 * (quat_x * quat_z + quat_w * quat_y),
        ],
        [
            2.0 * (quat_x * quat_y + quat_w * quat_z),
            1.0 - 2.0 * (quat_x * quat_x + quat_z * quat_z),
            2.0 * (quat_y * quat_z - quat_w * quat_x),
        ],
        [
            2.0 * (quat_x * quat_z - quat_w * quat_y),
            2.0 * (quat_y * quat_z + quat_w * quat_x),
            1.0 - 2.0 * (quat_x * quat_x + quat_y * quat_y),
        ],
    ]
    affine = [
        [camera_now[0], camera_now[1], camera_now[2]],
        [camera_now[3], camera_now[4], camera_now[5]],
    ]
    spread = [
        [
            (
                affine[i][0] * rotation[0][k]
                + affine[i][1] * rotation[1][k]
                + affine[i][2] * rotation[2][k]
            )
            * scales[k]
            for k in range(3)
        ]
        for i in range(2)
    ]
    cov_xx = (
        spread[0][0] * spread[0][0]
        + spread[0][1] * spread[0][1]
        + spread[0][2] * spread[0][2]
        + 0.3
    )
    cov_yy = (
        spread[1][0] * spread[1][0]
        + spread[1][1] * spread[1][1]
        + spread[1][2] * spread[1][2]
        + 0.3
    )
    cov_xy = spread[0][0] * spread[1][0] + spread[0][1] * spread[1][1] + spread[0][2] * spread[1][2]
    determinant = cov_xx * cov_yy - cov_xy * cov_xy
    centre_x = (
        affine[0][0] * means[0] + affine[0][1] * means[1] + affine[0][2] * means[2] + camera_now[6]
    )
    centre_y = (
        affine[1][0] * means[0] + affine[1][1] * means[1] + affine[1][2] * means[2] + camera_now[7]
    )
    basis = harmonics(camera_now[8:11])
    colours = 0.5 + jnp.einsum(
        "k,kcg->cg", basis, params[11:59].reshape(16, 3, -1), precision=lax.Precision.HIGHEST
    )
    opacity = jax.nn.sigmoid(params[10])
    geometry = jnp.stack(
        [centre_x, centre_y, cov_yy / determinant, -cov_xy / determinant, cov_xx / determinant]
    )
    return jnp.concatenate([geometry, colours, opacity[None]], axis=0)


def render(splat_rows, corner, strict_upper):
    side = math.isqrt(PIX)
    pixels = jnp.arange(PIX, dtype=jnp.int32)
    pos_x = corner[0] + (pixels % side).astype(jnp.float32) + 0.5
    pos_y = corner[1] + (pixels // side).astype(jnp.float32) + 0.5
    gap_x = pos_x[:, None] - splat_rows[0][None, :]
    gap_y = pos_y[:, None] - splat_rows[1][None, :]
    exponent = 0.5 * (
        splat_rows[2] * gap_x * gap_x
        + 2.0 * splat_rows[3] * gap_x * gap_y
        + splat_rows[4] * gap_y * gap_y
    )
    alphas = splat_rows[8] * jnp.exp(-exponent)
    log_keep = jnp.log1p(-alphas).reshape(PIX, DEPTH // BLOCK, BLOCK)
    inside = jnp.einsum("pbi,ij->pbj", log_keep, strict_upper, precision=lax.Precision.HIGHEST)
    totals = jnp.sum(log_keep, axis=2)
    before = jnp.cumsum(totals, axis=1) - totals
    transmit = jnp.exp(inside + before[:, :, None]).reshape(PIX, DEPTH)
    return jnp.einsum(
        "cn,pn->cp", splat_rows[5:8], alphas * transmit, precision=lax.Precision.HIGHEST
    )


def slot_plan(owner_list, block_list, owners, capacity):
    flat_owner = owner_list.reshape(-1)
    hits = (flat_owner[:, None] == jnp.arange(owners, dtype=jnp.int32)[None, :]).astype(jnp.int32)
    earlier = jnp.cumsum(hits, axis=0) - hits
    rank_in = jnp.sum(earlier * hits, axis=1)
    slot_place = flat_owner * capacity + rank_in
    wanted_list = (
        jnp.full((owners * capacity,), -1, jnp.int32).at[slot_place].set(block_list.reshape(-1))
    )
    return (slot_place, wanted_list)


def serve(projected, asked_blocks, blk_dev):
    grid = projected.reshape(9, blk_dev, BLOCK)
    chosen = jnp.take(grid, jnp.maximum(asked_blocks, 0), axis=1)
    return jnp.where((asked_blocks >= 0)[None, :, None], chosen, 0.0)


def adam_step(values, moment_one, moment_two, gradient):
    moment_one = 0.9 * moment_one + 0.1 * gradient
    moment_two = 0.999 * moment_two + 0.001 * gradient * gradient
    values = values - learn_rate * moment_one / (jnp.sqrt(moment_two) + adam_epsilon)
    return (values, moment_one, moment_two)


def local(
    params,
    first_moment,
    second_moment,
    camera,
    tile_corner,
    tile_owner,
    tile_block,
    depth_order,
    targets,
    migration,
):
    owners = lax.axis_size("row")
    local_gauss = params.shape[1]
    blk_dev = local_gauss // BLOCK
    tiles_dev = tile_owner.shape[2]
    requests = tiles_dev * LISTB
    capacity = max(2, 2 * ((requests + owners - 1) // owners))
    strict_upper = (jnp.arange(BLOCK)[:, None] < jnp.arange(BLOCK)[None, :]).astype(jnp.float32)
    current = params
    share_width = local_gauss // lax.axis_size("rep")
    share_start = lax.axis_index("rep") * share_width
    moment_one = lax.dynamic_slice_in_dim(first_moment, share_start, share_width, 1)
    moment_two = lax.dynamic_slice_in_dim(second_moment, share_start, share_width, 1)
    plans = [
        slot_plan(tile_owner[step_index, 0], tile_block[step_index, 0], owners, capacity)
        for step_index in range(ITERS)
    ]

    def one_tile(splat_rows, corner, target):
        picture, tile_back = jax.vjp(lambda r: render(r, corner, strict_upper), splat_rows)
        return (picture, tile_back(picture - target)[0])

    def paired(array):
        return array.reshape((tiles_dev // 2, 2) + array.shape[1:])

    pictures = []
    for step_index in range(ITERS):
        camera_now = camera[step_index, 0]
        projected, pullback = jax.vjp(lambda p: project(p, camera_now), current)
        slot_place = plans[step_index][0]
        asked_blocks = lax.all_to_all(
            plans[step_index][1], "row", split_axis=0, concat_axis=0, tiled=True
        )
        arrived = lax.all_to_all(
            serve(projected, asked_blocks, blk_dev), "row", split_axis=1, concat_axis=1, tiled=True
        )
        listed = jnp.take(arrived, slot_place, axis=1)
        tile_rows = jnp.transpose(listed.reshape(9, tiles_dev, DEPTH), (1, 0, 2))
        orders = depth_order[step_index, 0]
        sorted_rows = jnp.take_along_axis(tile_rows, orders[:, None, :], axis=2)
        picture, sorted_grads = lax.map(
            lambda pieces: jax.vmap(one_tile)(pieces[0], pieces[1], pieces[2]),
            (
                paired(sorted_rows),
                paired(tile_corner[step_index, 0]),
                paired(targets[step_index, 0]),
            ),
        )
        pictures.append(picture.reshape(tiles_dev, 3, PIX))
        sorted_grads = sorted_grads.reshape(tiles_dev, 9, DEPTH)
        list_grads = jax.vmap(lambda g, o: jnp.zeros_like(g).at[:, o].set(g))(sorted_grads, orders)
        request_grads = jnp.transpose(list_grads, (1, 0, 2)).reshape(9, requests * BLOCK)
        outgoing = (
            jnp.zeros((9, owners * capacity, BLOCK), jnp.float32)
            .at[:, slot_place]
            .set(request_grads.reshape(9, requests, BLOCK))
        )
        returned_grads = lax.all_to_all(outgoing, "row", split_axis=1, concat_axis=1, tiled=True)
        pick_table = (
            asked_blocks[:, None] == jnp.arange(blk_dev, dtype=jnp.int32)[None, :]
        ).astype(jnp.float32)
        row_grads = jnp.einsum(
            "csb,sk->ckb", returned_grads, pick_table, precision=lax.Precision.HIGHEST
        ).reshape(9, local_gauss)
        gradient = pullback(row_grads)[0]
        grad_part = lax.psum_scatter(gradient, "rep", scatter_dimension=1, tiled=True)
        own_params = lax.dynamic_slice_in_dim(current, share_start, share_width, 1)
        own_params, moment_one, moment_two = adam_step(
            own_params, moment_one, moment_two, grad_part
        )
        current = lax.all_gather(own_params, "rep", axis=1, tiled=True)
    moment_one, moment_two = (
        lax.all_gather(moment_one, "rep", axis=1, tiled=True),
        lax.all_gather(moment_two, "rep", axis=1, tiled=True),
    )
    stacked = jnp.stack([current, moment_one, moment_two]).reshape(3, P_SIZE, blk_dev, BLOCK)
    own_list = migration[0]
    leaving = jnp.take(stacked, own_list.reshape(-1), axis=2)
    neighbours = extended(leaving, (("row", 2),), MIGH)
    from_left = neighbours[:, :, 0:MIGH]
    from_right = neighbours[:, :, 3 * MIGH : 4 * MIGH]
    stacked = stacked.at[:, :, own_list[0]].set(from_left)
    stacked = stacked.at[:, :, own_list[1]].set(from_right)
    stacked = stacked.reshape(3, P_SIZE, local_gauss)
    return (stacked[0], stacked[1], stacked[2], jnp.stack(pictures)[:, None])


def solution(mesh):
    return jax.shard_map(
        local,
        mesh=mesh,
        in_specs=(
            P(None, "row"),
            P(None, "row"),
            P(None, "row"),
            P(None, "rep", None),
            P(None, "rep", "row", None),
            P(None, "rep", "row", None),
            P(None, "rep", "row", None),
            P(None, "rep", "row", None),
            P(None, "rep", "row", None, None),
            P("row", None, None),
        ),
        out_specs=(
            P(None, "row"),
            P(None, "row"),
            P(None, "row"),
            P(None, "rep", "row", None, None),
        ),
        check_vma=False,
    )
```

profile of v0, /device:TPU:0, one launch (start us, length us, event | category | flops | bytes accessed | tf_op | source)
XLA Modules:
  0.0 416.8 jit_solution(15263126143303634518)
XLA Ops:
  12.2 7.3 %all-to-all-start = ((s32[8,4,1]{1,2,0:T(1,128)}), s32[8,4,1]{1,2,0:T(1,128)S(1)}, u32[]{:S(2)}, u32[]{:S(2)}) async-start(s32[8,4,1]{1,2,0:T(1,128)} %bitcast.2), calls=%async_computation | async-start | bytes 8192 | tf_op jit(solution)/shard_map/all_to_all | solution.py:236
  50.7 6.2 %add_divide_fusion = (f32[1,4096]{1,0:T(1,128)S(1)}, f32[1,32,128]{2,0,1:T(1,128)S(1)}, f32[1,32,128]{2,0,1:T(1,128)S(1)}) fusion(f32[59,4096]{1,0:T(8,128)} %param.20, f32[]{:T(128)} %bitcast.10, f32[]{:T(128)} %bitcast.9, f32[]{:T(128)} %bitcast.8, f32[]{:T(128)} %bitcast.7, f32[]{:T(128)} %bitcast.15, f32[]{:T(128)} %bitcast.14, f32[]{:T(128)} %bitcast.13, ...), kind=kLoop, calls=%fused_computation.378 | loop fusion | flops 61440 | bytes 114720 | tf_op jit(solution)/shard_map/jvp()/div | solution.py:140
  56.9 4.7 %divide_bitcast_fusion.3 = (f32[1,32,128]{2,0,1:T(1,128)S(1)}, f32[1,4096]{1,0:T(1,128)S(1)}, f32[1,4096]{1,0:T(1,128)}, f32[1,4096]{1,0:T(1,128)S(1)}, f32[1,40...) fusion(f32[3,4096]{1,0:T(4,128)S(1)} %slice_exponential_fusion., ...), kind=kLoop, calls=%fused_computation.398 | loop fusion | flops 319488 | bytes 426032 | tf_op jit(solution)/shard_map/jvp()/concatenate | solution.py:144
  65.8 6.0 %all-to-all-start.1 = ((f32[9,32,128]{2,0,1:T(8,128)}), f32[9,32,128]{2,0,1:T(8,128)S(1)}, u32[]{:S(2)}, u32[]{:S(2)}) async-start(f32[9,32,128]{2,0,1:T(8,128)} %bitcast_select_fusion.1), calls=%async_computation.1 | async-start | bytes 524288 | tf_op jit(solution)/shard_map/all_to_all | solution.py:239
  74.3 6.0 %all-to-all-done.1 = f32[9,32,128]{2,0,1:T(8,128)S(1)} async-done(((f32[9,32,128]{2,0,1:T(8,128)}), f32[9,32,128]{2,0,1:T(8,128)S(1)}, u32[]{:S(2)}, u32[]{:S(2)}) %all-to-all-start.1) | async-done | bytes 147488 | tf_op jit(solution)/shard_map/all_to_all | solution.py:239
  81.4 13.0 %gather_fusion.3 = f32[2048,9]{1,0:T(8,128)S(1)} fusion(f32[4,9,512]{1,2,0:T(8,128)S(1)} %bitcast.496, s32[2048]{0:T(1024)S(1)} %bitcast.490), kind=kCustom, calls=%fused_computation.2.clone | custom fusion | bytes 163840 | tf_op jit(solution)/shard_map/jit(take_along_axis)/gather | solution.py:245
  95.8 35.3 %while.32 = (s32[]{:T(128)}, f32[2,2,3,256]{3,2,1,0:T(4,128)S(1)}, f32[2,2,9,512]{3,2,1,0:T(8,128)}, f32[2,2,9,512]{3,2,1,0:T(8,128)S(1)}, f32[2,2,2]{2,1,0:T(2,...) while((s32[]{:T(128)}, f32[2,2,3,256]{3,2,1,0:T(4,128)S(1)}, ...), condition=%wide.region_15.19_spmd.clone.clone, body=%wide.region_4.18_spmd.clone.clone.sunk | while | flops 868624896 | bytes 34132444 | solution.py:246
  132.3 6.1 %scatter_custom_fusion.6 = f32[9,2048]{0,1:T(8,128)S(1)} fusion(s32[2048]{0:T(1024)} %bitcast.586, f32[2048,9]{1,0:T(8,128)S(1)} %bitcast.515, f32[]{:T(128)} %constant.303.clone.1), kind=kCustom, calls=%fused_computation.228 | custom fusion | bytes 74240
  140.0 11.9 %all_to_all.38 = f32[9,32,128]{2,0,1:T(8,128)S(1)} all-to-all(f32[9,32,128]{2,0,1:T(8,128)S(1)} %scatter_fusion), channel_id=1, replica_groups=mesh['row'=8,'rep'=4] {'row'}, dimensions={1} | all-to-all | bytes 294912 | tf_op jit(solution)/shard_map/all_to_all | solution.py:263
  152.2 3.6 fusion.160
  156.8 4.0 add_add_fusion.19
  160.9 2.6 add_add_fusion.18
  172.3 3.5 all-to-all-start.3
  199.4 10.0 %all_gather.12 = f32[59,4096]{1,0:T(8,128)S(1)} all-gather(f32[59,1024]{1,0:T(8,128)S(1)} %divide_subtract_fusion.1), channel_id=1, replica_groups=mesh['row'=8,'rep'=4] {'rep'}, dimensions={1}, use_global_device_ids=true | all-gather | bytes 1208320 | tf_op jit(solution)/shard_map/all_gather | solution.py:276
  211.7 5.2 %fusion.124 = (f32[1,4096]{1,0:T(1,128)S(1)}, f32[1,32,128]{2,0,1:T(1,128)S(1)}, f32[1,32,128]{2,0,1:T(1,128)S(1)}) fusion(f32[59,4096]{1,0:T(8,128)S(1)} %all_gather.12, f32[]{:T(128)} %bitcast.86, f32[]{:T(128)} %bitcast.85, f32[]{:T(128)} %bitcast.84, f32[]{:T(128)} %bitcast.83, f32[]{:T(128)} %bitcast.91, f32[]{:T(128)} %bitcast.90, f32[]{:T(128)} %bitcast.89, ...), kind=kLoop, calls=%fused_computation.315 | loop fusion | flops 61440 | bytes 114720 | tf_op jit(solution)/shard_map/jvp()/div | solution.py:140
  216.9 4.9 %divide_bitcast_fusion = (f32[1,32,128]{2,0,1:T(1,128)S(1)}, f32[1,4096]{1,0:T(1,128)S(1)}, f32[1,4096]{1,0:T(1,128)}, f32[1,4096]{1,0:T(1,128)S(1)}, f32[1,4096...) fusion(f32[3,4096]{1,0:T(4,128)S(1)} %slice_exponential_fusion,, ...), kind=kLoop, calls=%fused_computation.395 | loop fusion | flops 319488 | bytes 426032 | tf_op jit(solution)/shard_map/jvp()/concatenate | solution.py:144
  223.4 6.0 %all-to-all-start.4 = ((f32[9,32,128]{2,0,1:T(8,128)}), f32[9,32,128]{2,0,1:T(8,128)S(1)}, u32[]{:S(2)}, u32[]{:S(2)}) async-start(f32[9,32,128]{2,0,1:T(8,128)} %bitcast_select_fusion), calls=%async_computation.5 | async-start | bytes 524288 | tf_op jit(solution)/shard_map/all_to_all | solution.py:239
  229.5 9.3 %all-to-all-done.4 = f32[9,32,128]{2,0,1:T(8,128)S(1)} async-done(((f32[9,32,128]{2,0,1:T(8,128)}), f32[9,32,128]{2,0,1:T(8,128)S(1)}, u32[]{:S(2)}, u32[]{:S(2)}) %all-to-all-start.4) | async-done | bytes 147488 | tf_op jit(solution)/shard_map/all_to_all | solution.py:239
  239.9 13.0 %gather_fusion.6 = f32[2048,9]{1,0:T(8,128)S(1)} fusion(f32[4,9,512]{1,2,0:T(8,128)S(1)} %bitcast.498, s32[2048]{0:T(1024)S(1)} %bitcast.489), kind=kCustom, calls=%fused_computation.5.clone | custom fusion | bytes 163840 | tf_op jit(solution)/shard_map/jit(take_along_axis)/gather | solution.py:245
  254.9 34.9 %while.33 = (s32[]{:T(128)}, f32[2,2,3,256]{3,2,1,0:T(4,128)}, f32[2,2,9,512]{3,2,1,0:T(8,128)}, f32[2,2,9,512]{3,2,1,0:T(8,128)S(1)}, f32[2,2,2]{2,1,0:T(2,128)...) while((s32[]{:T(128)}, f32[2,2,3,256]{3,2,1,0:T(4,128)}, ...), condition=%wide.region_35.39_spmd.clone.clone, body=%wide.region_24.38_spmd.clone.clone.sunk | while | flops 868624896 | bytes 34032544 | solution.py:246
  291.1 6.4 %scatter_custom_fusion.7 = f32[9,2048]{0,1:T(8,128)S(1)} fusion(s32[2048]{0:T(1024)} %bitcast.585, f32[2048,9]{1,0:T(8,128)S(1)} %bitcast.516, f32[]{:T(128)} %constant.303.clone.1), kind=kCustom, calls=%fused_computation.226 | custom fusion | bytes 74240
  299.1 12.5 %all_to_all.39 = f32[9,32,128]{2,0,1:T(8,128)S(1)} all-to-all(f32[9,32,128]{2,0,1:T(8,128)S(1)} %scatter_fusion.1), channel_id=1, replica_groups=mesh['row'=8,'rep'=4] {'row'}, dimensions={1} | all-to-all | bytes 294912 | tf_op jit(solution)/shard_map/all_to_all | solution.py:263
  311.8 3.8 fusion.159
  316.6 4.1 add_add_fusion.8
  320.9 2.6 add_add_fusion.7
  323.4 2.7 multiply_add_fusion.7
  332.2 21.7 %reduce-scatter.5.cloned.1.call-done = f32[59,1024]{1,0:T(8,128)} async-done(((f32[59,4096]{1,0:T(8,128)}), f32[59,1024]{1,0:T(8,128)}) %reduce-scatter.5.cloned.1.call-update) | async-done | bytes 241680 | tf_op jit(solution)/shard_map/reduce_scatter | solution.py:271
  355.3 9.5 %all_gather.13 = f32[59,4096]{1,0:T(8,128)S(1)} all-gather(f32[59,1024]{1,0:T(8,128)S(1)} %get-tuple-element.363), channel_id=1, replica_groups=mesh['row'=8,'rep'=4] {'rep'}, dimensions={1}, use_global_device_ids=true | all-gather | bytes 1208320 | tf_op jit(solution)/shard_map/all_gather | solution.py:276
  365.6 10.1 %all_gather.14 = f32[59,4096]{1,0:T(8,128)S(1)} all-gather(f32[59,1024]{1,0:T(8,128)S(1)} %get-tuple-element.364), channel_id=1, replica_groups=mesh['row'=8,'rep'=4] {'rep'}, dimensions={1}, use_global_device_ids=true | all-gather | bytes 1208320 | tf_op jit(solution)/shard_map/all_gather | solution.py:278
  376.0 10.1 %all_gather.15 = f32[59,4096]{1,0:T(8,128)S(1)} all-gather(f32[59,1024]{1,0:T(8,128)S(1)} %get-tuple-element.365), channel_id=1, replica_groups=mesh['row'=8,'rep'=4] {'rep'}, dimensions={1}, use_global_device_ids=true | all-gather | bytes 1208320 | tf_op jit(solution)/shard_map/all_gather | solution.py:279
  390.6 3.3 collective-permute-start.1
  396.5 3.0 collective-permute-done
  (549 shorter events, 146.4 us)
Async XLA Ops:
  7.2 43.4 %copy-start.85 = (s32[2]{0:T(128)S(1)}, s32[2]{0:T(128)}, u32[]{:S(2)}) copy-start(s32[2]{0:T(128)} %constant.451) | copy-start | bytes 28
  7.2 43.4 %copy-start.84 = (s32[2]{0:T(128)S(1)}, s32[2]{0:T(128)}, u32[]{:S(2)}) copy-start(s32[2]{0:T(128)} %constant.454) | copy-start | bytes 28
  7.2 41.6 %copy-start.25 = (s32[2,1,4,512]{3,2,1,0:T(4,128)S(1)}, s32[2,1,4,512]{3,2,1,0:T(4,128)}, u32[]{:S(2)}) copy-start(s32[2,1,4,512]{3,2,1,0:T(4,128)} %param.27) | copy-start | bytes 49156
  7.2 42.2 %copy-start.59 = (f32[2,1,4,3,256]{4,2,3,1,0:T(4,128)S(1)}, f32[2,1,4,3,256]{4,2,3,1,0:T(4,128)}, u32[]{:S(2)}) copy-start(f32[2,1,4,3,256]{4,2,3,1,0:T(4,128)} %param.28) | copy-start | bytes 73732
  7.2 42.8 %copy-start.82 = (f32[2,1,4,2]{2,3,1,0:T(2,128)S(1)}, f32[2,1,4,2]{2,3,1,0:T(2,128)}, u32[]{:S(2)}) copy-start(f32[2,1,4,2]{2,3,1,0:T(2,128)} %param.24) | copy-start | bytes 196
  8.0 38.4 %copy-start.65 = (s32[16]{0:T(128)}, s32[16]{0:T(128)S(1)}, u32[]{:S(2)}) copy-start(s32[16]{0:T(128)S(1)} %eq.75) | copy-start | bytes 196
  8.3 38.2 %copy-start.68 = (s32[16]{0:T(128)}, s32[16]{0:T(128)S(1)}, u32[]{:S(2)}) copy-start(s32[16]{0:T(128)S(1)} %select_reduce_fusion) | copy-start | bytes 196
  10.9 31.5 %copy-start.80 = (s32[16]{0:T(128)}, s32[16]{0:T(128)S(1)}, u32[]{:S(2)}) copy-start(s32[16]{0:T(128)S(1)} %get-tuple-element.563) | copy-start | bytes 196
  12.2 50.3 %all-to-all-start = ((s32[8,4,1]{1,2,0:T(1,128)}), s32[8,4,1]{1,2,0:T(1,128)S(1)}, u32[]{:S(2)}, u32[]{:S(2)}) async-start(s32[8,4,1]{1,2,0:T(1,128)} %bitcast.2), calls=%async_computation | async-start | bytes 8192 | tf_op jit(solution)/shard_map/all_to_all | solution.py:236
  32.5 48.3 %copy-start.15 = (f32[4096]{0:T(1024)}, f32[4096]{0:T(1024)S(1)}, u32[]{:S(2)}) copy-start(f32[4096]{0:T(1024)S(1)} %multiply_reduce_fusion.7) | copy-start | bytes 49156
  46.5 34.4 %copy-start.11 = (f32[4096]{0:T(1024)}, f32[4096]{0:T(1024)S(1)}, u32[]{:S(2)}) copy-start(f32[4096]{0:T(1024)S(1)} %get-tuple-element.524) | copy-start | bytes 49156
  56.9 37.5 %copy-start.19 = (f32[1,4096]{1,0:T(1,128)}, f32[1,4096]{1,0:T(1,128)S(1)}, u32[]{:S(2)}) copy-start(f32[1,4096]{1,0:T(1,128)S(1)} %get-tuple-element.476) | copy-start | bytes 49156
  65.8 14.5 %all-to-all-start.1 = ((f32[9,32,128]{2,0,1:T(8,128)}), f32[9,32,128]{2,0,1:T(8,128)S(1)}, u32[]{:S(2)}, u32[]{:S(2)}) async-start(f32[9,32,128]{2,0,1:T(8,128)} %bitcast_select_fusion.1), calls=%async_computation.1 | async-start | bytes 524288 | tf_op jit(solution)/shard_map/all_to_all | solution.py:239
  71.8 126.2 %reduce-scatter.3.cloned.1.call-start = ((), (), s32[]{:S(2)}) async-start(), calls=%async_computation.8 | async-start | bytes 1310720 | tf_op jit(solution)/shard_map/reduce_scatter | solution.py:271
  156.6 38.6 %copy-start.57 = (s32[1,4,4,128]{3,2,1,0:T(4,128)S(1)}, s32[1,4,4,128]{3,2,1,0:T(4,128)}, u32[]{:S(2)}) copy-start(s32[1,4,4,128]{3,2,1,0:T(4,128)} %get-tuple-element.517) | copy-start | bytes 24580
  156.6 38.7 %copy-start.56 = (f32[1,1,4,3,256]{4,2,3,1,0:T(4,128)S(1)}, f32[1,1,4,3,256]{4,2,3,1,0:T(4,128)}, u32[]{:S(2)}) copy-start(f32[1,1,4,3,256]{4,2,3,1,0:T(4,128)} %get-tuple-element.511) | copy-start | bytes 36868
  156.6 39.3 %copy-start.74 = (f32[1,1,4,2]{2,3,1,0:T(2,128)S(1)}, f32[1,1,4,2]{2,3,1,0:T(2,128)}, u32[]{:S(2)}) copy-start(f32[1,1,4,2]{2,3,1,0:T(2,128)} %get-tuple-element.533) | copy-start | bytes 100
  156.6 39.9 %copy-start.58 = (s32[1,4,4,128]{3,2,1,0:T(4,128)S(1)}, s32[1,4,4,128]{3,2,1,0:T(4,128)}, u32[]{:S(2)}) copy-start(s32[1,4,4,128]{3,2,1,0:T(4,128)} %get-tuple-element.565) | copy-start | bytes 24580
  172.3 24.9 %all-to-all-start.3 = ((s32[8,4,1]{1,2,0:T(1,128)}), s32[8,4,1]{1,2,0:T(1,128)S(1)}, u32[]{:S(2)}, u32[]{:S(2)}) async-start(s32[8,4,1]{1,2,0:T(1,128)} %bitcast.78), calls=%async_computation.4 | async-start | bytes 8192 | tf_op jit(solution)/shard_map/all_to_all | solution.py:236
  209.6 29.8 %copy-start.17 = (f32[4096]{0:T(1024)}, f32[4096]{0:T(1024)S(1)}, u32[]{:S(2)}) copy-start(f32[4096]{0:T(1024)S(1)} %multiply_reduce_fusion.5) | copy-start | bytes 49156
  211.7 41.3 %copy-start.64 = (pred[4,512]{1,0:T(4,128)(4,1)S(1)}, pred[4,512]{1,0:T(4,128)(4,1)}, u32[]{:S(2)}) copy-start(pred[4,512]{1,0:T(4,128)(4,1)} %get-tuple-element.515) | copy-start | bytes 6148
  216.8 36.5 %copy-start.21 = (f32[1,4096]{1,0:T(1,128)}, f32[1,4096]{1,0:T(1,128)S(1)}, u32[]{:S(2)}) copy-start(f32[1,4096]{1,0:T(1,128)S(1)} %get-tuple-element.473) | copy-start | bytes 49156
  223.4 15.4 %all-to-all-start.4 = ((f32[9,32,128]{2,0,1:T(8,128)}), f32[9,32,128]{2,0,1:T(8,128)S(1)}, u32[]{:S(2)}, u32[]{:S(2)}) async-start(f32[9,32,128]{2,0,1:T(8,128)} %bitcast_select_fusion), calls=%async_computation.5 | async-start | bytes 524288 | tf_op jit(solution)/shard_map/all_to_all | solution.py:239
  229.4 124.5 %reduce-scatter.5.cloned.1.call-start = ((), (), s32[]{:S(2)}) async-start(), calls=%async_computation.9 | async-start | bytes 1310720 | tf_op jit(solution)/shard_map/reduce_scatter | solution.py:271
  299.0 29.4 %copy-start.40 = (f32[1,4096]{1,0:T(1,128)S(1)}, f32[1,4096]{1,0:T(1,128)}, u32[]{:S(2)}) copy-start(f32[1,4096]{1,0:T(1,128)} %get-tuple-element.397) | copy-start | bytes 49156
  299.0 29.4 %copy-start.39 = (f32[1,4096]{1,0:T(1,128)S(1)}, f32[1,4096]{1,0:T(1,128)}, u32[]{:S(2)}) copy-start(f32[1,4096]{1,0:T(1,128)} %get-tuple-element.395) | copy-start | bytes 49156
  299.0 29.4 %copy-start.38 = (f32[1,4096]{1,0:T(1,128)S(1)}, f32[1,4096]{1,0:T(1,128)}, u32[]{:S(2)}) copy-start(f32[1,4096]{1,0:T(1,128)} %get-tuple-element.392) | copy-start | bytes 49156
  299.0 29.5 %copy-start.37 = (f32[1,4096]{1,0:T(1,128)S(1)}, f32[1,4096]{1,0:T(1,128)}, u32[]{:S(2)}) copy-start(f32[1,4096]{1,0:T(1,128)} %get-tuple-element.390) | copy-start | bytes 49156
  299.0 29.5 %copy-start.36 = (f32[1,4096]{1,0:T(1,128)S(1)}, f32[1,4096]{1,0:T(1,128)}, u32[]{:S(2)}) copy-start(f32[1,4096]{1,0:T(1,128)} %get-tuple-element.388) | copy-start | bytes 49156
  316.4 37.5 %copy-start.5 = (f32[59,1024]{1,0:T(8,128)S(1)}, f32[59,1024]{1,0:T(8,128)}, u32[]{:S(2)}) copy-start(f32[59,1024]{1,0:T(8,128)} %reduce-scatter.3.cloned.1.call-done) | copy-start | bytes 724996
  389.1 10.4 %collective-permute-start = (f32[3,59,2,128]{3,1,0,2:T(8,128)S(1)}, f32[3,59,2,128]{3,1,0,2:T(8,128)S(1)}, u32[]{:S(2)}, u32[]{:S(2)}) collective-permute-start(f32[3,59,2,128]{3,1,0,2:T(8,128)S(1)} %get-tuple-element.480), channel_id=1, source_target_pairs={{0,4},{4,8},{8,12},{12,16},{16,20},{20,24},{24,28},{28,0},{1,5},{5... | collective-permute-start | bytes 543752 | tf_op jit(solution)/shard_map/ppermute | solution.py:45
  390.6 11.4 %collective-permute-start.1 = (f32[3,59,2,128]{3,1,0,2:T(8,128)S(1)}, f32[3,59,2,128]{3,1,0,2:T(8,128)S(1)}, u32[]{:S(2)}, u32[]{:S(2)}) collective-permute-start(f32[3,59,2,128]{3,1,0,2:T(8,128)S(1)} %get-tuple-element.479), channel_id=1, source_target_pairs={{4,0},{8,4},{12,8},{16,12},{20,16},{24,20},{28,24},{0,28},{5,1},{9... | collective-permute-start | bytes 543752 | tf_op jit(solution)/shard_map/ppermute | solution.py:48
  (84 other events, 1079.8 us)
Sparse Core Ops, SparseCore 0:
  170.9 23.7 reduce-scatter.2
  330.9 22.9 reduce-scatter.4
where the time goes:
time: 424 us; the launch traced here: 417 us
  other arithmetic  97.6 us (23%)
  local copies, waits for them, and re-layouts  93.7 us (22%)
  blocking collectives  64.2 us (15%)
  between operations  55.2 us (13%)
  waiting for transfers between devices  40.1 us (9%)
  matrix products  36.5 us (9%)
  starting transfers between devices  27.7 us (7%)
    gather x2, local copies, waits for them, and re-layouts, local(): sorted_rows = jnp.take_along_axis(tile_rows, orders[:, None, :], axis=2)  26.1 us
    all_to_all x2, blocking collectives, local(): lax.all_to_all(outgoing, 'row', split_axis=1, concat_axis=1, tiled=True)  24.4 us
    unnamed x168, local copies, waits for them, and re-layouts  23.3 us
    reduce_scatter x2, waiting for transfers between devices, local(): lax.psum_scatter(gradient, 'rep', scatter_dimension=1, tiled=True)  21.7 us
    dot_general x12, matrix products, render(): jnp.einsum('cn,pn->cp', splat_rows[5:8], alphas * transmit, precision=lax...  21.7 us
    all_gather x2, blocking collectives, local(): current = lax.all_gather(own_params, 'rep', axis=1, tiled=True)  19.5 us
    all_to_all x2, waiting for transfers between devices, local(): lax.all_to_all(serve(projected, asked_blocks, blk_dev), 'row', split_axis...  15.3 us
    dot_general x8, matrix products, render(): jnp.einsum('pbi,ij->pbj', log_keep, strict_upper, precision=lax.Precision...  12.5 us
  transfers between devices with their start and end apart: 8, of which 4 were waited for; matrix products, arithmetic and copies ran while one was open for 8% of the time, Pallas kernels for 0%

commit v1 on v0

v1 whole, which is shorter than its diff:
```python
import math

import jax
import jax.numpy as jnp
from jax import lax
from jax.experimental import pallas as pl
from jax.experimental.pallas import tpu as pltpu
from jax.sharding import PartitionSpec as P

P_SIZE = 59
BLOCK = 128
LISTB = 4
PIX = 256
ITERS = 2
MIGH = 2
DEPTH = 512
SIDE = 16
HALF = DEPTH // 2
MIG_LANE = 64
CAM_ROWS = 16
LOG2E = 1.4426950408889634

harm_zero = 0.28209479177387814
harm_one = 0.4886025119029199
harm_two = (
    1.0925484305920792,
    -1.0925484305920792,
    0.31539156525252005,
    -1.0925484305920792,
    0.5462742152960396,
)
harm_three = (
    -0.5900435899266435,
    2.890611442640554,
    -0.4570457994644658,
    0.3731763325901154,
    -0.4570457994644658,
    1.445305721320277,
    -0.5900435899266435,
)
learn_rate = 0.01
adam_epsilon = 1e-08

f32 = jnp.float32
bf16 = jnp.bfloat16
VM = pl.BlockSpec(memory_space=pltpu.VMEM)
SM = pl.BlockSpec(memory_space=pltpu.SMEM)


def up8(count):
    return -(-count // 8) * 8


def harmonics(x, y, z):
    xx, yy, zz = x * x, y * y, z * z
    return [
        harm_zero + 0.0 * x,
        -harm_one * y,
        harm_one * z,
        -harm_one * x,
        harm_two[0] * x * y,
        harm_two[1] * y * z,
        harm_two[2] * (2.0 * zz - xx - yy),
        harm_two[3] * x * z,
        harm_two[4] * (xx - yy),
        harm_three[0] * y * (3.0 * xx - yy),
        harm_three[1] * x * y * z,
        harm_three[2] * y * (4.0 * zz - xx - yy),
        harm_three[3] * z * (2.0 * zz - 3.0 * xx - 3.0 * yy),
        harm_three[4] * x * (4.0 * zz - xx - yy),
        harm_three[5] * z * (xx - yy),
        harm_three[6] * x * (xx - 3.0 * yy),
    ]


def split(value, pieces):
    out = []
    for piece in range(pieces):
        part = value.astype(bf16)
        out.append(part)
        if piece < pieces - 1:
            value = value - part.astype(f32)
    return out


def dot(left, right, dims=((1,), (0,))):
    return lax.dot_general(left, right, (dims, ((), ())), preferred_element_type=f32)


NT = ((1,), (1,))
TN = ((0,), (0,))


def rank_of(owners, index):
    rank = jnp.int32(0)
    for other in range(index):
        rank = rank + (owners[other] == owners[index]).astype(jnp.int32)
    return rank


def request_kernel(capacity, owner_ref, block_ref, migration_ref, out_ref):
    owners = out_ref.shape[0]
    tiles = owner_ref.shape[2]
    lane = lax.broadcasted_iota(jnp.int32, (owners, BLOCK), 1)
    row = lax.broadcasted_iota(jnp.int32, (owners, BLOCK), 0)
    place = row * BLOCK + lane
    message = jnp.full((owners, BLOCK), -1, jnp.int32)
    for step in range(ITERS):
        names = [owner_ref[step, 0, t, j] for t in range(tiles) for j in range(LISTB)]
        for index in range(tiles * LISTB):
            target = names[index] * BLOCK + step * capacity + rank_of(names, index)
            block = block_ref[step, 0, index // LISTB, index % LISTB]
            message = jnp.where(place == target, block, message)
    for side in range(2):
        for j in range(MIGH):
            message = jnp.where(
                lane == MIG_LANE + side * MIGH + j, migration_ref[0, side, j], message
            )
    for owner in range(owners):
        out_ref[owner] = message[owner : owner + 1]


def geometry(row):
    scales = [jnp.exp(row(3 + k)) for k in range(3)]
    quats = [row(6 + k) for k in range(4)]
    norm = lax.rsqrt(
        quats[0] * quats[0] + quats[1] * quats[1] + quats[2] * quats[2] + quats[3] * quats[3]
    )
    w, x, y, z = [part * norm for part in quats]
    rotation = [
        [1.0 - 2.0 * (y * y + z * z), 2.0 * (x * y - w * z), 2.0 * (x * z + w * y)],
        [2.0 * (x * y + w * z), 1.0 - 2.0 * (x * x + z * z), 2.0 * (y * z - w * x)],
        [2.0 * (x * z - w * y), 2.0 * (y * z + w * x), 1.0 - 2.0 * (x * x + y * y)],
    ]
    return scales, (w, x, y, z), norm, rotation


def conic_of(scales, rotation, affine):
    spread = [
        [
            (
                affine[3 * i] * rotation[0][k]
                + affine[3 * i + 1] * rotation[1][k]
                + affine[3 * i + 2] * rotation[2][k]
            )
            * scales[k]
            for k in range(3)
        ]
        for i in range(2)
    ]
    one, two = spread
    cov_xx = one[0] * one[0] + one[1] * one[1] + one[2] * one[2] + 0.3
    cov_yy = two[0] * two[0] + two[1] * two[1] + two[2] * two[2] + 0.3
    cov_xy = one[0] * two[0] + one[1] * two[1] + one[2] * two[2]
    inverse = 1.0 / (cov_xx * cov_yy - cov_xy * cov_xy)
    return cov_yy * inverse, -cov_xy * inverse, cov_xx * inverse


def serve(step, capacity, blocks, camera_ref, asked_ref, dense, table, faint, out_ref):
    cam = [camera_ref[step, 0, k] for k in range(11)]
    basis = harmonics(cam[8], cam[9], cam[10])
    for group in range(blocks // 8):

        def row(p):
            return dense[p * blocks + 8 * group : p * blocks + 8 * group + 8, :]

        scales, _, _, rotation = geometry(row)
        conic = conic_of(scales, rotation, cam)
        means = [row(k) for k in range(3)]
        rows = [
            cam[0] * means[0] + cam[1] * means[1] + cam[2] * means[2] + cam[6],
            cam[3] * means[0] + cam[4] * means[1] + cam[5] * means[2] + cam[7],
            conic[0],
            conic[1],
            conic[2],
        ]
        for k in range(3):
            colour = basis[0] * row(11 + k)
            for j in range(1, 16):
                colour = colour + basis[j] * row(11 + 3 * j + k)
            rows.append(0.5 + colour)
        for k in range(8):
            table[pl.ds(64 * group + k, 8, stride=8), :] = rows[k]
        faint[8 * group : 8 * group + 8, :] = -LOG2E * jnp.log(1.0 + jnp.exp(-row(10)))
    owners = out_ref.shape[0]
    for peer in range(owners):
        for slot in range(capacity):
            block = jnp.maximum(asked_ref[peer, 0, step * capacity + slot], 0)
            out_ref[peer, 8 * slot : 8 * slot + 8, :] = table[
                pl.ds(pl.multiple_of(block * 8, 8), 8), :
            ]
            out_ref[peer, 8 * capacity + slot : 8 * capacity + slot + 1, :] = faint[
                pl.ds(block, 1), :
            ]


def row_groups():
    return [(first, min(8, P_SIZE - first)) for first in range(0, P_SIZE, 8)]


def start_kernel(capacity, params_ref, camera_ref, asked_ref, out_ref, dense, table, faint):
    blocks = params_ref.shape[1] // BLOCK
    for block in range(blocks):
        for first, count in row_groups():
            dense[pl.ds(first * blocks + block, count, stride=blocks), :] = params_ref[
                first : first + count, block * BLOCK : (block + 1) * BLOCK
            ]
    serve(0, capacity, blocks, camera_ref, asked_ref, dense, table, faint, out_ref)


def render_kernel(step, capacity, slots, final, *refs):
    if final:
        (
            arrived, corner_ref, owner_ref, block_ref, asked_ref, order_ref, target_ref, earlier_ref,
            picture_ref, out_ref, onehot, upper, lower, features, flat, coeffs,
        ) = refs
        for other in range(ITERS - 1):
            picture_ref[other] = earlier_ref[other]
    else:
        (
            arrived, corner_ref, owner_ref, order_ref, target_ref,
            picture_ref, out_ref, onehot, upper, lower, features, flat, coeffs,
        ) = refs
    owners = arrived.shape[0]
    tiles = owner_ref.shape[2]
    out_ref[...] = jnp.zeros_like(out_ref)

    first = lax.broadcasted_iota(jnp.int32, (HALF, HALF), 0)
    second = lax.broadcasted_iota(jnp.int32, (HALF, HALF), 1)
    upper[...] = jnp.where(first < second, 1.0, 0.0).astype(bf16)
    lower[...] = jnp.where(first > second, 1.0, 0.0).astype(bf16)
    pixel = lax.broadcasted_iota(jnp.int32, (PIX, BLOCK), 0)
    which = lax.broadcasted_iota(jnp.int32, (PIX, BLOCK), 1) // 3
    px = (pixel % SIDE).astype(f32) - (SIDE / 2 - 0.5)
    py = (pixel // SIDE).astype(f32) - (SIDE / 2 - 0.5)
    chosen = jnp.where(which == 0, 1.0, 0.0)
    for index, value in enumerate((px, py, px * px, px * py, py * py)):
        chosen = jnp.where(which == index + 1, value, chosen)
    features[...] = chosen.astype(bf16)
    pixel = lax.broadcasted_iota(jnp.int32, (16, PIX), 1)
    which = lax.broadcasted_iota(jnp.int32, (16, PIX), 0)
    px = (pixel % SIDE).astype(f32) - (SIDE / 2 - 0.5)
    py = (pixel // SIDE).astype(f32) - (SIDE / 2 - 0.5)
    chosen = jnp.where(which == 0, 1.0, 0.0)
    for index, value in enumerate((px, py, px * px, px * py, py * py)):
        chosen = jnp.where(which == index + 1, value, chosen)
    flat[...] = chosen.astype(bf16)
    coeffs[...] = jnp.zeros_like(coeffs)

    names = [owner_ref[step, 0, t, j] for t in range(tiles) for j in range(LISTB)]
    ranks = [rank_of(names, index) for index in range(tiles * LISTB)]

    for tile in range(tiles):
        order = order_ref[step, 0, tile : tile + 1, :]
        for piece in range(DEPTH // BLOCK):
            ids = lax.broadcasted_iota(jnp.int32, (BLOCK, DEPTH), 0) + piece * BLOCK
            onehot[piece * BLOCK : (piece + 1) * BLOCK, :] = jnp.where(
                ids == order, 1.0, 0.0
            ).astype(bf16)
        pieces, dims = [], []
        for j in range(LISTB):
            name, rank = names[tile * LISTB + j], ranks[tile * LISTB + j]
            pieces.append(arrived[name, pl.ds(pl.multiple_of(rank * 8, 8), 8), :])
            dims.append(
                jnp.broadcast_to(arrived[name, pl.ds(8 * capacity + rank, 1), :], (8, BLOCK))
            )
        sorted_rows, sorted_dim = [], []
        for piece in range(DEPTH // BLOCK):
            ids = jnp.broadcast_to(order[:, piece * BLOCK : (piece + 1) * BLOCK], (8, BLOCK))
            within, source = ids & (BLOCK - 1), ids // BLOCK
            got = jnp.take_along_axis(pieces[0], within, axis=1)
            dim = jnp.take_along_axis(dims[0], within, axis=1)
            for j in range(1, LISTB):
                got = jnp.where(source == j, jnp.take_along_axis(pieces[j], within, axis=1), got)
                dim = jnp.where(source == j, jnp.take_along_axis(dims[j], within, axis=1), dim)
            sorted_rows.append(got)
            sorted_dim.append(dim)
        rows = jnp.concatenate(sorted_rows, axis=1)
        faint = jnp.concatenate(sorted_dim, axis=1)[0:1]
        u = rows[0:1] - (corner_ref[step, 0, tile, 0] + SIDE / 2)
        v = rows[1:2] - (corner_ref[step, 0, tile, 1] + SIDE / 2)
        a, b, c = rows[2:3], rows[3:4], rows[4:5]
        colours = rows[5:8]
        half_a, half_b, half_c = (-0.5 * LOG2E) * a, -LOG2E * b, (-0.5 * LOG2E) * c
        values = (
            half_a * u * u + half_b * u * v + half_c * v * v + faint,
            -(2.0 * half_a * u + half_b * v),
            -(2.0 * half_c * v + half_b * u),
            half_a,
            half_b,
            half_c,
        )
        for index, value in enumerate(values):
            for piece, part in enumerate(split(value, 3)):
                coeffs[3 * index + piece : 3 * index + piece + 1, :] = part.astype(f32)
        form = coeffs[...].astype(bf16)
        col_h, col_m, col_l = [part.astype(f32) for part in split(colours, 3)]
        col_left = jnp.concatenate([col_h, col_m, col_l], axis=0).astype(bf16)
        col_right = jnp.concatenate(
            [col_h, col_m, col_h, col_m, col_l, col_h], axis=0
        ).astype(bf16)

        step_rows = 128
        moments = jnp.zeros((16, DEPTH), f32)
        col_grads = jnp.zeros((9, DEPTH), f32)
        for at in range(0, PIX, step_rows):
            feats = features[at : at + step_rows, 0:32]
            power = dot(feats, form)
            alpha = jnp.exp2(power)
            keep = jnp.log(1.0 - alpha)
            ratio = jnp.exp2(power - LOG2E * keep)
            keep_h, keep_m = split(keep, 2)
            tri = upper[...]
            near = dot(keep_h[:, :HALF], tri) + dot(keep_m[:, :HALF], tri)
            far = dot(keep_h[:, HALF:], tri) + dot(keep_m[:, HALF:], tri)
            far = far + (near[:, HALF - 1 : HALF] + keep[:, HALF - 1 : HALF])
            weight = alpha * jnp.exp(jnp.concatenate([near, far], axis=1))
            weight_h, weight_m = split(weight, 2)
            shades = dot(col_left, weight_h, NT) + dot(col_left, weight_m, NT)
            shades = shades[0:3] + shades[3:6] + shades[6:9]
            if final:
                picture_ref[step, 0, tile, :, at : at + step_rows] = shades
            else:
                picture_ref[step, 0, tile, :, at : at + step_rows] = shades
            error = shades - target_ref[step, 0, tile, :, at : at + step_rows]
            err_h, err_m, err_l = [part.astype(f32) for part in split(error, 3)]
            err_left = jnp.concatenate([err_h, err_m, err_l], axis=0).astype(bf16)
            err_right = jnp.concatenate(
                [err_h, err_h, err_m, err_m, err_h, err_l], axis=0
            ).astype(bf16)
            col_grads = col_grads + dot(err_left, weight_h) + dot(err_left, weight_m)
            flow = weight * dot(err_right, col_right, TN)
            flow_h, flow_m = split(flow, 2)
            tri = lower[...]
            far = dot(flow_h[:, HALF:], tri) + dot(flow_m[:, HALF:], tri)
            near = dot(flow_h[:, :HALF], tri) + dot(flow_m[:, :HALF], tri)
            near = near + (far[:, 0:1] + flow[:, HALF : HALF + 1])
            heat = flow - ratio * jnp.concatenate([near, far], axis=1)
            for part in split(heat, 3):
                moments = moments + dot(flat[:, at : at + step_rows], part)
        col_grads = col_grads[0:3] + col_grads[3:6] + col_grads[6:9]
        m00, m10, m01 = moments[0:1], moments[1:2], moments[2:3]
        m20, m11, m02 = moments[3:4], moments[4:5], moments[5:6]
        x1, y1 = m10 - u * m00, m01 - v * m00
        grads = [
            a * x1 + b * y1,
            b * x1 + c * y1,
            -0.5 * (m20 - 2.0 * u * m10 + u * u * m00),
            -(m11 - u * m01 - v * m10 + u * v * m00),
            -0.5 * (m02 - 2.0 * v * m01 + v * v * m00),
            col_grads,
            m00,
            jnp.zeros((7, DEPTH), f32),
        ]
        grads = jnp.concatenate(grads, axis=0)
        listed = jnp.zeros((16, DEPTH), f32)
        for part in split(grads, 3):
            listed = listed + dot(part, onehot[...], NT)
        for j in range(LISTB):
            name, rank = names[tile * LISTB + j], ranks[tile * LISTB + j]
            if final:
                block = block_ref[step, 0, tile, j]
                for k in range(MIGH):
                    goes_left = asked_ref[name, 0, MIG_LANE + k] == block
                    goes_right = asked_ref[name, 0, MIG_LANE + MIGH + k] == block
                    rank = jnp.where(goes_left, capacity + MIGH + k, rank)
                    rank = jnp.where(goes_right, capacity + k, rank)
                goes_left = jnp.bool_(False)
                goes_right = jnp.bool_(False)
                for k in range(MIGH):
                    goes_left |= asked_ref[name, 0, MIG_LANE + k] == block
                    goes_right |= asked_ref[name, 0, MIG_LANE + MIGH + k] == block
                below = jnp.where(name == 0, owners - 1, name - 1)
                above = jnp.where(name == owners - 1, 0, name + 1)
                name = jnp.where(goes_left, below, jnp.where(goes_right, above, name))
            lanes = slice(j * BLOCK, (j + 1) * BLOCK)
            main = pl.ds(pl.multiple_of(rank * 8, 8), 8)
            extra = pl.ds(8 * slots + rank, 1)
            if final:
                out_ref[name, main, :] = out_ref[name, main, :] + listed[0:8, lanes]
                out_ref[name, extra, :] = out_ref[name, extra, :] + listed[8:9, lanes]
            else:
                out_ref[name, main, :] = listed[0:8, lanes]
                out_ref[name, extra, :] = listed[8:9, lanes]


def gather_kernel(step, capacity, slots, returned, asked_ref, migration_ref, camera_ref, out_ref):
    owners = returned.shape[0]
    blocks = (out_ref.shape[0] - CAM_ROWS) // 9
    out_ref[...] = jnp.zeros_like(out_ref)

    def body(peer, carry):
        for slot in range(slots):
            if slot < capacity:
                block = jnp.maximum(asked_ref[peer, 0, step * capacity + slot], 0)
            else:
                block = migration_ref[0, (slot - capacity) // MIGH, (slot - capacity) % MIGH]
            main = pl.ds(pl.multiple_of(block * 8, 8), 8)
            extra = pl.ds(8 * blocks + block, 1)
            out_ref[main, :] = out_ref[main, :] + returned[peer, 8 * slot : 8 * slot + 8, :]
            out_ref[extra, :] = (
                out_ref[extra, :] + returned[peer, 8 * slots + slot : 8 * slots + slot + 1, :]
            )
        return carry

    lax.fori_loop(0, owners, body, 0)
    for index, k in enumerate((0, 1, 2, 3, 4, 5, 8, 9, 10)):
        at = 9 * blocks + index
        out_ref[at : at + 1, :] = jnp.full((1, BLOCK), camera_ref[step, 0, k], f32)


def collect(own_ref, others, scratch):
    mine = lax.axis_index("rep")
    scratch[mine] = own_ref[...]
    for offset, ref in others:
        scratch[mine ^ offset] = ref[...]


def pullback(blocks, cams, dense, grads):
    count = cams.shape[0]
    affine, basis = [], []
    for c in range(count):
        rows = [
            jnp.broadcast_to(cams[c, 9 * blocks + k : 9 * blocks + k + 1, :], (8, BLOCK))
            for k in range(9)
        ]
        affine.append(rows[0:6])
        basis.append(harmonics(rows[6], rows[7], rows[8]))
    for group in range(blocks // 8):

        def row(p):
            return dense[p * blocks + 8 * group : p * blocks + 8 * group + 8, :]

        def put(p, value):
            grads[p * blocks + 8 * group : p * blocks + 8 * group + 8, :] = value

        given = [
            [cams[c, pl.ds(64 * group + k, 8, stride=8), :] for k in range(8)] for c in range(count)
        ]
        scales, (w, x, y, z), norm, rotation = geometry(row)
        means = [0.0, 0.0, 0.0]
        sigma = [0.0] * 6
        for c in range(count):
            m = affine[c]
            a, b, d = conic_of(scales, rotation, m)
            g_x, g_y, g_a, g_b, g_d = given[c][0:5]
            for k in range(3):
                means[k] = means[k] + m[k] * g_x + m[3 + k] * g_y
            g_b = 0.5 * g_b
            t00, t01 = a * g_a + b * g_b, a * g_b + b * g_d
            t10, t11 = b * g_a + d * g_b, b * g_b + d * g_d
            h00 = -(t00 * a + t01 * b)
            h01 = -(t00 * b + t01 * d)
            h11 = -(t10 * b + t11 * d)
            top = [h00 * m[k] + h01 * m[3 + k] for k in range(3)]
            low = [h01 * m[k] + h11 * m[3 + k] for k in range(3)]
            for index, (i, k) in enumerate(((0, 0), (0, 1), (0, 2), (1, 1), (1, 2), (2, 2))):
                sigma[index] = sigma[index] + m[i] * top[k] + m[3 + i] * low[k]
        for k in range(3):
            put(k, means[k])
        full = [
            [sigma[0], sigma[1], sigma[2]],
            [sigma[1], sigma[3], sigma[4]],
            [sigma[2], sigma[4], sigma[5]],
        ]
        turn = [[None] * 3 for _ in range(3)]
        for k in range(3):
            column = [rotation[j][k] * scales[k] for j in range(3)]
            pulled = [
                2.0 * (full[j][0] * column[0] + full[j][1] * column[1] + full[j][2] * column[2])
                for j in range(3)
            ]
            put(
                3 + k, pulled[0] * column[0] + pulled[1] * column[1] + pulled[2] * column[2]
            )
            for j in range(3):
                turn[j][k] = pulled[j] * scales[k]
        g_w = 2.0 * (
            z * (turn[1][0] - turn[0][1])
            + y * (turn[0][2] - turn[2][0])
            + x * (turn[2][1] - turn[1][2])
        )
        g_x = 2.0 * (
            y * (turn[0][1] + turn[1][0])
            + z * (turn[0][2] + turn[2][0])
            - 2.0 * x * (turn[1][1] + turn[2][2])
            + w * (turn[2][1] - turn[1][2])
        )
        g_y = 2.0 * (
            x * (turn[0][1] + turn[1][0])
            + z * (turn[1][2] + turn[2][1])
            - 2.0 * y * (turn[0][0] + turn[2][2])
            + w * (turn[0][2] - turn[2][0])
        )
        g_z = 2.0 * (
            x * (turn[0][2] + turn[2][0])
            + y * (turn[1][2] + turn[2][1])
            - 2.0 * z * (turn[0][0] + turn[1][1])
            + w * (turn[1][0] - turn[0][1])
        )
        along = w * g_w + x * g_x + y * g_y + z * g_z
        for k, (part, pull) in enumerate(((w, g_w), (x, g_x), (y, g_y), (z, g_z))):
            put(6 + k, norm * (pull - part * along))
        faint = cams[0, 8 * blocks + 8 * group : 8 * blocks + 8 * group + 8, :]
        for c in range(1, count):
            faint = faint + cams[c, 8 * blocks + 8 * group : 8 * blocks + 8 * group + 8, :]
        put(10, faint / (1.0 + jnp.exp(row(10))))
        for j in range(16):
            for k in range(3):
                value = basis[0][j] * given[0][5 + k]
                for c in range(1, count):
                    value = value + basis[c][j] * given[c][5 + k]
                put(11 + 3 * j + k, value)


def adam(value, first, second, gradient):
    first = 0.9 * first + 0.1 * gradient
    second = 0.999 * second + 0.001 * gradient * gradient
    return value - learn_rate * first / (jnp.sqrt(second) + adam_epsilon), first, second


def update_kernel(capacity, *refs):
    (
        own_ref, near_ref, far_ref, cross_ref, params_ref, first_ref, second_ref, camera_ref,
        asked_ref, migration_ref, new_params, new_first, new_second, out_ref, left_ref, right_ref,
        cams, dense, grads, table, faint,
    ) = refs
    blocks = params_ref.shape[1] // BLOCK
    collect(own_ref, ((1, near_ref), (2, far_ref), (3, cross_ref)), cams)
    for block in range(blocks):
        for top, count in row_groups()[:2]:
            dense[pl.ds(top * blocks + block, count, stride=blocks), :] = params_ref[
                top : top + count, block * BLOCK : (block + 1) * BLOCK
            ]
    pullback(blocks, cams, dense, grads)
    for block in range(blocks):
        lanes = slice(block * BLOCK, (block + 1) * BLOCK)
        for top, count in row_groups():
            part = slice(top, top + count)
            where = pl.ds(top * blocks + block, count, stride=blocks)
            value, first, second = adam(
                params_ref[part, lanes], first_ref[part, lanes], second_ref[part, lanes],
                grads[where, :],
            )
            new_params[part, lanes] = value
            new_first[part, lanes] = first
            new_second[part, lanes] = second
            dense[where, :] = value
    serve(1, capacity, blocks, camera_ref, asked_ref, dense, table, faint, out_ref)
    for side, ref in ((0, left_ref), (1, right_ref)):
        for j in range(MIGH):
            lanes = pl.ds(pl.multiple_of(migration_ref[0, side, j] * BLOCK, BLOCK), BLOCK)
            for index, source in enumerate((new_params, new_first, new_second)):
                ref[index, :, j * BLOCK : (j + 1) * BLOCK] = source[:, lanes]


def final_kernel(*refs):
    (
        own_ref, near_ref, far_ref, cross_ref, params_ref, first_ref, second_ref, below_ref,
        above_ref, migration_ref, new_params, new_first, new_second, cams, dense, grads,
    ) = refs
    blocks = params_ref.shape[1] // BLOCK
    collect(own_ref, ((1, near_ref), (2, far_ref), (3, cross_ref)), cams)
    for block in range(blocks):
        for top, count in row_groups()[:2]:
            dense[pl.ds(top * blocks + block, count, stride=blocks), :] = params_ref[
                top : top + count, block * BLOCK : (block + 1) * BLOCK
            ]
    moved = [
        (migration_ref[0, side, j], ref, j)
        for side, ref in ((0, below_ref), (1, above_ref))
        for j in range(MIGH)
    ]
    for block, ref, j in moved:
        for top, count in row_groups()[:2]:
            dense[pl.ds(top * blocks + block, count, stride=blocks), :] = ref[
                0, top : top + count, j * BLOCK : (j + 1) * BLOCK
            ]
    pullback(blocks, cams, dense, grads)
    for block in range(blocks):
        lanes = slice(block * BLOCK, (block + 1) * BLOCK)
        for top, count in row_groups():
            part = slice(top, top + count)
            value, first, second = adam(
                params_ref[part, lanes], first_ref[part, lanes], second_ref[part, lanes],
                grads[pl.ds(top * blocks + block, count, stride=blocks), :],
            )
            new_params[part, lanes] = value
            new_first[part, lanes] = first
            new_second[part, lanes] = second
    for block, ref, j in moved:
        lanes = pl.ds(pl.multiple_of(block * BLOCK, BLOCK), BLOCK)
        source = slice(j * BLOCK, (j + 1) * BLOCK)
        for top, count in row_groups():
            part = slice(top, top + count)
            value, first, second = adam(
                ref[0, part, source], ref[1, part, source], ref[2, part, source],
                grads[pl.ds(top * blocks + block, count, stride=blocks), :],
            )
            new_params[part, lanes] = value
            new_first[part, lanes] = first
            new_second[part, lanes] = second


def shape(dims, dtype=f32):
    return jax.ShapeDtypeStruct(dims, dtype)


def bind(kernel, *static):
    def run(*refs):
        kernel(*static, *refs)

    return run


def swap(value, axis, offset):
    count = lax.axis_size(axis)
    return lax.ppermute(value, axis, [(i, i ^ offset) for i in range(count)])


def turn(value, axis, offset):
    count = lax.axis_size(axis)
    return lax.ppermute(value, axis, [(i, (i + offset) % count) for i in range(count)])


def exchange(value):
    far = swap(value, "rep", 2)
    near = swap(value, "rep", 1)
    cross = swap(far, "rep", 1)
    return near, far, cross


def row_exchange(value):
    return lax.all_to_all(value, "row", split_axis=0, concat_axis=0, tiled=True)


def local(
    params,
    first_moment,
    second_moment,
    camera,
    tile_corner,
    tile_owner,
    tile_block,
    depth_order,
    targets,
    migration,
):
    owners = lax.axis_size("row")
    replicas = lax.axis_size("rep")
    blocks = params.shape[1] // BLOCK
    tiles = tile_owner.shape[2]
    requests = tiles * LISTB
    capacity = max(2, 2 * ((requests + owners - 1) // owners))
    slots = capacity + 2 * MIGH
    dense = pltpu.VMEM((64 * blocks, BLOCK), f32)
    table = pltpu.VMEM((8 * blocks, BLOCK), f32)
    faint = pltpu.VMEM((blocks, BLOCK), f32)
    payload = 9 * blocks + CAM_ROWS
    cams = pltpu.VMEM((replicas, payload, BLOCK), f32)
    state = [shape(params.shape)] * 3

    lists = pl.pallas_call(
        bind(request_kernel, capacity),
        out_shape=shape((owners, 1, BLOCK), jnp.int32),
        in_specs=[SM, SM, SM],
        out_specs=VM,
    )(tile_owner, tile_block, migration)
    asked = row_exchange(lists)

    outgoing = pl.pallas_call(
        bind(start_kernel, capacity),
        out_shape=shape((owners, up8(9 * capacity), BLOCK)),
        in_specs=[VM, SM, SM],
        out_specs=VM,
        scratch_shapes=[dense, table, faint],
    )(params, camera, asked)

    render_scratch = [
        pltpu.VMEM((DEPTH, DEPTH), bf16),
        pltpu.VMEM((HALF, HALF), bf16),
        pltpu.VMEM((HALF, HALF), bf16),
        pltpu.VMEM((PIX, BLOCK), bf16),
        pltpu.VMEM((16, PIX), bf16),
        pltpu.VMEM((32, DEPTH), f32),
    ]
    pictures_shape = shape(targets.shape)

    def gather(step, count, returned):
        return pl.pallas_call(
            bind(gather_kernel, step, capacity, count),
            out_shape=shape((payload, BLOCK)),
            in_specs=[VM, SM, SM, SM],
            out_specs=VM,
        )(returned, asked, migration, camera)

    arrived = row_exchange(outgoing)
    pictures, back = pl.pallas_call(
        bind(render_kernel, 0, capacity, capacity, False),
        out_shape=[pictures_shape, shape((owners, up8(9 * capacity), BLOCK))],
        in_specs=[VM, SM, SM, VM, VM],
        out_specs=[VM, VM],
        scratch_shapes=render_scratch,
    )(arrived, tile_corner, tile_owner, depth_order, targets)
    own = gather(0, capacity, row_exchange(back))
    near, far, cross = exchange(own)
    leaving = shape((3, P_SIZE, MIGH * BLOCK))
    current, moment_one, moment_two, outgoing, left, right = pl.pallas_call(
        bind(update_kernel, capacity),
        out_shape=state + [shape((owners, up8(9 * capacity), BLOCK)), leaving, leaving],
        in_specs=[VM] * 7 + [SM] * 3,
        out_specs=[VM] * 6,
        scratch_shapes=[cams, dense, dense, table, faint],
    )(
        own, near, far, cross, params, first_moment, second_moment, camera, asked, migration
    )
    arrived = row_exchange(outgoing)
    below = turn(right, "row", 1)
    above = turn(left, "row", -1)
    pictures, back = pl.pallas_call(
        bind(render_kernel, 1, capacity, slots, True),
        out_shape=[pictures_shape, shape((owners, up8(9 * slots), BLOCK))],
        in_specs=[VM, SM, SM, SM, SM, VM, VM, VM],
        out_specs=[VM, VM],
        scratch_shapes=render_scratch,
    )(arrived, tile_corner, tile_owner, tile_block, asked, depth_order, targets, pictures)
    own = gather(1, slots, row_exchange(back))
    near, far, cross = exchange(own)
    current, moment_one, moment_two = pl.pallas_call(
        final_kernel,
        out_shape=state,
        in_specs=[VM] * 9 + [SM],
        out_specs=[VM] * 3,
        scratch_shapes=[cams, dense, dense],
    )(own, near, far, cross, current, moment_one, moment_two, below, above, migration)
    return current, moment_one, moment_two, pictures


def solution(mesh):
    return jax.shard_map(
        local,
        mesh=mesh,
        in_specs=(
            P(None, "row"),
            P(None, "row"),
            P(None, "row"),
            P(None, "rep", None),
            P(None, "rep", "row", None),
            P(None, "rep", "row", None),
            P(None, "rep", "row", None),
            P(None, "rep", "row", None),
            P(None, "rep", "row", None, None),
            P("row", None, None),
        ),
        out_specs=(
            P(None, "row"),
            P(None, "row"),
            P(None, "row"),
            P(None, "rep", "row", None, None),
        ),
        check_vma=False,
    )
```

time: 424 us -> 130 us (0.31); the launches traced: 417 us -> 129 us
  other arithmetic: 97.6 us -> 0 us
  local copies, waits for them, and re-layouts: 93.7 us -> 4.06 us
  between operations: 55.2 us -> 0.71 us
  Pallas kernels: 0 us -> 47.5 us
  matrix products: 36.5 us -> 0 us
  waiting for transfers between devices: 40.1 us -> 14.1 us
  starting transfers between devices: 27.7 us -> 11.7 us
  blocking collectives: 64.2 us -> 51 us
    pallas_call x0 -> x8, Pallas kernels: none -> 47.5 us  [the longest x1 13 us: local(): pl.pallas_call(bind(render_kernel, 1, capacity, slots, True), out_shape=[...]
    all_gather x4 -> x0, blocking collectives: 39.8 us -> none  [the longest x2 19.5 us: local(): current = lax.all_gather(own_params, 'rep', axis=1, tiled=True)]
    dot_general x24 -> x0, matrix products: 36.5 us -> none  [the longest x12 21.7 us: render(): jnp.einsum('cn,pn->cp', splat_rows[5:8], alphas * transmit, precision=lax...]
    gather x7 -> x0, local copies, waits for them, and re-layouts: 29.1 us -> none  [the longest x2 26.1 us: local(): sorted_rows = jnp.take_along_axis(tile_rows, orders[:, None, :], axis=2)]
    all_to_all x2 -> x4, blocking collectives: 24.4 us -> 51 us  [row_exchange(): return lax.all_to_all(value, 'row', split_axis=0, concat_axis=0, tiled=True)]
    add_any x22 -> x0, other arithmetic: 23.7 us -> none  [the longest x2 8.14 us: project(): quat_z * quat_z]
    reduce_scatter x2 -> x0, waiting for transfers between devices: 21.7 us -> none  [local(): lax.psum_scatter(gradient, 'rep', scatter_dimension=1, tiled=True)]
    all_to_all x4 -> x1, starting transfers between devices: 22.9 us -> 3.51 us  [row_exchange(): return lax.all_to_all(value, 'row', split_axis=0, concat_axis=0, tiled=True)]
  transfers between devices with their start and end apart: 8 -> 9, of which waited for: 4 -> 4; matrix products, arithmetic and copies ran while one was open for 8% -> 1% of each run, Pallas kernels for 0% -> 0%
where the time goes in v1:
time: 130 us; the launch traced here: 129 us
  blocking collectives  51 us (39%)
  Pallas kernels  47.5 us (37%)
  waiting for transfers between devices  14.1 us (11%)
  starting transfers between devices  11.7 us (9%)
  local copies, waits for them, and re-layouts  4.06 us (3%)
    all_to_all x4, blocking collectives, row_exchange(): return lax.all_to_all(value, 'row', split_axis=0, concat_axis=0, tiled=True)  51 us
    pallas_call x1, Pallas kernels, local(): pl.pallas_call(bind(render_kernel, 1, capacity, slots, True), out_shape=[...  13 us
    pallas_call x1, Pallas kernels, local(): pl.pallas_call(bind(render_kernel, 0, capacity, capacity, False), out_sha...  12.9 us
    pallas_call x1, Pallas kernels, local(): pl.pallas_call(bind(update_kernel, capacity), out_shape=state + [shape((o...  6.9 us
    all_to_all x1, waiting for transfers between devices, row_exchange(): return lax.all_to_all(value, 'row', split_axis=0, concat_axis=0, tiled=True)  6.19 us
    pallas_call x1, Pallas kernels, local(): pl.pallas_call(final_kernel, out_shape=state, in_specs=[VM] * 9 + [SM], o...  6.01 us
    ppermute x6, waiting for transfers between devices, swap(): return lax.ppermute(value, axis, [(i, i ^ offset) for i in range(count)])  5.32 us
    ppermute x2, starting transfers between devices, turn(): lax.ppermute(value, axis, [(i, (i + offset) % count) for i in range(count)])  4.72 us
  transfers between devices with their start and end apart: 9, of which 4 were waited for; matrix products, arithmetic and copies ran while one was open for 1% of the time, Pallas kernels for 0%

profile of v1, /device:TPU:0, one launch (start us, length us, event | category | flops | bytes accessed | tf_op | source)
XLA Modules:
  0.0 129.2 jit_solution(6600904828917014019)
XLA Ops:
  0.6 1.7 %shard_map.129 = s32[8,1,128]{2,1,0:T(1,128)} custom-call(s32[2,1,4,4]{3,2,1,0:T(4,128)} %refs_2_.8, s32[2,1,4,4]{3,2,1,0:T(4,128)} %refs_3_.6, s32[1,2,2]{2,1,0:T(2,128)} %refs_9_.3), custom_call_target="tpu_custom_call" | custom-call | tf_op jit(solution)/shard_map/pallas_call | solution.py:663
  2.4 13.8 %all_to_all.25.refs_2_.refs_1_.refs_8_.refs_4_ = s32[8,1,128]{2,1,0:T(1,128)} all-to-all(s32[8,1,128]{2,1,0:T(1,128)} %shard_map.129), channel_id=1, replica_groups=mesh['row'=8,'rep'=4] {'row'}, dimensions={0} | all-to-all | bytes 8192 | tf_op jit(solution)/shard_map/all_to_all | solution.py:634
  16.2 3.1 %shard_map.130 = f32[8,40,128]{2,1,0:T(8,128)} custom-call(f32[59,4096]{1,0:T(8,128)} %refs_4_.2, f32[2,1,11]{2,1,0:T(1,128)} %refs_3_.7, s32[8,1,128]{2,1,0:T(1,128)} %all_to_all.25.refs_2_.refs_1_.refs_8_.refs_4_), custom_call_target="tpu_custom_call" | custom-call | tf_op jit(solution)/shard_map/pallas_call | solution.py:671
  19.3 3.5 %all-to-all-start.1 = ((f32[8,40,128]{2,1,0:T(8,128)}), f32[8,40,128]{2,1,0:T(8,128)S(1)}, u32[]{:S(2)}, u32[]{:S(2)}) async-start(f32[8,40,128]{2,1,0:T(8,128)} %shard_map.130), calls=%async_computation.1 | async-start | bytes 327680 | tf_op jit(solution)/shard_map/all_to_all | solution.py:634
  22.8 0.7 copy.14.refs_1_
  23.5 0.6 copy.15.refs_4_.refs_6_
  24.1 6.2 %all-to-all-done.1.refs_0_ = f32[8,40,128]{2,1,0:T(8,128)S(1)} async-done(((f32[8,40,128]{2,1,0:T(8,128)}), f32[8,40,128]{2,1,0:T(8,128)S(1)}, u32[]{:S(2)}, u32[]{:S(2)}) %all-to-all-start.1) | async-done | bytes 163872 | tf_op jit(solution)/shard_map/all_to_all | solution.py:634
  30.3 0.7 copy-done
  31.0 12.9 %shard_map.131 = (f32[2,1,4,3,256]{4,3,2,1,0:T(4,128)}, f32[8,40,128]{2,1,0:T(8,128)}) custom-call(f32[8,40,128]{2,1,0:T(8,128)} %copy-done, f32[2,1,4,2]{3,2,1,0:T(4,128)} %copy.14.refs_1_, s32[2,1,4,4]{3,2,1,0:T(4,128)} %refs_2_.8, s32[2,1,4,512]{3,2,1,0:T(4,128)} %refs_5_.3, f32[2,1,4,3,256]{4,3,2,1,0:T(4,128)} %copy.15.refs_4_.refs_6_), custom_call_target="tpu_custom_call" | custom-call | tf_op jit(solution)/shard_map/pallas_call | solution.py:698
  43.8 11.6 %all_to_all.26.refs_0_ = f32[8,40,128]{2,1,0:T(8,128)} all-to-all(f32[8,40,128]{2,1,0:T(8,128)} %get-tuple-element.17), channel_id=1, replica_groups=mesh['row'=8,'rep'=4] {'row'}, dimensions={0} | all-to-all | bytes 327680 | tf_op jit(solution)/shard_map/all_to_all | solution.py:634
  55.4 1.8 %shard_map.132.refs_0_ = f32[304,128]{1,0:T(8,128)} custom-call(f32[8,40,128]{2,1,0:T(8,128)} %all_to_all.26.refs_0_, s32[8,1,128]{2,1,0:T(1,128)} %all_to_all.25.refs_2_.refs_1_.refs_8_.refs_4_, s32[1,2,2]{2,1,0:T(2,128)} %refs_9_.3, f32[2,1,11]{2,1,0:T(1,128)} %refs_3_.7), custom_call_target="tpu_custom_call" | custom-call | tf_op jit(solution)/shard_map/pallas_call | solution.py:690
  57.2 1.5 %collective-permute-start.1 = (f32[304,128]{1,0:T(8,128)}, f32[304,128]{1,0:T(8,128)S(1)}, u32[]{:S(2)}, u32[]{:S(2)}) collective-permute-start(f32[304,128]{1,0:T(8,128)} %shard_map.132.refs_0_), channel_id=1, source_target_pairs={{0,2},{1,3},{2,0},{3,1},{4,6},{5,7},{6,4},{7,5},{8,10},{9,11},{10,... | collective-permute-start | bytes 466952 | tf_op jit(solution)/shard_map/ppermute | solution.py:618
  58.7 3.9 %collective-permute-done.1.refs_2_ = f32[304,128]{1,0:T(8,128)S(1)} collective-permute-done((f32[304,128]{1,0:T(8,128)}, f32[304,128]{1,0:T(8,128)S(1)}, u32[]{:S(2)}, u32[]{:S(2)}) %collective-permute-start.1) | collective-permute-done | bytes 155680 | tf_op jit(solution)/shard_map/ppermute | solution.py:618
  62.7 1.4 %collective-permute-done.2.refs_3_ = f32[304,128]{1,0:T(8,128)S(1)} collective-permute-done((f32[304,128]{1,0:T(8,128)S(1)}, f32[304,128]{1,0:T(8,128)S(1)}, u32[]{:S(2)}, u32[]{:S(2)}) %collective-permute-start.2) | collective-permute-done | bytes 155680 | tf_op jit(solution)/shard_map/ppermute | solution.py:618
  64.0 0.7 copy-done.8
  64.7 6.9 %shard_map.133 = (f32[59,4096]{1,0:T(8,128)}, f32[59,4096]{1,0:T(8,128)}, f32[59,4096]{1,0:T(8,128)}, f32[8,40,128]{2,1,0:T(8,128)}, f32[3,59,256]{2,1,0:T(8,128)}, /*index=5*/f32[3,59,256]{2,1,0:T(8,128)}) custom-call(f32[304,128]{1,0:T(8,128)} %shard_map.132.refs_0_, f32[304,128]{1,0:T(8,128)} %copy-done.7, f32[304,128]{1,0:T(8,128)} %copy-done.6, ...), custom_call_target="tpu_custom_call" | custom-call | tf_op jit(solution)/shard_map/pallas_call | solution.py:708
  71.6 12.0 %all_to_all.27.refs_0_ = f32[8,40,128]{2,1,0:T(8,128)} all-to-all(f32[8,40,128]{2,1,0:T(8,128)} %get-tuple-element.18), channel_id=1, replica_groups=mesh['row'=8,'rep'=4] {'row'}, dimensions={0} | all-to-all | bytes 327680 | tf_op jit(solution)/shard_map/all_to_all | solution.py:634
  83.7 13.0 %shard_map.134 = (f32[2,1,4,3,256]{4,3,2,1,0:T(4,128)}, f32[8,72,128]{2,1,0:T(8,128)}) custom-call(f32[8,40,128]{2,1,0:T(8,128)} %all_to_all.27.refs_0_, f32[2,1,4,2]{3,2,1,0:T(4,128)} %copy.14.refs_1_, s32[2,1,4,4]{3,2,1,0:T(4,128)} %refs_2_.8, s32[2,1,4,4]{3,2,1,0:T(4,128)} %refs_3_.6, s32[8,1,128]{2,1,0:T(1,128)} %all_to_all.25.refs_2_.refs_1_.refs_8_.refs_4_, ...), custom_call_target="tpu_custom_call" | custom-call | tf_op jit(solution)/shard_map/pallas_call | solution.py:720
  96.7 13.6 %all_to_all.28.refs_0_ = f32[8,72,128]{2,1,0:T(8,128)} all-to-all(f32[8,72,128]{2,1,0:T(8,128)} %get-tuple-element.20), channel_id=1, replica_groups=mesh['row'=8,'rep'=4] {'row'}, dimensions={0} | all-to-all | bytes 589824 | tf_op jit(solution)/shard_map/all_to_all | solution.py:634
  110.3 2.1 %shard_map.135.refs_0_ = f32[304,128]{1,0:T(8,128)} custom-call(f32[8,72,128]{2,1,0:T(8,128)} %all_to_all.28.refs_0_, s32[8,1,128]{2,1,0:T(1,128)} %all_to_all.25.refs_2_.refs_1_.refs_8_.refs_4_, s32[1,2,2]{2,1,0:T(2,128)} %refs_9_.3, f32[2,1,11]{2,1,0:T(1,128)} %refs_3_.7), custom_call_target="tpu_custom_call" | custom-call | tf_op jit(solution)/shard_map/pallas_call | solution.py:690
  112.4 1.5 %collective-permute-start.4 = (f32[304,128]{1,0:T(8,128)}, f32[304,128]{1,0:T(8,128)S(1)}, u32[]{:S(2)}, u32[]{:S(2)}) collective-permute-start(f32[304,128]{1,0:T(8,128)} %shard_map.135.refs_0_), channel_id=1, source_target_pairs={{0,2},{1,3},{2,0},{3,1},{4,6},{5,7},{6,4},{7,5},{8,10},{9,11},{10,... | collective-permute-start | bytes 466952 | tf_op jit(solution)/shard_map/ppermute | solution.py:618
  113.9 0.7 collective-permute-start.6
  114.6 4.0 %collective-permute-start.7 = (f32[3,59,256]{2,1,0:T(8,128)S(1)}, f32[3,59,256]{2,1,0:T(8,128)S(1)}, u32[]{:S(2)}, u32[]{:S(2)}) collective-permute-start(f32[3,59,256]{2,1,0:T(8,128)S(1)} %copy-done.12), channel_id=1, source_target_pairs={{0,28},{4,0},{8,4},{12,8},{16,12},{20,16},{24,20},{28,24},{1,29},{... | collective-permute-start | bytes 543752 | tf_op jit(solution)/shard_map/ppermute | solution.py:623
  118.6 0.5 collective-permute-start.5
  119.1 0.6 copy.18
  119.7 2.6 %collective-permute-done.6.refs_7_ = f32[3,59,256]{2,1,0:T(8,128)S(1)} collective-permute-done((f32[3,59,256]{2,1,0:T(8,128)S(1)}, f32[3,59,256]{2,1,0:T(8,128)S(1)}, u32[]{:S(2)}, u32[]{:S(2)}) %collective-permute-start.6) | collective-permute-done | bytes 181280 | tf_op jit(solution)/shard_map/ppermute | solution.py:623
  122.3 0.0 collective-permute-done.7.refs_8_
  122.4 0.6 copy-done.1
  123.0 0.1 copy-done.2
  123.1 0.1 copy-done.4
  123.1 0.0 copy-done.5
  123.2 6.0 %shard_map.136 = (f32[59,4096]{1,0:T(8,128)}, f32[59,4096]{1,0:T(8,128)}, f32[59,4096]{1,0:T(8,128)}) custom-call(f32[304,128]{1,0:T(8,128)} %shard_map.135.refs_0_, f32[304,128]{1,0:T(8,128)} %copy-done.4, f32[304,128]{1,0:T(8,128)} %copy-done.3, f32[304,128]{1,0:T(8,128)} %copy-done.5, f32[59,4096]{1,0:T(8,128)} %get-tuple-element.21.refs_4_, ...), custom_call_target="tpu_custom_call" | custom-call | tf_op jit(solution)/shard_map/pallas_call | solution.py:729
  (29 shorter events, 0.1 us)
Async XLA Ops:
  19.3 3.5 %copy-start.11 = (f32[2,1,4,2]{2,3,1,0:T(2,128)S(1)}, f32[2,1,4,2]{2,3,1,0:T(2,128)}, u32[]{:S(2)}) copy-start(f32[2,1,4,2]{2,3,1,0:T(2,128)} %param.14) | copy-start | bytes 196
  19.3 4.2 %copy-start.10 = (f32[2,1,4,3,256]{4,2,3,1,0:T(4,128)S(1)}, f32[2,1,4,3,256]{4,2,3,1,0:T(4,128)}, u32[]{:S(2)}) copy-start(f32[2,1,4,3,256]{4,2,3,1,0:T(4,128)} %param.18) | copy-start | bytes 73732
  19.3 11.0 %all-to-all-start.1 = ((f32[8,40,128]{2,1,0:T(8,128)}), f32[8,40,128]{2,1,0:T(8,128)S(1)}, u32[]{:S(2)}, u32[]{:S(2)}) async-start(f32[8,40,128]{2,1,0:T(8,128)} %shard_map.130), calls=%async_computation.1 | async-start | bytes 327680 | tf_op jit(solution)/shard_map/all_to_all | solution.py:634
  30.3 0.7 copy-start
  57.2 5.4 %collective-permute-start.1 = (f32[304,128]{1,0:T(8,128)}, f32[304,128]{1,0:T(8,128)S(1)}, u32[]{:S(2)}, u32[]{:S(2)}) collective-permute-start(f32[304,128]{1,0:T(8,128)} %shard_map.132.refs_0_), channel_id=1, source_target_pairs={{0,2},{1,3},{2,0},{3,1},{4,6},{5,7},{6,4},{7,5},{8,10},{9,11},{10,... | collective-permute-start | bytes 466952 | tf_op jit(solution)/shard_map/ppermute | solution.py:618
  58.7 4.0 %collective-permute-start = (f32[304,128]{1,0:T(8,128)}, f32[304,128]{1,0:T(8,128)S(1)}, u32[]{:S(2)}, u32[]{:S(2)}) collective-permute-start(f32[304,128]{1,0:T(8,128)} %shard_map.132.refs_0_), channel_id=1, source_target_pairs={{0,1},{1,0},{2,3},{3,2},{4,5},{5,4},{6,7},{7,6},{8,9},{9,8},{10,11... | collective-permute-start | bytes 466952 | tf_op jit(solution)/shard_map/ppermute | solution.py:618
  62.7 1.4 %copy-start.6 = (f32[304,128]{1,0:T(8,128)}, f32[304,128]{1,0:T(8,128)S(1)}, u32[]{:S(2)}) copy-start(f32[304,128]{1,0:T(8,128)S(1)} %collective-permute-done.1.refs_2_) | copy-start | bytes 466948
  62.7 1.4 %collective-permute-start.2 = (f32[304,128]{1,0:T(8,128)S(1)}, f32[304,128]{1,0:T(8,128)S(1)}, u32[]{:S(2)}, u32[]{:S(2)}) collective-permute-start(f32[304,128]{1,0:T(8,128)S(1)} %collective-permute-done.1.refs_2_), channel_id=1, source_target_pairs={{0,1},{1,0},{2,3},{3,2},{4,5},{5,4},{6,7},{7,6},{8,9},{9,8},{10,11... | collective-permute-start | bytes 466952 | tf_op jit(solution)/shard_map/ppermute | solution.py:618
  62.7 1.4 %copy-start.7 = (f32[304,128]{1,0:T(8,128)}, f32[304,128]{1,0:T(8,128)S(1)}, u32[]{:S(2)}) copy-start(f32[304,128]{1,0:T(8,128)S(1)} %collective-permute-done.refs_1_) | copy-start | bytes 466948
  64.0 0.7 copy-start.8
  110.3 3.6 %copy-start.13 = (f32[3,59,256]{2,1,0:T(8,128)S(1)}, f32[3,59,256]{2,1,0:T(8,128)}, u32[]{:S(2)}) copy-start(f32[3,59,256]{2,1,0:T(8,128)} %get-tuple-element.24) | copy-start | bytes 543748
  110.3 4.3 %copy-start.12 = (f32[3,59,256]{2,1,0:T(8,128)S(1)}, f32[3,59,256]{2,1,0:T(8,128)}, u32[]{:S(2)}) copy-start(f32[3,59,256]{2,1,0:T(8,128)} %get-tuple-element.25) | copy-start | bytes 543748
  110.3 8.8 %copy-start.9 = (f32[2,1,4,3,256]{4,3,2,1,0:T(4,128)S(1)}, f32[2,1,4,3,256]{4,3,2,1,0:T(4,128)}, u32[]{:S(2)}) copy-start(f32[2,1,4,3,256]{4,3,2,1,0:T(4,128)} %get-tuple-element.33) | copy-start | bytes 73732
  112.4 6.2 %collective-permute-start.4 = (f32[304,128]{1,0:T(8,128)}, f32[304,128]{1,0:T(8,128)S(1)}, u32[]{:S(2)}, u32[]{:S(2)}) collective-permute-start(f32[304,128]{1,0:T(8,128)} %shard_map.135.refs_0_), channel_id=1, source_target_pairs={{0,2},{1,3},{2,0},{3,1},{4,6},{5,7},{6,4},{7,5},{8,10},{9,11},{10,... | collective-permute-start | bytes 466952 | tf_op jit(solution)/shard_map/ppermute | solution.py:618
  113.9 8.5 %collective-permute-start.6 = (f32[3,59,256]{2,1,0:T(8,128)S(1)}, f32[3,59,256]{2,1,0:T(8,128)S(1)}, u32[]{:S(2)}, u32[]{:S(2)}) collective-permute-start(f32[3,59,256]{2,1,0:T(8,128)S(1)} %copy-done.13), channel_id=1, source_target_pairs={{0,4},{4,8},{8,12},{12,16},{16,20},{20,24},{24,28},{28,0},{1,5},{5... | collective-permute-start | bytes 543752 | tf_op jit(solution)/shard_map/ppermute | solution.py:623
  114.6 7.8 %collective-permute-start.7 = (f32[3,59,256]{2,1,0:T(8,128)S(1)}, f32[3,59,256]{2,1,0:T(8,128)S(1)}, u32[]{:S(2)}, u32[]{:S(2)}) collective-permute-start(f32[3,59,256]{2,1,0:T(8,128)S(1)} %copy-done.12), channel_id=1, source_target_pairs={{0,28},{4,0},{8,4},{12,8},{16,12},{20,16},{24,20},{28,24},{1,29},{... | collective-permute-start | bytes 543752 | tf_op jit(solution)/shard_map/ppermute | solution.py:623
  118.6 3.8 %collective-permute-start.3 = (f32[304,128]{1,0:T(8,128)}, f32[304,128]{1,0:T(8,128)S(1)}, u32[]{:S(2)}, u32[]{:S(2)}) collective-permute-start(f32[304,128]{1,0:T(8,128)} %shard_map.135.refs_0_), channel_id=1, source_target_pairs={{0,1},{1,0},{2,3},{3,2},{4,5},{5,4},{6,7},{7,6},{8,9},{9,8},{10,11... | collective-permute-start | bytes 466952 | tf_op jit(solution)/shard_map/ppermute | solution.py:618
  118.6 3.8 %copy-start.3 = (f32[304,128]{1,0:T(8,128)}, f32[304,128]{1,0:T(8,128)S(1)}, u32[]{:S(2)}) copy-start(f32[304,128]{1,0:T(8,128)S(1)} %collective-permute-done.4.refs_2_) | copy-start | bytes 466948
  118.6 3.8 %collective-permute-start.5 = (f32[304,128]{1,0:T(8,128)S(1)}, f32[304,128]{1,0:T(8,128)S(1)}, u32[]{:S(2)}, u32[]{:S(2)}) collective-permute-start(f32[304,128]{1,0:T(8,128)S(1)} %collective-permute-done.4.refs_2_), channel_id=1, source_target_pairs={{0,1},{1,0},{2,3},{3,2},{4,5},{5,4},{6,7},{7,6},{8,9},{9,8},{10,11... | collective-permute-start | bytes 466952 | tf_op jit(solution)/shard_map/ppermute | solution.py:618
  122.3 0.7 copy-start.1
  122.4 0.7 copy-start.2
  122.4 0.8 copy-start.4
  122.4 0.8 copy-start.5

commit v2 on v1

--- a/solution.py
+++ b/solution.py
@@ -15,7 +15,6 @@
 MIGH = 2
 DEPTH = 512
 SIDE = 16
-HALF = DEPTH // 2
 MIG_LANE = 64
 CAM_ROWS = 16
 LOG2E = 1.4426950408889634
@@ -208,77 +207,102 @@
     serve(0, capacity, blocks, camera_ref, asked_ref, dense, table, faint, out_ref)
 
 
+def pixel_features(rows, per):
+    pixel = lax.broadcasted_iota(jnp.int32, (rows, PIX), 1)
+    which = lax.broadcasted_iota(jnp.int32, (rows, PIX), 0) // per
+    px = (pixel % SIDE).astype(f32) - (SIDE / 2 - 0.5)
+    py = (pixel // SIDE).astype(f32) - (SIDE / 2 - 0.5)
+    chosen = jnp.where(which == 0, 1.0, 0.0)
+    for index, value in enumerate((px, py, px * px, px * py, py * py)):
+        chosen = jnp.where(which == index + 1, value, chosen)
+    return chosen.astype(bf16)
+
+
+def lane_gather(pieces, within, source):
+    got = jnp.take_along_axis(pieces[0], within, axis=1)
+    for j in range(1, len(pieces)):
+        got = jnp.where(source == j, jnp.take_along_axis(pieces[j], within, axis=1), got)
+    return got
+
+
 def render_kernel(step, capacity, slots, final, *refs):
     if final:
         (
             arrived, corner_ref, owner_ref, block_ref, asked_ref, order_ref, target_ref, earlier_ref,
-            picture_ref, out_ref, onehot, upper, lower, features, flat, coeffs,
+            picture_ref, out_ref, onehot, coeffs, alphas, locals_, weights, weight_h, weight_m,
+            flows, behind, heat_h, heat_m,
         ) = refs
         for other in range(ITERS - 1):
             picture_ref[other] = earlier_ref[other]
     else:
         (
             arrived, corner_ref, owner_ref, order_ref, target_ref,
-            picture_ref, out_ref, onehot, upper, lower, features, flat, coeffs,
+            picture_ref, out_ref, onehot, coeffs, alphas, locals_, weights, weight_h, weight_m,
+            flows, behind, heat_h, heat_m,
         ) = refs
     owners = arrived.shape[0]
     tiles = owner_ref.shape[2]
+    lists = DEPTH // BLOCK
+    segments = 8
+    steps = DEPTH // segments
     out_ref[...] = jnp.zeros_like(out_ref)
-
-    first = lax.broadcasted_iota(jnp.int32, (HALF, HALF), 0)
-    second = lax.broadcasted_iota(jnp.int32, (HALF, HALF), 1)
-    upper[...] = jnp.where(first < second, 1.0, 0.0).astype(bf16)
-    lower[...] = jnp.where(first > second, 1.0, 0.0).astype(bf16)
-    pixel = lax.broadcasted_iota(jnp.int32, (PIX, BLOCK), 0)
-    which = lax.broadcasted_iota(jnp.int32, (PIX, BLOCK), 1) // 3
-    px = (pixel % SIDE).astype(f32) - (SIDE / 2 - 0.5)
-    py = (pixel // SIDE).astype(f32) - (SIDE / 2 - 0.5)
-    chosen = jnp.where(which == 0, 1.0, 0.0)
-    for index, value in enumerate((px, py, px * px, px * py, py * py)):
-        chosen = jnp.where(which == index + 1, value, chosen)
-    features[...] = chosen.astype(bf16)
-    pixel = lax.broadcasted_iota(jnp.int32, (16, PIX), 1)
-    which = lax.broadcasted_iota(jnp.int32, (16, PIX), 0)
-    px = (pixel % SIDE).astype(f32) - (SIDE / 2 - 0.5)
-    py = (pixel // SIDE).astype(f32) - (SIDE / 2 - 0.5)
-    chosen = jnp.where(which == 0, 1.0, 0.0)
-    for index, value in enumerate((px, py, px * px, px * py, py * py)):
-        chosen = jnp.where(which == index + 1, value, chosen)
-    flat[...] = chosen.astype(bf16)
     coeffs[...] = jnp.zeros_like(coeffs)
+    features = pixel_features(32, 3)
+    flat = pixel_features(16, 1)
 
     names = [owner_ref[step, 0, t, j] for t in range(tiles) for j in range(LISTB)]
     ranks = [rank_of(names, index) for index in range(tiles * LISTB)]
 
+    order = order_ref[step, 0]
+    order = jnp.concatenate([order, order], axis=0) if tiles == 4 else order
+    order_pieces = [order[:, k * BLOCK : (k + 1) * BLOCK] for k in range(lists)]
+    woven = []
+    for k in range(lists):
+        row = lax.broadcasted_iota(jnp.int32, order_pieces[0].shape, 1) + k * BLOCK
+        nth = (row % segments) * steps + row // segments
+        woven.append(lane_gather(order_pieces, nth & (BLOCK - 1), nth // BLOCK))
+    all_within = [piece & (BLOCK - 1) for piece in woven]
+    all_source = [piece // BLOCK for piece in woven]
+    faint_pieces = []
+    for j in range(LISTB):
+        parts = [
+            arrived[
+                names[t * LISTB + j], pl.ds(8 * capacity + ranks[t * LISTB + j], 1), :
+            ]
+            for t in range(tiles)
+        ]
+        faint_pieces.append(jnp.concatenate(parts * (8 // tiles), axis=0))
+    all_faint = [
+        lane_gather(faint_pieces, all_within[k], all_source[k]) for k in range(lists)
+    ]
+    row_id = lax.broadcasted_iota(jnp.int32, (BLOCK, BLOCK), 0).astype(f32).astype(bf16)
+    sub = lax.broadcasted_iota(jnp.int32, (segments, PIX), 0)
+
     for tile in range(tiles):
-        order = order_ref[step, 0, tile : tile + 1, :]
-        for piece in range(DEPTH // BLOCK):
-            ids = lax.broadcasted_iota(jnp.int32, (BLOCK, DEPTH), 0) + piece * BLOCK
-            onehot[piece * BLOCK : (piece + 1) * BLOCK, :] = jnp.where(
-                ids == order, 1.0, 0.0
-            ).astype(bf16)
-        pieces, dims = [], []
-        for j in range(LISTB):
-            name, rank = names[tile * LISTB + j], ranks[tile * LISTB + j]
-            pieces.append(arrived[name, pl.ds(pl.multiple_of(rank * 8, 8), 8), :])
-            dims.append(
-                jnp.broadcast_to(arrived[name, pl.ds(8 * capacity + rank, 1), :], (8, BLOCK))
-            )
-        sorted_rows, sorted_dim = [], []
-        for piece in range(DEPTH // BLOCK):
-            ids = jnp.broadcast_to(order[:, piece * BLOCK : (piece + 1) * BLOCK], (8, BLOCK))
-            within, source = ids & (BLOCK - 1), ids // BLOCK
-            got = jnp.take_along_axis(pieces[0], within, axis=1)
-            dim = jnp.take_along_axis(dims[0], within, axis=1)
-            for j in range(1, LISTB):
-                got = jnp.where(source == j, jnp.take_along_axis(pieces[j], within, axis=1), got)
-                dim = jnp.where(source == j, jnp.take_along_axis(dims[j], within, axis=1), dim)
-            sorted_rows.append(got)
-            sorted_dim.append(dim)
+        one = slice(tile, tile + 1)
+        pieces = [
+            arrived[
+                names[tile * LISTB + j],
+                pl.ds(pl.multiple_of(ranks[tile * LISTB + j] * 8, 8), 8),
+                :,
+            ]
+            for j in range(LISTB)
+        ]
+        sorted_rows = []
+        for k in range(lists):
+            within = jnp.broadcast_to(all_within[k][one], (8, BLOCK))
+            source = jnp.broadcast_to(all_source[k][one], (8, BLOCK))
+            sorted_rows.append(lane_gather(pieces, within, source))
+            local = woven[k][one].astype(f32)
+            for piece in range(lists):
+                inside = jnp.where(all_source[k][one] == piece, local - piece * BLOCK, -1.0)
+                onehot[
+                    piece * BLOCK : (piece + 1) * BLOCK, k * BLOCK : (k + 1) * BLOCK
+                ] = jnp.where(row_id == inside.astype(bf16), jnp.ones((), bf16), jnp.zeros((), bf16))
         rows = jnp.concatenate(sorted_rows, axis=1)
-        faint = jnp.concatenate(sorted_dim, axis=1)[0:1]
-        u = rows[0:1] - (corner_ref[step, 0, tile, 0] + SIDE / 2)
-        v = rows[1:2] - (corner_ref[step, 0, tile, 1] + SIDE / 2)
+        faint = jnp.concatenate([part[one] for part in all_faint], axis=1)
+        u = rows[0:1] - (corner_ref[step, 0, 0, tile] + SIDE / 2)
+        v = rows[1:2] - (corner_ref[step, 0, 1, tile] + SIDE / 2)
         a, b, c = rows[2:3], rows[3:4], rows[4:5]
         colours = rows[5:8]
         half_a, half_b, half_c = (-0.5 * LOG2E) * a, -LOG2E * b, (-0.5 * LOG2E) * c
@@ -300,44 +324,61 @@
             [col_h, col_m, col_h, col_m, col_l, col_h], axis=0
         ).astype(bf16)
 
-        step_rows = 128
-        moments = jnp.zeros((16, DEPTH), f32)
-        col_grads = jnp.zeros((9, DEPTH), f32)
-        for at in range(0, PIX, step_rows):
-            feats = features[at : at + step_rows, 0:32]
-            power = dot(feats, form)
-            alpha = jnp.exp2(power)
-            keep = jnp.log(1.0 - alpha)
-            ratio = jnp.exp2(power - LOG2E * keep)
-            keep_h, keep_m = split(keep, 2)
-            tri = upper[...]
-            near = dot(keep_h[:, :HALF], tri) + dot(keep_m[:, :HALF], tri)
-            far = dot(keep_h[:, HALF:], tri) + dot(keep_m[:, HALF:], tri)
-            far = far + (near[:, HALF - 1 : HALF] + keep[:, HALF - 1 : HALF])
-            weight = alpha * jnp.exp(jnp.concatenate([near, far], axis=1))
-            weight_h, weight_m = split(weight, 2)
-            shades = dot(col_left, weight_h, NT) + dot(col_left, weight_m, NT)
-            shades = shades[0:3] + shades[3:6] + shades[6:9]
-            if final:
-                picture_ref[step, 0, tile, :, at : at + step_rows] = shades
-            else:
-                picture_ref[step, 0, tile, :, at : at + step_rows] = shades
-            error = shades - target_ref[step, 0, tile, :, at : at + step_rows]
-            err_h, err_m, err_l = [part.astype(f32) for part in split(error, 3)]
-            err_left = jnp.concatenate([err_h, err_m, err_l], axis=0).astype(bf16)
-            err_right = jnp.concatenate(
-                [err_h, err_h, err_m, err_m, err_h, err_l], axis=0
-            ).astype(bf16)
-            col_grads = col_grads + dot(err_left, weight_h) + dot(err_left, weight_m)
-            flow = weight * dot(err_right, col_right, TN)
-            flow_h, flow_m = split(flow, 2)
-            tri = lower[...]
-            far = dot(flow_h[:, HALF:], tri) + dot(flow_m[:, HALF:], tri)
-            near = dot(flow_h[:, :HALF], tri) + dot(flow_m[:, :HALF], tri)
-            near = near + (far[:, 0:1] + flow[:, HALF : HALF + 1])
-            heat = flow - ratio * jnp.concatenate([near, far], axis=1)
-            for part in split(heat, 3):
-                moments = moments + dot(flat[:, at : at + step_rows], part)
+        passed = jnp.ones((segments, PIX), f32)
+        for k in range(lists):
+            power = dot(form[:, k * BLOCK : (k + 1) * BLOCK], features, TN)
+            for at in range(0, BLOCK, segments):
+                here = slice(k * BLOCK + at, k * BLOCK + at + segments)
+                alpha = jnp.exp2(power[at : at + segments])
+                alphas[here, :] = alpha
+                locals_[here, :] = passed
+                passed = passed * (1.0 - alpha)
+        for shift in (1, 2, 4):
+            passed = passed * jnp.where(sub >= shift, pltpu.roll(passed, shift, 0), 1.0)
+        passed = jnp.where(sub >= 1, pltpu.roll(passed, 1, 0), 1.0)
+        passed = jnp.concatenate([passed, passed], axis=0)
+        for at in range(0, DEPTH, 2 * segments):
+            here = slice(at, at + 2 * segments)
+            weight = alphas[here, :] * (locals_[here, :] * passed)
+            weights[here, :] = weight
+            weight_h[here, :], weight_m[here, :] = split(weight, 2)
+
+        shades = dot(col_left, weight_h[...]) + dot(col_left, weight_m[...])
+        shades = shades[0:3] + shades[3:6] + shades[6:9]
+        for k in range(3):
+            picture_ref[step, 0, k, one, :] = shades[k : k + 1]
+        error = shades - jnp.concatenate(
+            [target_ref[step, 0, k, one, :] for k in range(3)], axis=0
+        )
+        err_h, err_m, err_l = [part.astype(f32) for part in split(error, 3)]
+        err_left = jnp.concatenate([err_h, err_m, err_l], axis=0).astype(bf16)
+        err_right = jnp.concatenate(
+            [err_h, err_h, err_m, err_m, err_h, err_l], axis=0
+        ).astype(bf16)
+        col_grads = dot(err_left, weight_h[...], NT) + dot(err_left, weight_m[...], NT)
+
+        total = jnp.zeros((segments, PIX), f32)
+        for k in reversed(range(lists)):
+            seen = dot(col_right[:, k * BLOCK : (k + 1) * BLOCK], err_right, TN)
+            for at in reversed(range(0, BLOCK, segments)):
+                here = slice(k * BLOCK + at, k * BLOCK + at + segments)
+                flow = weights[here, :] * seen[at : at + segments]
+                flows[here, :] = flow
+                behind[here, :] = total
+                total = total + flow
+        for shift in (1, 2, 4):
+            total = total + jnp.where(
+                sub < segments - shift, pltpu.roll(total, segments - shift, 0), 0.0
+            )
+        total = jnp.where(sub < segments - 1, pltpu.roll(total, segments - 1, 0), 0.0)
+        total = jnp.concatenate([total, total], axis=0)
+        for at in range(0, DEPTH, 2 * segments):
+            here = slice(at, at + 2 * segments)
+            alpha = alphas[here, :]
+            heat = flows[here, :] - (alpha / (1.0 - alpha)) * (behind[here, :] + total)
+            heat_h[here, :], heat_m[here, :] = split(heat, 2)
+        moments = dot(flat, heat_h[...], NT) + dot(flat, heat_m[...], NT)
+
         col_grads = col_grads[0:3] + col_grads[3:6] + col_grads[6:9]
         m00, m10, m01 = moments[0:1], moments[1:2], moments[2:3]
         m20, m11, m02 = moments[3:4], moments[4:5], moments[5:6]
@@ -353,26 +394,21 @@
             jnp.zeros((7, DEPTH), f32),
         ]
         grads = jnp.concatenate(grads, axis=0)
-        listed = jnp.zeros((16, DEPTH), f32)
-        for part in split(grads, 3):
-            listed = listed + dot(part, onehot[...], NT)
+        listed = dot(jnp.concatenate(split(grads, 3), axis=0), onehot[...], NT)
+        listed = listed[0:16] + listed[16:32] + listed[32:48]
         for j in range(LISTB):
             name, rank = names[tile * LISTB + j], ranks[tile * LISTB + j]
             if final:
                 block = block_ref[step, 0, tile, j]
+                hop = jnp.int32(0)
                 for k in range(MIGH):
                     goes_left = asked_ref[name, 0, MIG_LANE + k] == block
                     goes_right = asked_ref[name, 0, MIG_LANE + MIGH + k] == block
                     rank = jnp.where(goes_left, capacity + MIGH + k, rank)
                     rank = jnp.where(goes_right, capacity + k, rank)
-                goes_left = jnp.bool_(False)
-                goes_right = jnp.bool_(False)
-                for k in range(MIGH):
-                    goes_left |= asked_ref[name, 0, MIG_LANE + k] == block
-                    goes_right |= asked_ref[name, 0, MIG_LANE + MIGH + k] == block
-                below = jnp.where(name == 0, owners - 1, name - 1)
-                above = jnp.where(name == owners - 1, 0, name + 1)
-                name = jnp.where(goes_left, below, jnp.where(goes_right, above, name))
+                    hop = hop - goes_left.astype(jnp.int32) + goes_right.astype(jnp.int32)
+                name = name + hop
+                name = jnp.where(name < 0, owners - 1, jnp.where(name >= owners, 0, name))
             lanes = slice(j * BLOCK, (j + 1) * BLOCK)
             main = pl.ds(pl.multiple_of(rank * 8, 8), 8)
             extra = pl.ds(8 * slots + rank, 1)
@@ -516,7 +552,8 @@
 def adam(value, first, second, gradient):
     first = 0.9 * first + 0.1 * gradient
     second = 0.999 * second + 0.001 * gradient * gradient
-    return value - learn_rate * first / (jnp.sqrt(second) + adam_epsilon), first, second
+    root = second * lax.rsqrt(second)
+    return value - learn_rate * first / (root + adam_epsilon), first, second
 
 
 def update_kernel(capacity, *refs):
@@ -676,15 +713,16 @@
         scratch_shapes=[dense, table, faint],
     )(params, camera, asked)
 
+    deep = pltpu.VMEM((DEPTH, PIX), f32)
+    packed = pltpu.VMEM((DEPTH, PIX), bf16)
     render_scratch = [
         pltpu.VMEM((DEPTH, DEPTH), bf16),
-        pltpu.VMEM((HALF, HALF), bf16),
-        pltpu.VMEM((HALF, HALF), bf16),
-        pltpu.VMEM((PIX, BLOCK), bf16),
-        pltpu.VMEM((16, PIX), bf16),
         pltpu.VMEM((32, DEPTH), f32),
+        deep, deep, deep, packed, packed, deep, deep, packed, packed,
     ]
-    pictures_shape = shape(targets.shape)
+    corners = jnp.swapaxes(tile_corner, 2, 3)
+    photos = jnp.swapaxes(targets, 2, 3)
+    pictures_shape = shape(photos.shape)
 
     def gather(step, count, returned):
         return pl.pallas_call(
@@ -701,7 +739,7 @@
         in_specs=[VM, SM, SM, VM, VM],
         out_specs=[VM, VM],
         scratch_shapes=render_scratch,
-    )(arrived, tile_corner, tile_owner, depth_order, targets)
+    )(arrived, corners, tile_owner, depth_order, photos)
     own = gather(0, capacity, row_exchange(back))
     near, far, cross = exchange(own)
     leaving = shape((3, P_SIZE, MIGH * BLOCK))
@@ -723,7 +761,7 @@
         in_specs=[VM, SM, SM, SM, SM, VM, VM, VM],
         out_specs=[VM, VM],
         scratch_shapes=render_scratch,
-    )(arrived, tile_corner, tile_owner, tile_block, asked, depth_order, targets, pictures)
+    )(arrived, corners, tile_owner, tile_block, asked, depth_order, photos, pictures)
     own = gather(1, slots, row_exchange(back))
     near, far, cross = exchange(own)
     current, moment_one, moment_two = pl.pallas_call(
@@ -733,7 +771,7 @@
         out_specs=[VM] * 3,
         scratch_shapes=[cams, dense, dense],
     )(own, near, far, cross, current, moment_one, moment_two, below, above, migration)
-    return current, moment_one, moment_two, pictures
+    return current, moment_one, moment_two, jnp.swapaxes(pictures, 2, 3)
 
 
 def solution(mesh):

time: 130 us -> 119 us (0.915)
  blocking collectives: 51 us -> 62.5 us
  Pallas kernels: 47.5 us -> 36.9 us
  waiting for transfers between devices: 14.1 us -> 8.55 us
  starting transfers between devices: 11.7 us -> 8.21 us
  local copies, waits for them, and re-layouts: 4.06 us -> 1.51 us
    all_to_all x4 -> x5, blocking collectives: 51 us -> 62.5 us  [row_exchange(): return lax.all_to_all(value, 'row', split_axis=0, concat_axis=0, tiled=True)]
    all_to_all x1 -> x0, waiting for transfers between devices: 6.19 us -> none  [row_exchange(): return lax.all_to_all(value, 'row', split_axis=0, concat_axis=0, tiled=True)]
    pallas_call x1, Pallas kernels: 12.9 us -> 7.68 us  [local(): pl.pallas_call(bind(render_kernel, 0, capacity, capacity, False), out_sha...]
    pallas_call x1, Pallas kernels: 13 us -> 7.86 us  [local(): pl.pallas_call(bind(render_kernel, 1, capacity, slots, True), out_shape=[...]
    all_to_all x1 -> x0, starting transfers between devices: 3.51 us -> none  [row_exchange(): return lax.all_to_all(value, 'row', split_axis=0, concat_axis=0, tiled=True)]
    unnamed x31 -> x20, local copies, waits for them, and re-layouts: 4.06 us -> 1.51 us
  transfers between devices with their start and end apart: 9 -> 8, of which waited for: 4 -> 3; matrix products, arithmetic and copies ran while one was open for 1% -> 0% of each run, Pallas kernels for 0% -> 0%
where the time goes in v2:
time: 119 us; the launch traced here: 118 us
  blocking collectives  62.5 us (53%)
  Pallas kernels  36.9 us (31%)
  waiting for transfers between devices  8.55 us (7%)
  starting transfers between devices  8.21 us (7%)
  local copies, waits for them, and re-layouts  1.51 us (1%)
    all_to_all x5, blocking collectives, row_exchange(): return lax.all_to_all(value, 'row', split_axis=0, concat_axis=0, tiled=True)  62.5 us
    pallas_call x1, Pallas kernels, local(): pl.pallas_call(bind(render_kernel, 1, capacity, slots, True), out_shape=[...  7.86 us
    pallas_call x1, Pallas kernels, local(): pl.pallas_call(bind(render_kernel, 0, capacity, capacity, False), out_sha...  7.68 us
    pallas_call x1, Pallas kernels, local(): pl.pallas_call(bind(update_kernel, capacity), out_shape=state + [shape((o...  6.87 us
    pallas_call x1, Pallas kernels, local(): pl.pallas_call(final_kernel, out_shape=state, in_specs=[VM] * 9 + [SM], o...  5.83 us
    ppermute x6, waiting for transfers between devices, swap(): return lax.ppermute(value, axis, [(i, i ^ offset) for i in range(count)])  5.32 us
    ppermute x2, starting transfers between devices, turn(): lax.ppermute(value, axis, [(i, (i + offset) % count) for i in range(count)])  4.72 us
    pallas_call x2, Pallas kernels, gather(): pl.pallas_call(bind(gather_kernel, step, capacity, count), out_shape=shap...  3.86 us
  transfers between devices with their start and end apart: 8, of which 3 were waited for; matrix products, arithmetic and copies ran while one was open for 0% of the time, Pallas kernels for 0%

profile of v2, /device:TPU:0, one launch (start us, length us, event | category | flops | bytes accessed | tf_op | source)
XLA Modules:
  0.0 118.3 jit_solution(5306267617162684067)
XLA Ops:
  0.6 1.7 %shard_map.129 = s32[8,1,128]{2,1,0:T(1,128)} custom-call(s32[2,1,4,4]{3,2,1,0:T(4,128)} %refs_2_.8, s32[2,1,4,4]{3,2,1,0:T(4,128)} %refs_3_.6, s32[1,2,2]{2,1,0:T(2,128)} %refs_9_.3), custom_call_target="tpu_custom_call" | custom-call | tf_op jit(solution)/shard_map/pallas_call | solution.py:700
  2.4 13.7 %all_to_all.25.refs_2_.refs_1_.refs_8_.refs_4_ = s32[8,1,128]{2,1,0:T(1,128)} all-to-all(s32[8,1,128]{2,1,0:T(1,128)} %shard_map.129), channel_id=1, replica_groups=mesh['row'=8,'rep'=4] {'row'}, dimensions={0} | all-to-all | bytes 8192 | tf_op jit(solution)/shard_map/all_to_all | solution.py:671
  16.0 3.1 %shard_map.130 = f32[8,40,128]{2,1,0:T(8,128)} custom-call(f32[59,4096]{1,0:T(8,128)} %refs_4_.1, f32[2,1,11]{2,1,0:T(1,128)} %refs_3_.7, s32[8,1,128]{2,1,0:T(1,128)} %all_to_all.25.refs_2_.refs_1_.refs_8_.refs_4_), custom_call_target="tpu_custom_call" | custom-call | tf_op jit(solution)/shard_map/pallas_call | solution.py:708
  19.1 11.6 %all_to_all.26.refs_0_ = f32[8,40,128]{2,1,0:T(8,128)} all-to-all(f32[8,40,128]{2,1,0:T(8,128)} %shard_map.130), channel_id=1, replica_groups=mesh['row'=8,'rep'=4] {'row'}, dimensions={0} | all-to-all | bytes 327680 | tf_op jit(solution)/shard_map/all_to_all | solution.py:671
  30.7 7.7 %shard_map.131 = (f32[2,1,3,4,256]{4,3,2,1,0:T(4,128)}, f32[8,40,128]{2,1,0:T(8,128)}) custom-call(f32[8,40,128]{2,1,0:T(8,128)} %all_to_all.26.refs_0_, f32[2,1,2,4]{3,2,1,0:T(2,128)} %bitcast.5, s32[2,1,4,4]{3,2,1,0:T(4,128)} %refs_2_.8, s32[2,1,4,512]{3,2,1,0:T(4,128)} %refs_5_.3, f32[2,1,3,4,256]{4,3,2,1,0:T(4,128)} %bitcast.3), custom_call_target="tpu_custom_call" | custom-call | tf_op jit(solution)/shard_map/pallas_call | solution.py:736
  38.4 11.6 %all_to_all.27.refs_0_ = f32[8,40,128]{2,1,0:T(8,128)} all-to-all(f32[8,40,128]{2,1,0:T(8,128)} %get-tuple-element.17), channel_id=1, replica_groups=mesh['row'=8,'rep'=4] {'row'}, dimensions={0} | all-to-all | bytes 327680 | tf_op jit(solution)/shard_map/all_to_all | solution.py:671
  49.9 1.8 %shard_map.132.refs_0_ = f32[304,128]{1,0:T(8,128)} custom-call(f32[8,40,128]{2,1,0:T(8,128)} %all_to_all.27.refs_0_, s32[8,1,128]{2,1,0:T(1,128)} %all_to_all.25.refs_2_.refs_1_.refs_8_.refs_4_, s32[1,2,2]{2,1,0:T(2,128)} %refs_9_.3, f32[2,1,11]{2,1,0:T(1,128)} %refs_3_.7), custom_call_target="tpu_custom_call" | custom-call | tf_op jit(solution)/shard_map/pallas_call | solution.py:728
  51.7 1.5 %collective-permute-start.1 = (f32[304,128]{1,0:T(8,128)}, f32[304,128]{1,0:T(8,128)S(1)}, u32[]{:S(2)}, u32[]{:S(2)}) collective-permute-start(f32[304,128]{1,0:T(8,128)} %shard_map.132.refs_0_), channel_id=1, source_target_pairs={{0,2},{1,3},{2,0},{3,1},{4,6},{5,7},{6,4},{7,5},{8,10},{9,11},{10,... | collective-permute-start | bytes 466952 | tf_op jit(solution)/shard_map/ppermute | solution.py:655
  53.2 0.0 collective-permute-start
  53.2 3.9 %collective-permute-done.1.refs_2_ = f32[304,128]{1,0:T(8,128)S(1)} collective-permute-done((f32[304,128]{1,0:T(8,128)}, f32[304,128]{1,0:T(8,128)S(1)}, u32[]{:S(2)}, u32[]{:S(2)}) %collective-permute-start.1) | collective-permute-done | bytes 155680 | tf_op jit(solution)/shard_map/ppermute | solution.py:655
  57.2 0.0 collective-permute-done.refs_1_
  57.2 1.4 %collective-permute-done.2.refs_3_ = f32[304,128]{1,0:T(8,128)S(1)} collective-permute-done((f32[304,128]{1,0:T(8,128)S(1)}, f32[304,128]{1,0:T(8,128)S(1)}, u32[]{:S(2)}, u32[]{:S(2)}) %collective-permute-start.2) | collective-permute-done | bytes 155680 | tf_op jit(solution)/shard_map/ppermute | solution.py:655
  58.6 0.7 copy-done.7
  59.2 6.9 %shard_map.133 = (f32[59,4096]{1,0:T(8,128)}, f32[59,4096]{1,0:T(8,128)}, f32[59,4096]{1,0:T(8,128)}, f32[8,40,128]{2,1,0:T(8,128)}, f32[3,59,256]{2,1,0:T(8,128)}, /*index=5*/f32[3,59,256]{2,1,0:T(8,128)}) custom-call(f32[304,128]{1,0:T(8,128)} %shard_map.132.refs_0_, f32[304,128]{1,0:T(8,128)} %copy-done.6, f32[304,128]{1,0:T(8,128)} %copy-done.5, ...), custom_call_target="tpu_custom_call" | custom-call | tf_op jit(solution)/shard_map/pallas_call | solution.py:746
  66.1 12.0 %all_to_all.28.refs_0_ = f32[8,40,128]{2,1,0:T(8,128)} all-to-all(f32[8,40,128]{2,1,0:T(8,128)} %get-tuple-element.18), channel_id=1, replica_groups=mesh['row'=8,'rep'=4] {'row'}, dimensions={0} | all-to-all | bytes 327680 | tf_op jit(solution)/shard_map/all_to_all | solution.py:671
  78.2 7.9 %shard_map.134 = (f32[2,1,3,4,256]{4,3,2,1,0:T(4,128)}, f32[8,72,128]{2,1,0:T(8,128)}) custom-call(f32[8,40,128]{2,1,0:T(8,128)} %all_to_all.28.refs_0_, f32[2,1,2,4]{3,2,1,0:T(2,128)} %bitcast.6, s32[2,1,4,4]{3,2,1,0:T(4,128)} %refs_2_.8, s32[2,1,4,4]{3,2,1,0:T(4,128)} %refs_3_.6, s32[8,1,128]{2,1,0:T(1,128)} %all_to_all.25.refs_2_.refs_1_.refs_8_.refs_4_, ...), custom_call_target="tpu_custom_call" | custom-call | tf_op jit(solution)/shard_map/pallas_call | solution.py:758
  86.0 13.6 %all_to_all.29.refs_0_ = f32[8,72,128]{2,1,0:T(8,128)} all-to-all(f32[8,72,128]{2,1,0:T(8,128)} %get-tuple-element.20), channel_id=1, replica_groups=mesh['row'=8,'rep'=4] {'row'}, dimensions={0} | all-to-all | bytes 589824 | tf_op jit(solution)/shard_map/all_to_all | solution.py:671
  99.6 2.0 %shard_map.135.refs_0_ = f32[304,128]{1,0:T(8,128)} custom-call(f32[8,72,128]{2,1,0:T(8,128)} %all_to_all.29.refs_0_, s32[8,1,128]{2,1,0:T(1,128)} %all_to_all.25.refs_2_.refs_1_.refs_8_.refs_4_, s32[1,2,2]{2,1,0:T(2,128)} %refs_9_.3, f32[2,1,11]{2,1,0:T(1,128)} %refs_3_.7), custom_call_target="tpu_custom_call" | custom-call | tf_op jit(solution)/shard_map/pallas_call | solution.py:728
  101.7 1.5 %collective-permute-start.4 = (f32[304,128]{1,0:T(8,128)}, f32[304,128]{1,0:T(8,128)S(1)}, u32[]{:S(2)}, u32[]{:S(2)}) collective-permute-start(f32[304,128]{1,0:T(8,128)} %shard_map.135.refs_0_), channel_id=1, source_target_pairs={{0,2},{1,3},{2,0},{3,1},{4,6},{5,7},{6,4},{7,5},{8,10},{9,11},{10,... | collective-permute-start | bytes 466952 | tf_op jit(solution)/shard_map/ppermute | solution.py:655
  103.2 0.7 collective-permute-start.6
  103.9 4.0 %collective-permute-start.7 = (f32[3,59,256]{2,1,0:T(8,128)S(1)}, f32[3,59,256]{2,1,0:T(8,128)S(1)}, u32[]{:S(2)}, u32[]{:S(2)}) collective-permute-start(f32[3,59,256]{2,1,0:T(8,128)S(1)} %copy-done.8), channel_id=1, source_target_pairs={{0,28},{4,0},{8,4},{12,8},{16,12},{20,16},{24,20},{28,24},{1,29},{... | collective-permute-start | bytes 543752 | tf_op jit(solution)/shard_map/ppermute | solution.py:660
  107.9 0.0 collective-permute-start.3
  107.9 0.0 collective-permute-done.4.refs_2_
  107.9 0.5 collective-permute-start.5
  108.4 3.2 %collective-permute-done.6.refs_7_ = f32[3,59,256]{2,1,0:T(8,128)S(1)} collective-permute-done((f32[3,59,256]{2,1,0:T(8,128)S(1)}, f32[3,59,256]{2,1,0:T(8,128)S(1)}, u32[]{:S(2)}, u32[]{:S(2)}) %collective-permute-start.6) | collective-permute-done | bytes 181280 | tf_op jit(solution)/shard_map/ppermute | solution.py:660
  111.6 0.0 collective-permute-done.7.refs_8_
  111.6 0.0 collective-permute-done.3.refs_1_
  111.7 0.6 copy-done
  112.3 0.1 copy-done.1
  112.4 0.1 copy-done.3
  112.5 0.0 copy-done.4
  112.5 5.8 %shard_map.136 = (f32[59,4096]{1,0:T(8,128)}, f32[59,4096]{1,0:T(8,128)}, f32[59,4096]{1,0:T(8,128)}) custom-call(f32[304,128]{1,0:T(8,128)} %shard_map.135.refs_0_, f32[304,128]{1,0:T(8,128)} %copy-done.3, f32[304,128]{1,0:T(8,128)} %copy-done.2, f32[304,128]{1,0:T(8,128)} %copy-done.4, f32[59,4096]{1,0:T(8,128)} %get-tuple-element.21.refs_4_, ...), custom_call_target="tpu_custom_call" | custom-call | tf_op jit(solution)/shard_map/pallas_call | solution.py:767
  (17 shorter events, 0.0 us)
Async XLA Ops:
  51.7 5.4 %collective-permute-start.1 = (f32[304,128]{1,0:T(8,128)}, f32[304,128]{1,0:T(8,128)S(1)}, u32[]{:S(2)}, u32[]{:S(2)}) collective-permute-start(f32[304,128]{1,0:T(8,128)} %shard_map.132.refs_0_), channel_id=1, source_target_pairs={{0,2},{1,3},{2,0},{3,1},{4,6},{5,7},{6,4},{7,5},{8,10},{9,11},{10,... | collective-permute-start | bytes 466952 | tf_op jit(solution)/shard_map/ppermute | solution.py:655
  53.2 4.0 %collective-permute-start = (f32[304,128]{1,0:T(8,128)}, f32[304,128]{1,0:T(8,128)S(1)}, u32[]{:S(2)}, u32[]{:S(2)}) collective-permute-start(f32[304,128]{1,0:T(8,128)} %shard_map.132.refs_0_), channel_id=1, source_target_pairs={{0,1},{1,0},{2,3},{3,2},{4,5},{5,4},{6,7},{7,6},{8,9},{9,8},{10,11... | collective-permute-start | bytes 466952 | tf_op jit(solution)/shard_map/ppermute | solution.py:655
  57.2 1.4 %copy-start.5 = (f32[304,128]{1,0:T(8,128)}, f32[304,128]{1,0:T(8,128)S(1)}, u32[]{:S(2)}) copy-start(f32[304,128]{1,0:T(8,128)S(1)} %collective-permute-done.1.refs_2_) | copy-start | bytes 466948
  57.2 1.4 %collective-permute-start.2 = (f32[304,128]{1,0:T(8,128)S(1)}, f32[304,128]{1,0:T(8,128)S(1)}, u32[]{:S(2)}, u32[]{:S(2)}) collective-permute-start(f32[304,128]{1,0:T(8,128)S(1)} %collective-permute-done.1.refs_2_), channel_id=1, source_target_pairs={{0,1},{1,0},{2,3},{3,2},{4,5},{5,4},{6,7},{7,6},{8,9},{9,8},{10,11... | collective-permute-start | bytes 466952 | tf_op jit(solution)/shard_map/ppermute | solution.py:655
  57.2 1.4 %copy-start.6 = (f32[304,128]{1,0:T(8,128)}, f32[304,128]{1,0:T(8,128)S(1)}, u32[]{:S(2)}) copy-start(f32[304,128]{1,0:T(8,128)S(1)} %collective-permute-done.refs_1_) | copy-start | bytes 466948
  58.6 0.7 copy-start.7
  99.6 3.5 %copy-start.9 = (f32[3,59,256]{2,1,0:T(8,128)S(1)}, f32[3,59,256]{2,1,0:T(8,128)}, u32[]{:S(2)}) copy-start(f32[3,59,256]{2,1,0:T(8,128)} %get-tuple-element.24) | copy-start | bytes 543748
  99.6 4.2 %copy-start.8 = (f32[3,59,256]{2,1,0:T(8,128)S(1)}, f32[3,59,256]{2,1,0:T(8,128)}, u32[]{:S(2)}) copy-start(f32[3,59,256]{2,1,0:T(8,128)} %get-tuple-element.25) | copy-start | bytes 543748
  101.7 6.2 %collective-permute-start.4 = (f32[304,128]{1,0:T(8,128)}, f32[304,128]{1,0:T(8,128)S(1)}, u32[]{:S(2)}, u32[]{:S(2)}) collective-permute-start(f32[304,128]{1,0:T(8,128)} %shard_map.135.refs_0_), channel_id=1, source_target_pairs={{0,2},{1,3},{2,0},{3,1},{4,6},{5,7},{6,4},{7,5},{8,10},{9,11},{10,... | collective-permute-start | bytes 466952 | tf_op jit(solution)/shard_map/ppermute | solution.py:655
  103.2 8.5 %collective-permute-start.6 = (f32[3,59,256]{2,1,0:T(8,128)S(1)}, f32[3,59,256]{2,1,0:T(8,128)S(1)}, u32[]{:S(2)}, u32[]{:S(2)}) collective-permute-start(f32[3,59,256]{2,1,0:T(8,128)S(1)} %copy-done.9), channel_id=1, source_target_pairs={{0,4},{4,8},{8,12},{12,16},{16,20},{20,24},{24,28},{28,0},{1,5},{5... | collective-permute-start | bytes 543752 | tf_op jit(solution)/shard_map/ppermute | solution.py:660
  103.9 7.8 %collective-permute-start.7 = (f32[3,59,256]{2,1,0:T(8,128)S(1)}, f32[3,59,256]{2,1,0:T(8,128)S(1)}, u32[]{:S(2)}, u32[]{:S(2)}) collective-permute-start(f32[3,59,256]{2,1,0:T(8,128)S(1)} %copy-done.8), channel_id=1, source_target_pairs={{0,28},{4,0},{8,4},{12,8},{16,12},{20,16},{24,20},{28,24},{1,29},{... | collective-permute-start | bytes 543752 | tf_op jit(solution)/shard_map/ppermute | solution.py:660
  107.9 3.8 %collective-permute-start.3 = (f32[304,128]{1,0:T(8,128)}, f32[304,128]{1,0:T(8,128)S(1)}, u32[]{:S(2)}, u32[]{:S(2)}) collective-permute-start(f32[304,128]{1,0:T(8,128)} %shard_map.135.refs_0_), channel_id=1, source_target_pairs={{0,1},{1,0},{2,3},{3,2},{4,5},{5,4},{6,7},{7,6},{8,9},{9,8},{10,11... | collective-permute-start | bytes 466952 | tf_op jit(solution)/shard_map/ppermute | solution.py:655
  107.9 3.8 %copy-start.2 = (f32[304,128]{1,0:T(8,128)}, f32[304,128]{1,0:T(8,128)S(1)}, u32[]{:S(2)}) copy-start(f32[304,128]{1,0:T(8,128)S(1)} %collective-permute-done.4.refs_2_) | copy-start | bytes 466948
  107.9 3.8 %collective-permute-start.5 = (f32[304,128]{1,0:T(8,128)S(1)}, f32[304,128]{1,0:T(8,128)S(1)}, u32[]{:S(2)}, u32[]{:S(2)}) collective-permute-start(f32[304,128]{1,0:T(8,128)S(1)} %collective-permute-done.4.refs_2_), channel_id=1, source_target_pairs={{0,1},{1,0},{2,3},{3,2},{4,5},{5,4},{6,7},{7,6},{8,9},{9,8},{10,11... | collective-permute-start | bytes 466952 | tf_op jit(solution)/shard_map/ppermute | solution.py:655
  111.6 0.7 copy-start
  111.6 0.8 copy-start.1
  111.6 0.8 copy-start.3
  111.7 0.8 copy-start.4

commit v3 on v2

--- a/solution.py
+++ b/solution.py
@@ -1,11 +1,10 @@
-import math
-
 import jax
 import jax.numpy as jnp
 from jax import lax
 from jax.experimental import pallas as pl
 from jax.experimental.pallas import tpu as pltpu
 from jax.sharding import PartitionSpec as P
+
 
 P_SIZE = 59
 BLOCK = 128
@@ -46,6 +45,10 @@
 SM = pl.BlockSpec(memory_space=pltpu.SMEM)
 
 
+def pitch(blocks):
+    return blocks + 1 - blocks % 2
+
+
 def up8(count):
     return -(-count // 8) * 8
 
@@ -155,13 +158,14 @@
     return cov_yy * inverse, -cov_xy * inverse, cov_xx * inverse
 
 
-def serve(step, capacity, blocks, camera_ref, asked_ref, dense, table, faint, out_ref):
+def serve(step, capacity, blocks, camera_ref, asked_ref, dense, table, out_ref):
+    wide = pitch(blocks)
     cam = [camera_ref[step, 0, k] for k in range(11)]
     basis = harmonics(cam[8], cam[9], cam[10])
     for group in range(blocks // 8):
 
         def row(p):
-            return dense[p * blocks + 8 * group : p * blocks + 8 * group + 8, :]
+            return dense[p * wide + 8 * group : p * wide + 8 * group + 8, :]
 
         scales, _, _, rotation = geometry(row)
         conic = conic_of(scales, rotation, cam)
@@ -178,18 +182,16 @@
             for j in range(1, 16):
                 colour = colour + basis[j] * row(11 + 3 * j + k)
             rows.append(0.5 + colour)
-        for k in range(8):
-            table[pl.ds(64 * group + k, 8, stride=8), :] = rows[k]
-        faint[8 * group : 8 * group + 8, :] = -LOG2E * jnp.log(1.0 + jnp.exp(-row(10)))
+        rows.append(-LOG2E * jnp.log(1.0 + jnp.exp(-row(10))))
+        for k in range(9):
+            table[pl.ds(72 * group + k, 8, stride=9), :] = rows[k]
     owners = out_ref.shape[0]
     for peer in range(owners):
         for slot in range(capacity):
             block = jnp.maximum(asked_ref[peer, 0, step * capacity + slot], 0)
-            out_ref[peer, 8 * slot : 8 * slot + 8, :] = table[
-                pl.ds(pl.multiple_of(block * 8, 8), 8), :
-            ]
-            out_ref[peer, 8 * capacity + slot : 8 * capacity + slot + 1, :] = faint[
-                pl.ds(block, 1), :
+            out_ref[peer, 8 * slot : 8 * slot + 8, :] = table[pl.ds(block * 9, 8), :]
+            out_ref[peer, 8 * capacity + slot : 8 * capacity + slot + 1, :] = table[
+                pl.ds(block * 9 + 8, 1), :
             ]
 
 
@@ -197,14 +199,14 @@
     return [(first, min(8, P_SIZE - first)) for first in range(0, P_SIZE, 8)]
 
 
-def start_kernel(capacity, params_ref, camera_ref, asked_ref, out_ref, dense, table, faint):
+def start_kernel(capacity, params_ref, camera_ref, asked_ref, out_ref, dense, table):
     blocks = params_ref.shape[1] // BLOCK
     for block in range(blocks):
         for first, count in row_groups():
-            dense[pl.ds(first * blocks + block, count, stride=blocks), :] = params_ref[
+            dense[pl.ds(first * pitch(blocks) + block, count, stride=pitch(blocks)), :] = params_ref[
                 first : first + count, block * BLOCK : (block + 1) * BLOCK
             ]
-    serve(0, capacity, blocks, camera_ref, asked_ref, dense, table, faint, out_ref)
+    serve(0, capacity, blocks, camera_ref, asked_ref, dense, table, out_ref)
 
 
 def pixel_features(rows, per):
@@ -225,21 +227,32 @@
     return got
 
 
+HEAT_PIECES = 2
+
+
+def put(ref, rows, value):
+    for k in range(ref.shape[0]):
+        ref[k, rows, :] = value[:, k * BLOCK : (k + 1) * BLOCK]
+
+
+def get(ref, first, count):
+    return jnp.concatenate([ref[k, first : first + count, :] for k in range(ref.shape[0])], axis=1)
+
+
+COL_ROWS = {0: (0, 9, 15), 1: (3, 12), 2: (6,)}
+
+
 def render_kernel(step, capacity, slots, final, *refs):
     if final:
         (
             arrived, corner_ref, owner_ref, block_ref, asked_ref, order_ref, target_ref, earlier_ref,
-            picture_ref, out_ref, onehot, coeffs, alphas, locals_, weights, weight_h, weight_m,
-            flows, behind, heat_h, heat_m,
+            picture_ref, out_ref, *scratch,
         ) = refs
         for other in range(ITERS - 1):
             picture_ref[other] = earlier_ref[other]
     else:
-        (
-            arrived, corner_ref, owner_ref, order_ref, target_ref,
-            picture_ref, out_ref, onehot, coeffs, alphas, locals_, weights, weight_h, weight_m,
-            flows, behind, heat_h, heat_m,
-        ) = refs
+        arrived, corner_ref, owner_ref, order_ref, target_ref, picture_ref, out_ref, *scratch = refs
+    onehots, sorted_ref, coeffs, shades_ref, sums_ref, grads_ref, *per_tile = scratch
     owners = arrived.shape[0]
     tiles = owner_ref.shape[2]
     lists = DEPTH // BLOCK
@@ -254,7 +267,7 @@
     ranks = [rank_of(names, index) for index in range(tiles * LISTB)]
 
     order = order_ref[step, 0]
-    order = jnp.concatenate([order, order], axis=0) if tiles == 4 else order
+    order = jnp.concatenate([order] * (8 // tiles), axis=0)
     order_pieces = [order[:, k * BLOCK : (k + 1) * BLOCK] for k in range(lists)]
     woven = []
     for k in range(lists):
@@ -272,9 +285,8 @@
             for t in range(tiles)
         ]
         faint_pieces.append(jnp.concatenate(parts * (8 // tiles), axis=0))
-    all_faint = [
-        lane_gather(faint_pieces, all_within[k], all_source[k]) for k in range(lists)
-    ]
+    faint = [lane_gather(faint_pieces, all_within[k], all_source[k]) for k in range(lists)]
+    faint = jnp.concatenate(faint, axis=1)[0:tiles]
     row_id = lax.broadcasted_iota(jnp.int32, (BLOCK, BLOCK), 0).astype(f32).astype(bf16)
     sub = lax.broadcasted_iota(jnp.int32, (segments, PIX), 0)
 
@@ -288,61 +300,66 @@
             ]
             for j in range(LISTB)
         ]
-        sorted_rows = []
         for k in range(lists):
             within = jnp.broadcast_to(all_within[k][one], (8, BLOCK))
             source = jnp.broadcast_to(all_source[k][one], (8, BLOCK))
-            sorted_rows.append(lane_gather(pieces, within, source))
-            local = woven[k][one].astype(f32)
-            for piece in range(lists):
-                inside = jnp.where(all_source[k][one] == piece, local - piece * BLOCK, -1.0)
-                onehot[
-                    piece * BLOCK : (piece + 1) * BLOCK, k * BLOCK : (k + 1) * BLOCK
-                ] = jnp.where(row_id == inside.astype(bf16), jnp.ones((), bf16), jnp.zeros((), bf16))
-        rows = jnp.concatenate(sorted_rows, axis=1)
-        faint = jnp.concatenate([part[one] for part in all_faint], axis=1)
-        u = rows[0:1] - (corner_ref[step, 0, 0, tile] + SIDE / 2)
-        v = rows[1:2] - (corner_ref[step, 0, 1, tile] + SIDE / 2)
-        a, b, c = rows[2:3], rows[3:4], rows[4:5]
-        colours = rows[5:8]
-        half_a, half_b, half_c = (-0.5 * LOG2E) * a, -LOG2E * b, (-0.5 * LOG2E) * c
-        values = (
-            half_a * u * u + half_b * u * v + half_c * v * v + faint,
-            -(2.0 * half_a * u + half_b * v),
-            -(2.0 * half_c * v + half_b * u),
-            half_a,
-            half_b,
-            half_c,
-        )
-        for index, value in enumerate(values):
-            for piece, part in enumerate(split(value, 3)):
-                coeffs[3 * index + piece : 3 * index + piece + 1, :] = part.astype(f32)
-        form = coeffs[...].astype(bf16)
-        col_h, col_m, col_l = [part.astype(f32) for part in split(colours, 3)]
-        col_left = jnp.concatenate([col_h, col_m, col_l], axis=0).astype(bf16)
-        col_right = jnp.concatenate(
-            [col_h, col_m, col_h, col_m, col_l, col_h], axis=0
-        ).astype(bf16)
-
+            sorted_ref[k, pl.ds(tile, 8, stride=9), :] = lane_gather(
+                pieces, within, source
+            )
+
+    def param(k):
+        return get(sorted_ref, 9 * k, tiles)
+
+    which = lax.broadcasted_iota(jnp.int32, (tiles, DEPTH), 0)
+    corner_x = jnp.zeros((tiles, DEPTH), f32)
+    corner_y = jnp.zeros((tiles, DEPTH), f32)
+    for tile in range(tiles):
+        corner_x = jnp.where(which == tile, corner_ref[step, 0, 0, tile], corner_x)
+        corner_y = jnp.where(which == tile, corner_ref[step, 0, 1, tile], corner_y)
+    all_u = u = param(0) - (corner_x + SIDE / 2)
+    all_v = v = param(1) - (corner_y + SIDE / 2)
+    half_a, half_b, half_c = (
+        (-0.5 * LOG2E) * param(2), -LOG2E * param(3), (-0.5 * LOG2E) * param(4)
+    )
+    values = (
+        half_a * u * u + half_b * u * v + half_c * v * v + faint,
+        -(2.0 * half_a * u + half_b * v),
+        -(2.0 * half_c * v + half_b * u),
+        half_a,
+        half_b,
+        half_c,
+    )
+    for index, value in enumerate(values):
+        for piece, part in enumerate(split(value, 3)):
+            put(coeffs, pl.ds(3 * index + piece, tiles, stride=33), part.astype(f32))
+    for k in range(3):
+        for piece, part in enumerate(split(param(5 + k), 3)):
+            for at in COL_ROWS[piece]:
+                put(shades_ref, pl.ds(at + k, tiles, stride=19), part.astype(f32))
+
+    def opening(tile, ratios, locals_, weight_h, weight_m, mixed, heats):
+        form = get(coeffs, 33 * tile, 32).astype(bf16)
         passed = jnp.ones((segments, PIX), f32)
         for k in range(lists):
             power = dot(form[:, k * BLOCK : (k + 1) * BLOCK], features, TN)
             for at in range(0, BLOCK, segments):
                 here = slice(k * BLOCK + at, k * BLOCK + at + segments)
                 alpha = jnp.exp2(power[at : at + segments])
-                alphas[here, :] = alpha
-                locals_[here, :] = passed
-                passed = passed * (1.0 - alpha)
+                keep = 1.0 - alpha
+                ratios[here, :] = alpha / keep
+                locals_[here, :] = alpha * passed
+                passed = passed * keep
         for shift in (1, 2, 4):
             passed = passed * jnp.where(sub >= shift, pltpu.roll(passed, shift, 0), 1.0)
-        passed = jnp.where(sub >= 1, pltpu.roll(passed, 1, 0), 1.0)
-        passed = jnp.concatenate([passed, passed], axis=0)
+        return jnp.where(sub >= 1, pltpu.roll(passed, 1, 0), 1.0)
+
+    def picture(tile, passed, ratios, locals_, weight_h, weight_m, mixed, heats):
+        one = slice(tile, tile + 1)
+        twice = jnp.concatenate([passed, passed], axis=0)
         for at in range(0, DEPTH, 2 * segments):
             here = slice(at, at + 2 * segments)
-            weight = alphas[here, :] * (locals_[here, :] * passed)
-            weights[here, :] = weight
-            weight_h[here, :], weight_m[here, :] = split(weight, 2)
-
+            weight_h[here, :], weight_m[here, :] = split(locals_[here, :] * twice, 2)
+        col_left = get(shades_ref, 19 * tile, 9).astype(bf16)
         shades = dot(col_left, weight_h[...]) + dot(col_left, weight_m[...])
         shades = shades[0:3] + shades[3:6] + shades[6:9]
         for k in range(3):
@@ -351,37 +368,63 @@
             [target_ref[step, 0, k, one, :] for k in range(3)], axis=0
         )
         err_h, err_m, err_l = [part.astype(f32) for part in split(error, 3)]
-        err_left = jnp.concatenate([err_h, err_m, err_l], axis=0).astype(bf16)
-        err_right = jnp.concatenate(
-            [err_h, err_h, err_m, err_m, err_h, err_l], axis=0
+        return jnp.concatenate([err_h, err_h, err_h, err_m, err_m, err_l], axis=0).astype(bf16)
+
+    def closing(tile, passed, errors, ratios, locals_, weight_h, weight_m, mixed, heats):
+        err_left = jnp.concatenate(
+            [errors.astype(f32)[0:3], errors.astype(f32)[9:12], errors.astype(f32)[15:18]], axis=0
         ).astype(bf16)
         col_grads = dot(err_left, weight_h[...], NT) + dot(err_left, weight_m[...], NT)
-
+        put(sums_ref, pl.ds(72 + tile, 8, stride=9), col_grads[0:8])
+        put(sums_ref, slice(144 + tile, 145 + tile), col_grads[8:9])
+        col_right = get(shades_ref, 19 * tile, 18).astype(bf16)
         total = jnp.zeros((segments, PIX), f32)
         for k in reversed(range(lists)):
-            seen = dot(col_right[:, k * BLOCK : (k + 1) * BLOCK], err_right, TN)
+            seen = dot(col_right[:, k * BLOCK : (k + 1) * BLOCK], errors, TN)
             for at in reversed(range(0, BLOCK, segments)):
                 here = slice(k * BLOCK + at, k * BLOCK + at + segments)
-                flow = weights[here, :] * seen[at : at + segments]
-                flows[here, :] = flow
-                behind[here, :] = total
+                flow = locals_[here, :] * passed * seen[at : at + segments]
+                mixed[here, :] = flow - ratios[here, :] * total
                 total = total + flow
         for shift in (1, 2, 4):
             total = total + jnp.where(
                 sub < segments - shift, pltpu.roll(total, segments - shift, 0), 0.0
             )
         total = jnp.where(sub < segments - 1, pltpu.roll(total, segments - 1, 0), 0.0)
-        total = jnp.concatenate([total, total], axis=0)
+        twice = jnp.concatenate([total, total], axis=0)
         for at in range(0, DEPTH, 2 * segments):
             here = slice(at, at + 2 * segments)
-            alpha = alphas[here, :]
-            heat = flows[here, :] - (alpha / (1.0 - alpha)) * (behind[here, :] + total)
-            heat_h[here, :], heat_m[here, :] = split(heat, 2)
-        moments = dot(flat, heat_h[...], NT) + dot(flat, heat_m[...], NT)
-
-        col_grads = col_grads[0:3] + col_grads[3:6] + col_grads[6:9]
-        m00, m10, m01 = moments[0:1], moments[1:2], moments[2:3]
-        m20, m11, m02 = moments[3:4], moments[4:5], moments[5:6]
+            parts = split(mixed[here, :] - ratios[here, :] * twice, HEAT_PIECES)
+            for ref, part in zip(heats, parts):
+                ref[here, :] = part
+        moments = dot(flat, heats[0][...], NT)
+        for ref in heats[1:]:
+            moments = moments + dot(flat, ref[...], NT)
+        put(sums_ref, pl.ds(tile, 8, stride=9), moments[0:8])
+
+    def unsort_matrix(tile):
+        one = slice(tile, tile + 1)
+        for k in range(lists):
+            local = woven[k][one].astype(f32)
+            for piece in range(lists):
+                inside = jnp.where(all_source[k][one] == piece, local - piece * BLOCK, -1.0)
+                onehots[
+                    tile, piece * BLOCK : (piece + 1) * BLOCK, k * BLOCK : (k + 1) * BLOCK
+                ] = jnp.where(row_id == inside.astype(bf16), jnp.ones((), bf16), jnp.zeros((), bf16))
+
+    def buffers(tile):
+        each = len(per_tile) // tiles
+        mine = per_tile[each * tile : each * tile + each]
+        return (*mine[0:5], mine[5:])
+
+    def finish(first, count):
+        def summed(row):
+            return get(sums_ref, 9 * row + first, count)
+
+        group = slice(first, first + count)
+        a, b, c = [get(sorted_ref, 9 * k + first, count) for k in (2, 3, 4)]
+        u, v = all_u[group], all_v[group]
+        m00, m10, m01, m20, m11, m02 = [summed(k) for k in range(6)]
         x1, y1 = m10 - u * m00, m01 - v * m00
         grads = [
             a * x1 + b * y1,
@@ -389,12 +432,17 @@
             -0.5 * (m20 - 2.0 * u * m10 + u * u * m00),
             -(m11 - u * m01 - v * m10 + u * v * m00),
             -0.5 * (m02 - 2.0 * v * m01 + v * v * m00),
-            col_grads,
+            *[summed(8 + k) + summed(11 + k) + summed(14 + k) for k in range(3)],
             m00,
-            jnp.zeros((7, DEPTH), f32),
         ]
-        grads = jnp.concatenate(grads, axis=0)
-        listed = dot(jnp.concatenate(split(grads, 3), axis=0), onehot[...], NT)
+        for k, value in enumerate(grads):
+            for piece, part in enumerate(split(value, 3)):
+                put(grads_ref, pl.ds(49 * first + 16 * piece + k, count, stride=49), part.astype(f32))
+        for tile in range(first, first + count):
+            unsort(tile)
+
+    def unsort(tile):
+        listed = dot(get(grads_ref, 49 * tile, 48).astype(bf16), onehots[tile], NT)
         listed = listed[0:16] + listed[16:32] + listed[32:48]
         for j in range(LISTB):
             name, rank = names[tile * LISTB + j], ranks[tile * LISTB + j]
@@ -420,6 +468,19 @@
                 out_ref[name, extra, :] = listed[8:9, lanes]
 
 
+    passes, errors = {}, {}
+    for tile in range(tiles):
+        passes[tile] = opening(tile, *buffers(tile))
+    for tile in range(tiles):
+        errors[tile] = picture(tile, passes[tile], *buffers(tile))
+    for tile in range(tiles):
+        unsort_matrix(tile)
+    for tile in range(tiles):
+        closing(tile, passes[tile], errors[tile], *buffers(tile))
+        if tile % 2 == 1 or tile == tiles - 1:
+            finish(tile - tile % 2, 1 + tile % 2)
+
+
 def gather_kernel(step, capacity, slots, returned, asked_ref, migration_ref, camera_ref, out_ref):
     owners = returned.shape[0]
     blocks = (out_ref.shape[0] - CAM_ROWS) // 9
@@ -431,8 +492,8 @@
                 block = jnp.maximum(asked_ref[peer, 0, step * capacity + slot], 0)
             else:
                 block = migration_ref[0, (slot - capacity) // MIGH, (slot - capacity) % MIGH]
-            main = pl.ds(pl.multiple_of(block * 8, 8), 8)
-            extra = pl.ds(8 * blocks + block, 1)
+            main = pl.ds(block * 9, 8)
+            extra = pl.ds(block * 9 + 8, 1)
             out_ref[main, :] = out_ref[main, :] + returned[peer, 8 * slot : 8 * slot + 8, :]
             out_ref[extra, :] = (
                 out_ref[extra, :] + returned[peer, 8 * slots + slot : 8 * slots + slot + 1, :]
@@ -454,6 +515,7 @@
 
 def pullback(blocks, cams, dense, grads):
     count = cams.shape[0]
+    wide = pitch(blocks)
     affine, basis = [], []
     for c in range(count):
         rows = [
@@ -465,13 +527,13 @@
     for group in range(blocks // 8):
 
         def row(p):
-            return dense[p * blocks + 8 * group : p * blocks + 8 * group + 8, :]
+            return dense[p * wide + 8 * group : p * wide + 8 * group + 8, :]
 
         def put(p, value):
-            grads[p * blocks + 8 * group : p * blocks + 8 * group + 8, :] = value
+            grads[p * wide + 8 * group : p * wide + 8 * group + 8, :] = value
 
         given = [
-            [cams[c, pl.ds(64 * group + k, 8, stride=8), :] for k in range(8)] for c in range(count)
+            [cams[c, pl.ds(72 * group + k, 8, stride=9), :] for k in range(9)] for c in range(count)
         ]
         scales, (w, x, y, z), norm, rotation = geometry(row)
         means = [0.0, 0.0, 0.0]
@@ -537,9 +599,9 @@
         along = w * g_w + x * g_x + y * g_y + z * g_z
         for k, (part, pull) in enumerate(((w, g_w), (x, g_x), (y, g_y), (z, g_z))):
             put(6 + k, norm * (pull - part * along))
-        faint = cams[0, 8 * blocks + 8 * group : 8 * blocks + 8 * group + 8, :]
+        faint = given[0][8]
         for c in range(1, count):
-            faint = faint + cams[c, 8 * blocks + 8 * group : 8 * blocks + 8 * group + 8, :]
+            faint = faint + given[c][8]
         put(10, faint / (1.0 + jnp.exp(row(10))))
         for j in range(16):
             for k in range(3):
@@ -560,13 +622,14 @@
     (
         own_ref, near_ref, far_ref, cross_ref, params_ref, first_ref, second_ref, camera_ref,
         asked_ref, migration_ref, new_params, new_first, new_second, out_ref, left_ref, right_ref,
-        cams, dense, grads, table, faint,
+        cams, dense, grads, table,
     ) = refs
     blocks = params_ref.shape[1] // BLOCK
+    wide = pitch(blocks)
     collect(own_ref, ((1, near_ref), (2, far_ref), (3, cross_ref)), cams)
     for block in range(blocks):
         for top, count in row_groups()[:2]:
-            dense[pl.ds(top * blocks + block, count, stride=blocks), :] = params_ref[
+            dense[pl.ds(top * wide + block, count, stride=wide), :] = params_ref[
                 top : top + count, block * BLOCK : (block + 1) * BLOCK
             ]
     pullback(blocks, cams, dense, grads)
@@ -574,7 +637,7 @@
         lanes = slice(block * BLOCK, (block + 1) * BLOCK)
         for top, count in row_groups():
             part = slice(top, top + count)
-            where = pl.ds(top * blocks + block, count, stride=blocks)
+            where = pl.ds(top * wide + block, count, stride=wide)
             value, first, second = adam(
                 params_ref[part, lanes], first_ref[part, lanes], second_ref[part, lanes],
                 grads[where, :],
@@ -583,7 +646,7 @@
             new_first[part, lanes] = first
             new_second[part, lanes] = second
             dense[where, :] = value
-    serve(1, capacity, blocks, camera_ref, asked_ref, dense, table, faint, out_ref)
+    serve(1, capacity, blocks, camera_ref, asked_ref, dense, table, out_ref)
     for side, ref in ((0, left_ref), (1, right_ref)):
         for j in range(MIGH):
             lanes = pl.ds(pl.multiple_of(migration_ref[0, side, j] * BLOCK, BLOCK), BLOCK)
@@ -597,10 +660,11 @@
         above_ref, migration_ref, new_params, new_first, new_second, cams, dense, grads,
     ) = refs
     blocks = params_ref.shape[1] // BLOCK
+    wide = pitch(blocks)
     collect(own_ref, ((1, near_ref), (2, far_ref), (3, cross_ref)), cams)
     for block in range(blocks):
         for top, count in row_groups()[:2]:
-            dense[pl.ds(top * blocks + block, count, stride=blocks), :] = params_ref[
+            dense[pl.ds(top * wide + block, count, stride=wide), :] = params_ref[
                 top : top + count, block * BLOCK : (block + 1) * BLOCK
             ]
     moved = [
@@ -610,7 +674,7 @@
     ]
     for block, ref, j in moved:
         for top, count in row_groups()[:2]:
-            dense[pl.ds(top * blocks + block, count, stride=blocks), :] = ref[
+            dense[pl.ds(top * wide + block, count, stride=wide), :] = ref[
                 0, top : top + count, j * BLOCK : (j + 1) * BLOCK
             ]
     pullback(blocks, cams, dense, grads)
@@ -620,7 +684,7 @@
             part = slice(top, top + count)
             value, first, second = adam(
                 params_ref[part, lanes], first_ref[part, lanes], second_ref[part, lanes],
-                grads[pl.ds(top * blocks + block, count, stride=blocks), :],
+                grads[pl.ds(top * wide + block, count, stride=wide), :],
             )
             new_params[part, lanes] = value
             new_first[part, lanes] = first
@@ -632,7 +696,7 @@
             part = slice(top, top + count)
             value, first, second = adam(
                 ref[0, part, source], ref[1, part, source], ref[2, part, source],
-                grads[pl.ds(top * blocks + block, count, stride=blocks), :],
+                grads[pl.ds(top * wide + block, count, stride=wide), :],
             )
             new_params[part, lanes] = value
             new_first[part, lanes] = first
@@ -690,9 +754,8 @@
     requests = tiles * LISTB
     capacity = max(2, 2 * ((requests + owners - 1) // owners))
     slots = capacity + 2 * MIGH
-    dense = pltpu.VMEM((64 * blocks, BLOCK), f32)
-    table = pltpu.VMEM((8 * blocks, BLOCK), f32)
-    faint = pltpu.VMEM((blocks, BLOCK), f32)
+    dense = pltpu.VMEM((64 * pitch(blocks), BLOCK), f32)
+    table = pltpu.VMEM((9 * blocks, BLOCK), f32)
     payload = 9 * blocks + CAM_ROWS
     cams = pltpu.VMEM((replicas, payload, BLOCK), f32)
     state = [shape(params.shape)] * 3
@@ -710,16 +773,19 @@
         out_shape=shape((owners, up8(9 * capacity), BLOCK)),
         in_specs=[VM, SM, SM],
         out_specs=VM,
-        scratch_shapes=[dense, table, faint],
+        scratch_shapes=[dense, table],
     )(params, camera, asked)
 
     deep = pltpu.VMEM((DEPTH, PIX), f32)
     packed = pltpu.VMEM((DEPTH, PIX), bf16)
     render_scratch = [
-        pltpu.VMEM((DEPTH, DEPTH), bf16),
-        pltpu.VMEM((32, DEPTH), f32),
-        deep, deep, deep, packed, packed, deep, deep, packed, packed,
-    ]
+        pltpu.VMEM((tiles, DEPTH, DEPTH), bf16),
+        pltpu.VMEM((DEPTH // BLOCK, 80, BLOCK), f32),
+        pltpu.VMEM((DEPTH // BLOCK, 33 * tiles, BLOCK), f32),
+        pltpu.VMEM((DEPTH // BLOCK, 19 * tiles, BLOCK), f32),
+        pltpu.VMEM((DEPTH // BLOCK, 160, BLOCK), f32),
+        pltpu.VMEM((DEPTH // BLOCK, 49 * tiles, BLOCK), f32),
+    ] + [deep, deep, packed, packed, deep, *[packed] * HEAT_PIECES] * tiles
     corners = jnp.swapaxes(tile_corner, 2, 3)
     photos = jnp.swapaxes(targets, 2, 3)
     pictures_shape = shape(photos.shape)
@@ -731,6 +797,15 @@
             in_specs=[VM, SM, SM, SM],
             out_specs=VM,
         )(returned, asked, migration, camera)
+
+    def second(arrived, pictures):
+        return pl.pallas_call(
+            bind(render_kernel, 1, capacity, slots, True),
+            out_shape=[pictures_shape, shape((owners, up8(9 * slots), BLOCK))],
+            in_specs=[VM, SM, SM, SM, SM, VM, VM, VM],
+            out_specs=[VM, VM],
+            scratch_shapes=render_scratch,
+        )(arrived, corners, tile_owner, tile_block, asked, depth_order, photos, pictures)
 
     arrived = row_exchange(outgoing)
     pictures, back = pl.pallas_call(
@@ -748,20 +823,14 @@
         out_shape=state + [shape((owners, up8(9 * capacity), BLOCK)), leaving, leaving],
         in_specs=[VM] * 7 + [SM] * 3,
         out_specs=[VM] * 6,
-        scratch_shapes=[cams, dense, dense, table, faint],
+        scratch_shapes=[cams, dense, dense, table],
     )(
         own, near, far, cross, params, first_moment, second_moment, camera, asked, migration
     )
     arrived = row_exchange(outgoing)
     below = turn(right, "row", 1)
     above = turn(left, "row", -1)
-    pictures, back = pl.pallas_call(
-        bind(render_kernel, 1, capacity, slots, True),
-        out_shape=[pictures_shape, shape((owners, up8(9 * slots), BLOCK))],
-        in_specs=[VM, SM, SM, SM, SM, VM, VM, VM],
-        out_specs=[VM, VM],
-        scratch_shapes=render_scratch,
-    )(arrived, corners, tile_owner, tile_block, asked, depth_order, photos, pictures)
+    pictures, back = second(arrived, pictures)
     own = gather(1, slots, row_exchange(back))
     near, far, cross = exchange(own)
     current, moment_one, moment_two = pl.pallas_call(

time: 119 us -> 113 us (0.950)
  Pallas kernels: 36.9 us -> 30.7 us
    pallas_call x1, Pallas kernels: 6.87 us -> 5.19 us  [local(): pl.pallas_call(bind(update_kernel, capacity), out_shape=state + [shape((o...]
    pallas_call x1, Pallas kernels: 7.86 us -> 6.58 us  [second(): pl.pallas_call(bind(render_kernel, 1, capacity, slots, True), out_shape=[...]
    pallas_call x1, Pallas kernels: 7.68 us -> 6.42 us  [local(): pl.pallas_call(bind(render_kernel, 0, capacity, capacity, False), out_sha...]
where the time goes in v3:
time: 113 us; the launch traced here: 112 us
  blocking collectives  62.5 us (55%)
  Pallas kernels  30.7 us (27%)
  waiting for transfers between devices  8.55 us (8%)
  starting transfers between devices  8.22 us (7%)
  local copies, waits for them, and re-layouts  1.51 us (1%)
    all_to_all x5, blocking collectives, row_exchange(): return lax.all_to_all(value, 'row', split_axis=0, concat_axis=0, tiled=True)  62.5 us
    pallas_call x1, Pallas kernels, second(): pl.pallas_call(bind(render_kernel, 1, capacity, slots, True), out_shape=[...  6.58 us
    pallas_call x1, Pallas kernels, local(): pl.pallas_call(bind(render_kernel, 0, capacity, capacity, False), out_sha...  6.42 us
    ppermute x6, waiting for transfers between devices, swap(): return lax.ppermute(value, axis, [(i, i ^ offset) for i in range(count)])  5.32 us
    pallas_call x1, Pallas kernels, local(): pl.pallas_call(bind(update_kernel, capacity), out_shape=state + [shape((o...  5.19 us
    pallas_call x1, Pallas kernels, local(): pl.pallas_call(final_kernel, out_shape=state, in_specs=[VM] * 9 + [SM], o...  4.97 us
    ppermute x2, starting transfers between devices, turn(): lax.ppermute(value, axis, [(i, (i + offset) % count) for i in range(count)])  4.72 us
    pallas_call x2, Pallas kernels, gather(): pl.pallas_call(bind(gather_kernel, step, capacity, count), out_shape=shap...  3.68 us
  transfers between devices with their start and end apart: 8, of which 3 were waited for; matrix products, arithmetic and copies ran while one was open for 0% of the time, Pallas kernels for 0%

profile of v3, /device:TPU:0, one launch (start us, length us, event | category | flops | bytes accessed | tf_op | source)
XLA Modules:
  0.0 112.2 jit_solution(11570976979469498193)
XLA Ops:
  0.6 1.7 %shard_map.129 = s32[8,1,128]{2,1,0:T(1,128)} custom-call(s32[2,1,4,4]{3,2,1,0:T(4,128)} %refs_2_.8, s32[2,1,4,4]{3,2,1,0:T(4,128)} %refs_3_.6, s32[1,2,2]{2,1,0:T(2,128)} %refs_9_.3), custom_call_target="tpu_custom_call" | custom-call | tf_op jit(solution)/shard_map/pallas_call | solution.py:763
  2.4 13.7 %all_to_all.25.refs_2_.refs_1_.refs_8_.refs_4_ = s32[8,1,128]{2,1,0:T(1,128)} all-to-all(s32[8,1,128]{2,1,0:T(1,128)} %shard_map.129), channel_id=1, replica_groups=mesh['row'=8,'rep'=4] {'row'}, dimensions={0} | all-to-all | bytes 8192 | tf_op jit(solution)/shard_map/all_to_all | solution.py:735
  16.0 2.1 %shard_map.130 = f32[8,40,128]{2,1,0:T(8,128)} custom-call(f32[59,4096]{1,0:T(8,128)} %refs_4_.1, f32[2,1,11]{2,1,0:T(1,128)} %refs_3_.7, s32[8,1,128]{2,1,0:T(1,128)} %all_to_all.25.refs_2_.refs_1_.refs_8_.refs_4_), custom_call_target="tpu_custom_call" | custom-call | tf_op jit(solution)/shard_map/pallas_call | solution.py:771
  18.2 11.6 %all_to_all.26.refs_0_ = f32[8,40,128]{2,1,0:T(8,128)} all-to-all(f32[8,40,128]{2,1,0:T(8,128)} %shard_map.130), channel_id=1, replica_groups=mesh['row'=8,'rep'=4] {'row'}, dimensions={0} | all-to-all | bytes 327680 | tf_op jit(solution)/shard_map/all_to_all | solution.py:735
  29.7 6.4 %shard_map.131 = (f32[2,1,3,4,256]{4,3,2,1,0:T(4,128)}, f32[8,40,128]{2,1,0:T(8,128)}) custom-call(f32[8,40,128]{2,1,0:T(8,128)} %all_to_all.26.refs_0_, f32[2,1,2,4]{3,2,1,0:T(2,128)} %bitcast.5, s32[2,1,4,4]{3,2,1,0:T(4,128)} %refs_2_.8, s32[2,1,4,512]{3,2,1,0:T(4,128)} %refs_5_.3, f32[2,1,3,4,256]{4,3,2,1,0:T(4,128)} %bitcast.3), custom_call_target="tpu_custom_call" | custom-call | tf_op jit(solution)/shard_map/pallas_call | solution.py:811
  36.2 11.6 %all_to_all.27.refs_0_ = f32[8,40,128]{2,1,0:T(8,128)} all-to-all(f32[8,40,128]{2,1,0:T(8,128)} %get-tuple-element.17), channel_id=1, replica_groups=mesh['row'=8,'rep'=4] {'row'}, dimensions={0} | all-to-all | bytes 327680 | tf_op jit(solution)/shard_map/all_to_all | solution.py:735
  47.7 1.8 %shard_map.132.refs_0_ = f32[304,128]{1,0:T(8,128)} custom-call(f32[8,40,128]{2,1,0:T(8,128)} %all_to_all.27.refs_0_, s32[8,1,128]{2,1,0:T(1,128)} %all_to_all.25.refs_2_.refs_1_.refs_8_.refs_4_, s32[1,2,2]{2,1,0:T(2,128)} %refs_9_.3, f32[2,1,11]{2,1,0:T(1,128)} %refs_3_.7), custom_call_target="tpu_custom_call" | custom-call | tf_op jit(solution)/shard_map/pallas_call | solution.py:794
  49.5 1.5 %collective-permute-start.1 = (f32[304,128]{1,0:T(8,128)}, f32[304,128]{1,0:T(8,128)S(1)}, u32[]{:S(2)}, u32[]{:S(2)}) collective-permute-start(f32[304,128]{1,0:T(8,128)} %shard_map.132.refs_0_), channel_id=1, source_target_pairs={{0,2},{1,3},{2,0},{3,1},{4,6},{5,7},{6,4},{7,5},{8,10},{9,11},{10,... | collective-permute-start | bytes 466952 | tf_op jit(solution)/shard_map/ppermute | solution.py:719
  51.0 0.0 collective-permute-start
  51.0 3.9 %collective-permute-done.1.refs_2_ = f32[304,128]{1,0:T(8,128)S(1)} collective-permute-done((f32[304,128]{1,0:T(8,128)}, f32[304,128]{1,0:T(8,128)S(1)}, u32[]{:S(2)}, u32[]{:S(2)}) %collective-permute-start.1) | collective-permute-done | bytes 155680 | tf_op jit(solution)/shard_map/ppermute | solution.py:719
  54.9 0.0 collective-permute-start.2
  54.9 0.0 collective-permute-done.refs_1_
  55.0 1.4 %collective-permute-done.2.refs_3_ = f32[304,128]{1,0:T(8,128)S(1)} collective-permute-done((f32[304,128]{1,0:T(8,128)S(1)}, f32[304,128]{1,0:T(8,128)S(1)}, u32[]{:S(2)}, u32[]{:S(2)}) %collective-permute-start.2) | collective-permute-done | bytes 155680 | tf_op jit(solution)/shard_map/ppermute | solution.py:719
  56.3 0.7 copy-done.7
  57.0 5.2 %shard_map.133 = (f32[59,4096]{1,0:T(8,128)}, f32[59,4096]{1,0:T(8,128)}, f32[59,4096]{1,0:T(8,128)}, f32[8,40,128]{2,1,0:T(8,128)}, f32[3,59,256]{2,1,0:T(8,128)}, /*index=5*/f32[3,59,256]{2,1,0:T(8,128)}) custom-call(f32[304,128]{1,0:T(8,128)} %shard_map.132.refs_0_, f32[304,128]{1,0:T(8,128)} %copy-done.6, f32[304,128]{1,0:T(8,128)} %copy-done.5, ...), custom_call_target="tpu_custom_call" | custom-call | tf_op jit(solution)/shard_map/pallas_call | solution.py:821
  62.2 12.0 %all_to_all.28.refs_0_ = f32[8,40,128]{2,1,0:T(8,128)} all-to-all(f32[8,40,128]{2,1,0:T(8,128)} %get-tuple-element.18), channel_id=1, replica_groups=mesh['row'=8,'rep'=4] {'row'}, dimensions={0} | all-to-all | bytes 327680 | tf_op jit(solution)/shard_map/all_to_all | solution.py:735
  74.2 6.6 %shard_map.134 = (f32[2,1,3,4,256]{4,3,2,1,0:T(4,128)}, f32[8,72,128]{2,1,0:T(8,128)}) custom-call(f32[8,40,128]{2,1,0:T(8,128)} %all_to_all.28.refs_0_, f32[2,1,2,4]{3,2,1,0:T(2,128)} %bitcast.6, s32[2,1,4,4]{3,2,1,0:T(4,128)} %refs_2_.8, s32[2,1,4,4]{3,2,1,0:T(4,128)} %refs_3_.6, s32[8,1,128]{2,1,0:T(1,128)} %all_to_all.25.refs_2_.refs_1_.refs_8_.refs_4_, ...), custom_call_target="tpu_custom_call" | custom-call | tf_op jit(solution)/shard_map/pallas_call | solution.py:802
  80.8 13.6 %all_to_all.29.refs_0_ = f32[8,72,128]{2,1,0:T(8,128)} all-to-all(f32[8,72,128]{2,1,0:T(8,128)} %get-tuple-element.20), channel_id=1, replica_groups=mesh['row'=8,'rep'=4] {'row'}, dimensions={0} | all-to-all | bytes 589824 | tf_op jit(solution)/shard_map/all_to_all | solution.py:735
  94.4 1.9 %shard_map.135.refs_0_ = f32[304,128]{1,0:T(8,128)} custom-call(f32[8,72,128]{2,1,0:T(8,128)} %all_to_all.29.refs_0_, s32[8,1,128]{2,1,0:T(1,128)} %all_to_all.25.refs_2_.refs_1_.refs_8_.refs_4_, s32[1,2,2]{2,1,0:T(2,128)} %refs_9_.3, f32[2,1,11]{2,1,0:T(1,128)} %refs_3_.7), custom_call_target="tpu_custom_call" | custom-call | tf_op jit(solution)/shard_map/pallas_call | solution.py:794
  96.3 1.5 %collective-permute-start.4 = (f32[304,128]{1,0:T(8,128)}, f32[304,128]{1,0:T(8,128)S(1)}, u32[]{:S(2)}, u32[]{:S(2)}) collective-permute-start(f32[304,128]{1,0:T(8,128)} %shard_map.135.refs_0_), channel_id=1, source_target_pairs={{0,2},{1,3},{2,0},{3,1},{4,6},{5,7},{6,4},{7,5},{8,10},{9,11},{10,... | collective-permute-start | bytes 466952 | tf_op jit(solution)/shard_map/ppermute | solution.py:719
  97.8 0.7 collective-permute-start.6
  98.5 4.0 %collective-permute-start.7 = (f32[3,59,256]{2,1,0:T(8,128)S(1)}, f32[3,59,256]{2,1,0:T(8,128)S(1)}, u32[]{:S(2)}, u32[]{:S(2)}) collective-permute-start(f32[3,59,256]{2,1,0:T(8,128)S(1)} %copy-done.8), channel_id=1, source_target_pairs={{0,28},{4,0},{8,4},{12,8},{16,12},{20,16},{24,20},{28,24},{1,29},{... | collective-permute-start | bytes 543752 | tf_op jit(solution)/shard_map/ppermute | solution.py:724
  102.6 0.0 collective-permute-start.3
  102.6 0.5 collective-permute-start.5
  103.1 3.2 %collective-permute-done.6.refs_7_ = f32[3,59,256]{2,1,0:T(8,128)S(1)} collective-permute-done((f32[3,59,256]{2,1,0:T(8,128)S(1)}, f32[3,59,256]{2,1,0:T(8,128)S(1)}, u32[]{:S(2)}, u32[]{:S(2)}) %collective-permute-start.6) | collective-permute-done | bytes 181280 | tf_op jit(solution)/shard_map/ppermute | solution.py:724
  106.3 0.0 collective-permute-done.7.refs_8_
  106.3 0.0 collective-permute-done.3.refs_1_
  106.4 0.6 copy-done
  107.0 0.1 copy-done.1
  107.1 0.1 copy-done.3
  107.1 0.0 copy-done.4
  107.2 5.0 %shard_map.136 = (f32[59,4096]{1,0:T(8,128)}, f32[59,4096]{1,0:T(8,128)}, f32[59,4096]{1,0:T(8,128)}) custom-call(f32[304,128]{1,0:T(8,128)} %shard_map.135.refs_0_, f32[304,128]{1,0:T(8,128)} %copy-done.3, f32[304,128]{1,0:T(8,128)} %copy-done.2, f32[304,128]{1,0:T(8,128)} %copy-done.4, f32[59,4096]{1,0:T(8,128)} %get-tuple-element.21.refs_4_, ...), custom_call_target="tpu_custom_call" | custom-call | tf_op jit(solution)/shard_map/pallas_call | solution.py:836
  (17 shorter events, 0.0 us)
Async XLA Ops:
  49.5 5.4 %collective-permute-start.1 = (f32[304,128]{1,0:T(8,128)}, f32[304,128]{1,0:T(8,128)S(1)}, u32[]{:S(2)}, u32[]{:S(2)}) collective-permute-start(f32[304,128]{1,0:T(8,128)} %shard_map.132.refs_0_), channel_id=1, source_target_pairs={{0,2},{1,3},{2,0},{3,1},{4,6},{5,7},{6,4},{7,5},{8,10},{9,11},{10,... | collective-permute-start | bytes 466952 | tf_op jit(solution)/shard_map/ppermute | solution.py:719
  51.0 4.0 %collective-permute-start = (f32[304,128]{1,0:T(8,128)}, f32[304,128]{1,0:T(8,128)S(1)}, u32[]{:S(2)}, u32[]{:S(2)}) collective-permute-start(f32[304,128]{1,0:T(8,128)} %shard_map.132.refs_0_), channel_id=1, source_target_pairs={{0,1},{1,0},{2,3},{3,2},{4,5},{5,4},{6,7},{7,6},{8,9},{9,8},{10,11... | collective-permute-start | bytes 466952 | tf_op jit(solution)/shard_map/ppermute | solution.py:719
  54.9 1.4 %copy-start.5 = (f32[304,128]{1,0:T(8,128)}, f32[304,128]{1,0:T(8,128)S(1)}, u32[]{:S(2)}) copy-start(f32[304,128]{1,0:T(8,128)S(1)} %collective-permute-done.1.refs_2_) | copy-start | bytes 466948
  54.9 1.4 %collective-permute-start.2 = (f32[304,128]{1,0:T(8,128)S(1)}, f32[304,128]{1,0:T(8,128)S(1)}, u32[]{:S(2)}, u32[]{:S(2)}) collective-permute-start(f32[304,128]{1,0:T(8,128)S(1)} %collective-permute-done.1.refs_2_), channel_id=1, source_target_pairs={{0,1},{1,0},{2,3},{3,2},{4,5},{5,4},{6,7},{7,6},{8,9},{9,8},{10,11... | collective-permute-start | bytes 466952 | tf_op jit(solution)/shard_map/ppermute | solution.py:719
  54.9 1.4 %copy-start.6 = (f32[304,128]{1,0:T(8,128)}, f32[304,128]{1,0:T(8,128)S(1)}, u32[]{:S(2)}) copy-start(f32[304,128]{1,0:T(8,128)S(1)} %collective-permute-done.refs_1_) | copy-start | bytes 466948
  56.3 0.7 copy-start.7
  94.4 3.4 %copy-start.9 = (f32[3,59,256]{2,1,0:T(8,128)S(1)}, f32[3,59,256]{2,1,0:T(8,128)}, u32[]{:S(2)}) copy-start(f32[3,59,256]{2,1,0:T(8,128)} %get-tuple-element.24) | copy-start | bytes 543748
  94.4 4.1 %copy-start.8 = (f32[3,59,256]{2,1,0:T(8,128)S(1)}, f32[3,59,256]{2,1,0:T(8,128)}, u32[]{:S(2)}) copy-start(f32[3,59,256]{2,1,0:T(8,128)} %get-tuple-element.25) | copy-start | bytes 543748
  96.3 6.2 %collective-permute-start.4 = (f32[304,128]{1,0:T(8,128)}, f32[304,128]{1,0:T(8,128)S(1)}, u32[]{:S(2)}, u32[]{:S(2)}) collective-permute-start(f32[304,128]{1,0:T(8,128)} %shard_map.135.refs_0_), channel_id=1, source_target_pairs={{0,2},{1,3},{2,0},{3,1},{4,6},{5,7},{6,4},{7,5},{8,10},{9,11},{10,... | collective-permute-start | bytes 466952 | tf_op jit(solution)/shard_map/ppermute | solution.py:719
  97.8 8.5 %collective-permute-start.6 = (f32[3,59,256]{2,1,0:T(8,128)S(1)}, f32[3,59,256]{2,1,0:T(8,128)S(1)}, u32[]{:S(2)}, u32[]{:S(2)}) collective-permute-start(f32[3,59,256]{2,1,0:T(8,128)S(1)} %copy-done.9), channel_id=1, source_target_pairs={{0,4},{4,8},{8,12},{12,16},{16,20},{20,24},{24,28},{28,0},{1,5},{5... | collective-permute-start | bytes 543752 | tf_op jit(solution)/shard_map/ppermute | solution.py:724
  98.5 7.8 %collective-permute-start.7 = (f32[3,59,256]{2,1,0:T(8,128)S(1)}, f32[3,59,256]{2,1,0:T(8,128)S(1)}, u32[]{:S(2)}, u32[]{:S(2)}) collective-permute-start(f32[3,59,256]{2,1,0:T(8,128)S(1)} %copy-done.8), channel_id=1, source_target_pairs={{0,28},{4,0},{8,4},{12,8},{16,12},{20,16},{24,20},{28,24},{1,29},{... | collective-permute-start | bytes 543752 | tf_op jit(solution)/shard_map/ppermute | solution.py:724
  102.6 3.8 %collective-permute-start.3 = (f32[304,128]{1,0:T(8,128)}, f32[304,128]{1,0:T(8,128)S(1)}, u32[]{:S(2)}, u32[]{:S(2)}) collective-permute-start(f32[304,128]{1,0:T(8,128)} %shard_map.135.refs_0_), channel_id=1, source_target_pairs={{0,1},{1,0},{2,3},{3,2},{4,5},{5,4},{6,7},{7,6},{8,9},{9,8},{10,11... | collective-permute-start | bytes 466952 | tf_op jit(solution)/shard_map/ppermute | solution.py:719
  102.6 3.8 %copy-start.2 = (f32[304,128]{1,0:T(8,128)}, f32[304,128]{1,0:T(8,128)S(1)}, u32[]{:S(2)}) copy-start(f32[304,128]{1,0:T(8,128)S(1)} %collective-permute-done.4.refs_2_) | copy-start | bytes 466948
  102.6 3.8 %collective-permute-start.5 = (f32[304,128]{1,0:T(8,128)S(1)}, f32[304,128]{1,0:T(8,128)S(1)}, u32[]{:S(2)}, u32[]{:S(2)}) collective-permute-start(f32[304,128]{1,0:T(8,128)S(1)} %collective-permute-done.4.refs_2_), channel_id=1, source_target_pairs={{0,1},{1,0},{2,3},{3,2},{4,5},{5,4},{6,7},{7,6},{8,9},{9,8},{10,11... | collective-permute-start | bytes 466952 | tf_op jit(solution)/shard_map/ppermute | solution.py:719
  106.3 0.7 copy-start
  106.3 0.8 copy-start.1
  106.3 0.8 copy-start.3
  106.3 0.8 copy-start.4

commit v4 on v3

--- a/solution.py
+++ b/solution.py
@@ -100,7 +100,7 @@
     return rank
 
 
-def request_kernel(capacity, owner_ref, block_ref, migration_ref, out_ref):
+def request_kernel(capacity, owner_ref, block_ref, migration_ref, out_ref, ranks_ref):
     owners = out_ref.shape[0]
     tiles = owner_ref.shape[2]
     lane = lax.broadcasted_iota(jnp.int32, (owners, BLOCK), 1)
@@ -110,7 +110,9 @@
     for step in range(ITERS):
         names = [owner_ref[step, 0, t, j] for t in range(tiles) for j in range(LISTB)]
         for index in range(tiles * LISTB):
-            target = names[index] * BLOCK + step * capacity + rank_of(names, index)
+            rank = rank_of(names, index)
+            ranks_ref[step, index] = rank
+            target = names[index] * BLOCK + step * capacity + rank
             block = block_ref[step, 0, index // LISTB, index % LISTB]
             message = jnp.where(place == target, block, message)
     for side in range(2):
@@ -158,7 +160,7 @@
     return cov_yy * inverse, -cov_xy * inverse, cov_xx * inverse
 
 
-def serve(step, capacity, blocks, camera_ref, asked_ref, dense, table, out_ref):
+def fill_table(step, blocks, camera_ref, dense, table):
     wide = pitch(blocks)
     cam = [camera_ref[step, 0, k] for k in range(11)]
     basis = harmonics(cam[8], cam[9], cam[10])
@@ -185,6 +187,9 @@
         rows.append(-LOG2E * jnp.log(1.0 + jnp.exp(-row(10))))
         for k in range(9):
             table[pl.ds(72 * group + k, 8, stride=9), :] = rows[k]
+
+
+def serve(step, capacity, asked_ref, table, out_ref):
     owners = out_ref.shape[0]
     for peer in range(owners):
         for slot in range(capacity):
@@ -199,14 +204,19 @@
     return [(first, min(8, P_SIZE - first)) for first in range(0, P_SIZE, 8)]
 
 
-def start_kernel(capacity, params_ref, camera_ref, asked_ref, out_ref, dense, table):
+def project_kernel(params_ref, camera_ref, table, dense):
     blocks = params_ref.shape[1] // BLOCK
+    wide = pitch(blocks)
     for block in range(blocks):
         for first, count in row_groups():
-            dense[pl.ds(first * pitch(blocks) + block, count, stride=pitch(blocks)), :] = params_ref[
+            dense[pl.ds(first * wide + block, count, stride=wide), :] = params_ref[
                 first : first + count, block * BLOCK : (block + 1) * BLOCK
             ]
-    serve(0, capacity, blocks, camera_ref, asked_ref, dense, table, out_ref)
+    fill_table(0, blocks, camera_ref, dense, table)
+
+
+def serve_kernel(capacity, table, asked_ref, out_ref):
+    serve(0, capacity, asked_ref, table, out_ref)
 
 
 def pixel_features(rows, per):
@@ -245,13 +255,13 @@
 def render_kernel(step, capacity, slots, final, *refs):
     if final:
         (
-            arrived, corner_ref, owner_ref, block_ref, asked_ref, order_ref, target_ref, earlier_ref,
+            arrived, corner_ref, owner_ref, ranks_ref, block_ref, asked_ref, order_ref, target_ref, earlier_ref,
             picture_ref, out_ref, *scratch,
         ) = refs
         for other in range(ITERS - 1):
             picture_ref[other] = earlier_ref[other]
     else:
-        arrived, corner_ref, owner_ref, order_ref, target_ref, picture_ref, out_ref, *scratch = refs
+        arrived, corner_ref, owner_ref, ranks_ref, order_ref, target_ref, picture_ref, out_ref, *scratch = refs
     onehots, sorted_ref, coeffs, shades_ref, sums_ref, grads_ref, *per_tile = scratch
     owners = arrived.shape[0]
     tiles = owner_ref.shape[2]
@@ -264,7 +274,7 @@
     flat = pixel_features(16, 1)
 
     names = [owner_ref[step, 0, t, j] for t in range(tiles) for j in range(LISTB)]
-    ranks = [rank_of(names, index) for index in range(tiles * LISTB)]
+    ranks = [ranks_ref[step, index] for index in range(tiles * LISTB)]
 
     order = order_ref[step, 0]
     order = jnp.concatenate([order] * (8 // tiles), axis=0)
@@ -646,7 +656,8 @@
             new_first[part, lanes] = first
             new_second[part, lanes] = second
             dense[where, :] = value
-    serve(1, capacity, blocks, camera_ref, asked_ref, dense, table, out_ref)
+    fill_table(1, blocks, camera_ref, dense, table)
+    serve(1, capacity, asked_ref, table, out_ref)
     for side, ref in ((0, left_ref), (1, right_ref)):
         for j in range(MIGH):
             lanes = pl.ds(pl.multiple_of(migration_ref[0, side, j] * BLOCK, BLOCK), BLOCK)
@@ -714,6 +725,14 @@
     return run
 
 
+def grant(mebibytes):
+    return pltpu.CompilerParams(vmem_limit_bytes=mebibytes << 20)
+
+
+def near_core(*values):
+    return [pltpu.with_memory_space_constraint(value, pltpu.VMEM) for value in values]
+
+
 def swap(value, axis, offset):
     count = lax.axis_size(axis)
     return lax.ppermute(value, axis, [(i, i ^ offset) for i in range(count)])
@@ -759,22 +778,31 @@
     payload = 9 * blocks + CAM_ROWS
     cams = pltpu.VMEM((replicas, payload, BLOCK), f32)
     state = [shape(params.shape)] * 3
-
-    lists = pl.pallas_call(
+    kept = [pltpu.VMEM(params.shape, f32)] * 3
+
+    lists, ranks = pl.pallas_call(
         bind(request_kernel, capacity),
-        out_shape=shape((owners, 1, BLOCK), jnp.int32),
+        out_shape=[
+            shape((owners, 1, BLOCK), jnp.int32), shape((ITERS, requests), jnp.int32)
+        ],
         in_specs=[SM, SM, SM],
-        out_specs=VM,
+        out_specs=[VM, SM],
+        compiler_params=grant(8),
     )(tile_owner, tile_block, migration)
     asked = row_exchange(lists)
-
+    projected = pl.pallas_call(
+        project_kernel,
+        out_shape=shape((9 * blocks, BLOCK)),
+        in_specs=[VM, SM],
+        out_specs=VM,
+        scratch_shapes=[dense],
+        compiler_params=grant(8),
+    )(params, camera)
+    message = shape((owners, up8(9 * capacity), BLOCK))
     outgoing = pl.pallas_call(
-        bind(start_kernel, capacity),
-        out_shape=shape((owners, up8(9 * capacity), BLOCK)),
-        in_specs=[VM, SM, SM],
-        out_specs=VM,
-        scratch_shapes=[dense, table],
-    )(params, camera, asked)
+        bind(serve_kernel, capacity), out_shape=message, in_specs=[VM, SM], out_specs=VM,
+        compiler_params=grant(8),
+    )(projected, asked)
 
     deep = pltpu.VMEM((DEPTH, PIX), f32)
     packed = pltpu.VMEM((DEPTH, PIX), bf16)
@@ -793,39 +821,47 @@
     def gather(step, count, returned):
         return pl.pallas_call(
             bind(gather_kernel, step, capacity, count),
-            out_shape=shape((payload, BLOCK)),
+            out_shape=pltpu.VMEM((payload, BLOCK), f32),
+            compiler_params=grant(8),
             in_specs=[VM, SM, SM, SM],
             out_specs=VM,
-        )(returned, asked, migration, camera)
+        )(*near_core(returned), asked, migration, camera)
 
     def second(arrived, pictures):
         return pl.pallas_call(
             bind(render_kernel, 1, capacity, slots, True),
             out_shape=[pictures_shape, shape((owners, up8(9 * slots), BLOCK))],
-            in_specs=[VM, SM, SM, SM, SM, VM, VM, VM],
+            in_specs=[VM, SM, SM, SM, SM, SM, VM, VM, VM],
             out_specs=[VM, VM],
             scratch_shapes=render_scratch,
-        )(arrived, corners, tile_owner, tile_block, asked, depth_order, photos, pictures)
+            compiler_params=grant(24),
+        )(
+            *near_core(arrived), corners, tile_owner, ranks, tile_block, asked, depth_order, photos,
+            pictures,
+        )
 
     arrived = row_exchange(outgoing)
     pictures, back = pl.pallas_call(
         bind(render_kernel, 0, capacity, capacity, False),
         out_shape=[pictures_shape, shape((owners, up8(9 * capacity), BLOCK))],
-        in_specs=[VM, SM, SM, VM, VM],
+        in_specs=[VM, SM, SM, SM, VM, VM],
         out_specs=[VM, VM],
         scratch_shapes=render_scratch,
-    )(arrived, corners, tile_owner, depth_order, photos)
+        compiler_params=grant(24),
+    )(*near_core(arrived), corners, tile_owner, ranks, depth_order, photos)
     own = gather(0, capacity, row_exchange(back))
     near, far, cross = exchange(own)
-    leaving = shape((3, P_SIZE, MIGH * BLOCK))
+    leaving = pltpu.VMEM((3, P_SIZE, MIGH * BLOCK), f32)
     current, moment_one, moment_two, outgoing, left, right = pl.pallas_call(
         bind(update_kernel, capacity),
-        out_shape=state + [shape((owners, up8(9 * capacity), BLOCK)), leaving, leaving],
+        out_shape=kept + [shape((owners, up8(9 * capacity), BLOCK)), leaving, leaving],
         in_specs=[VM] * 7 + [SM] * 3,
         out_specs=[VM] * 6,
         scratch_shapes=[cams, dense, dense, table],
+        compiler_params=grant(16),
     )(
-        own, near, far, cross, params, first_moment, second_moment, camera, asked, migration
+        *near_core(own, near, far, cross, params, first_moment, second_moment),
+        camera, asked, migration,
     )
     arrived = row_exchange(outgoing)
     below = turn(right, "row", 1)
@@ -839,7 +875,10 @@
         in_specs=[VM] * 9 + [SM],
         out_specs=[VM] * 3,
         scratch_shapes=[cams, dense, dense],
-    )(own, near, far, cross, current, moment_one, moment_two, below, above, migration)
+        compiler_params=grant(16),
+    )(
+        *near_core(own, near, far, cross, current, moment_one, moment_two, below, above), migration
+    )
     return current, moment_one, moment_two, jnp.swapaxes(pictures, 2, 3)
 
 

time: 113 us -> 99.7 us (0.88)
  blocking collectives: 62.5 us -> 43.4 us
  Pallas kernels: 30.7 us -> 21.6 us
  starting transfers between devices: 8.22 us -> 15.7 us
  waiting for transfers between devices: 8.55 us -> 13.2 us
  local copies, waits for them, and re-layouts: 1.51 us -> 4.54 us
    all_to_all x5 -> x4, blocking collectives: 62.5 us -> 43.4 us  [row_exchange(): return lax.all_to_all(value, 'row', split_axis=0, concat_axis=0, tiled=True)]
    all_to_all x0 -> x1, starting transfers between devices: none -> 7.32 us  [row_exchange(): return lax.all_to_all(value, 'row', split_axis=0, concat_axis=0, tiled=True)]
    pallas_call x5 -> x6, Pallas kernels: 12.7 us -> 6.78 us  [the longest x1 2.12 us: local(): pl.pallas_call(bind(update_kernel, capacity), out_shape=kept + [shape((ow...]
    all_to_all x0 -> x1, waiting for transfers between devices: none -> 4.38 us  [row_exchange(): return lax.all_to_all(value, 'row', split_axis=0, concat_axis=0, tiled=True)]
    unnamed x20 -> x28, local copies, waits for them, and re-layouts: 1.51 us -> 4.54 us
    pallas_call x1, Pallas kernels: 4.97 us -> 3.41 us  [local(): pl.pallas_call(final_kernel, out_shape=state, in_specs=[VM] * 9 + [SM], o...]
  transfers between devices with their start and end apart: 8 -> 9, of which waited for: 3 -> 5; matrix products, arithmetic and copies ran while one was open for 0% -> 0% of each run, Pallas kernels for 0% -> 1%
where the time goes in v4:
time: 99.7 us; the launch traced here: 99.2 us
  blocking collectives  43.4 us (44%)
  Pallas kernels  21.6 us (22%)
  starting transfers between devices  15.7 us (16%)
  waiting for transfers between devices  13.2 us (13%)
  local copies, waits for them, and re-layouts  4.54 us (5%)
    all_to_all x4, blocking collectives, row_exchange(): return lax.all_to_all(value, 'row', split_axis=0, concat_axis=0, tiled=True)  43.4 us
    all_to_all x1, starting transfers between devices, row_exchange(): return lax.all_to_all(value, 'row', split_axis=0, concat_axis=0, tiled=True)  7.32 us
    pallas_call x1, Pallas kernels, second(): pl.pallas_call(bind(render_kernel, 1, capacity, slots, True), out_shape=[...  6.08 us
    pallas_call x1, Pallas kernels, local(): pl.pallas_call(bind(render_kernel, 0, capacity, capacity, False), out_sha...  5.36 us
    ppermute x6, waiting for transfers between devices, swap(): return lax.ppermute(value, axis, [(i, i ^ offset) for i in range(count)])  5.12 us
    ppermute x2, starting transfers between devices, turn(): lax.ppermute(value, axis, [(i, (i + offset) % count) for i in range(count)])  4.72 us
    unnamed x28, local copies, waits for them, and re-layouts  4.54 us
    all_to_all x1, waiting for transfers between devices, row_exchange(): return lax.all_to_all(value, 'row', split_axis=0, concat_axis=0, tiled=True)  4.38 us
  transfers between devices with their start and end apart: 9, of which 5 were waited for; matrix products, arithmetic and copies ran while one was open for 0% of the time, Pallas kernels for 1%

profile of v4, /device:TPU:0, one launch (start us, length us, event | category | flops | bytes accessed | tf_op | source)
XLA Modules:
  0.0 99.2 jit_solution(8072007148494746527)
XLA Ops:
  0.6 0.7 copy-done.6
  1.3 0.7 copy-done.8
  2.0 0.7 copy-done.10
  2.7 1.6 %shard_map.130 = (s32[8,1,128]{2,1,0:T(1,128)}, s32[2,16]{1,0:T(2,128)S(1)}) custom-call(s32[2,1,4,4]{3,2,1,0:T(4,128)S(1)} %copy-done.6, s32[2,1,4,4]{3,2,1,0:T(4,128)S(1)} %copy-done.10, s32[1,2,2]{2,1,0:T(2,128)S(1)} %copy-done.8), custom_call_target="tpu_custom_call" | custom-call | tf_op jit(solution)/shard_map/pallas_call | solution.py:783
  4.3 7.3 %all-to-all-start = ((s32[8,1,128]{2,1,0:T(1,128)}), s32[8,1,128]{2,1,0:T(1,128)S(1)}, u32[]{:S(2)}, u32[]{:S(2)}) async-start(s32[8,1,128]{2,1,0:T(1,128)} %get-tuple-element.19), calls=%async_computation | async-start | bytes 8192 | tf_op jit(solution)/shard_map/all_to_all | solution.py:754
  11.6 1.2 %copy-done = f32[59,4096]{1,0:T(8,128)S(1)} copy-done((f32[59,4096]{1,0:T(8,128)S(1)}, f32[59,4096]{1,0:T(8,128)}, u32[]{:S(2)}) %copy-start) | copy-done | bytes 966680
  12.8 0.0 copy-start.2
  12.9 0.8 shard_map.129.refs_0_
  13.6 0.0 copy-start.1
  13.6 4.4 %all-to-all-done.refs_1_.refs_8_.refs_5_ = s32[8,1,128]{2,1,0:T(1,128)S(1)} async-done(((s32[8,1,128]{2,1,0:T(1,128)}), s32[8,1,128]{2,1,0:T(1,128)S(1)}, u32[]{:S(2)}, u32[]{:S(2)}) %all-to-all-start) | async-done | bytes 4128 | tf_op jit(solution)/shard_map/all_to_all | solution.py:754
  18.0 0.7 shard_map.131
  18.7 10.0 %all_to_all.25.refs_0_ = f32[8,40,128]{2,1,0:T(8,128)S(1)} all-to-all(f32[8,40,128]{2,1,0:T(8,128)S(1)} %shard_map.131), channel_id=1, replica_groups=mesh['row'=8,'rep'=4] {'row'}, dimensions={0} | all-to-all | bytes 327680 | tf_op jit(solution)/shard_map/all_to_all | solution.py:754
  28.7 5.4 %shard_map.132 = (f32[2,1,3,4,256]{4,3,2,1,0:T(4,128)S(1)}, f32[8,40,128]{2,1,0:T(8,128)S(1)}) custom-call(f32[8,40,128]{2,1,0:T(8,128)S(1)} %all_to_all.25.refs_0_, f32[2,1,2,4]{3,2,1,0:T(2,128)S(1)} %bitcast.5, s32[2,1,4,4]{3,2,1,0:T(4,128)S(1)} %copy-done.7, s32[2,16]{1,0:T(2,128)S(1)} %get-tuple-element.20.refs_3_, s32[2,1,4,512]{3,2,1,0:T(4,128)S(1)} %copy-done.5, ...), custom_call_target="tpu_custom_call" | custom-call | tf_op jit(solution)/shard_map/pallas_call | solution.py:844
  34.0 10.1 %all_to_all.26.refs_0_ = f32[8,40,128]{2,1,0:T(8,128)S(1)} all-to-all(f32[8,40,128]{2,1,0:T(8,128)S(1)} %get-tuple-element.21), channel_id=1, replica_groups=mesh['row'=8,'rep'=4] {'row'}, dimensions={0} | all-to-all | bytes 327680 | tf_op jit(solution)/shard_map/all_to_all | solution.py:754
  44.1 0.8 shard_map.133.refs_0_
  44.9 1.6 %collective-permute-start.1 = (f32[304,128]{1,0:T(8,128)S(1)}, f32[304,128]{1,0:T(8,128)S(1)}, u32[]{:S(2)}, u32[]{:S(2)}) collective-permute-start(f32[304,128]{1,0:T(8,128)S(1)} %shard_map.133.refs_0_), channel_id=1, source_target_pairs={{0,2},{1,3},{2,0},{3,1},{4,6},{5,7},{6,4},{7,5},{8,10},{9,11},{10,... | collective-permute-start | bytes 466952 | tf_op jit(solution)/shard_map/ppermute | solution.py:738
  46.5 3.7 %collective-permute-done.1.refs_2_ = f32[304,128]{1,0:T(8,128)S(1)} collective-permute-done((f32[304,128]{1,0:T(8,128)S(1)}, f32[304,128]{1,0:T(8,128)S(1)}, u32[]{:S(2)}, u32[]{:S(2)}) %collective-permute-start.1) | collective-permute-done | bytes 155680 | tf_op jit(solution)/shard_map/ppermute | solution.py:738
  50.2 1.4 %collective-permute-done.2.refs_3_ = f32[304,128]{1,0:T(8,128)S(1)} collective-permute-done((f32[304,128]{1,0:T(8,128)S(1)}, f32[304,128]{1,0:T(8,128)S(1)}, u32[]{:S(2)}, u32[]{:S(2)}) %collective-permute-start.2) | collective-permute-done | bytes 155680 | tf_op jit(solution)/shard_map/ppermute | solution.py:738
  51.6 1.2 %copy-done.3 = f32[59,4096]{1,0:T(8,128)S(1)} copy-done((f32[59,4096]{1,0:T(8,128)S(1)}, f32[59,4096]{1,0:T(8,128)}, u32[]{:S(2)}) %copy-start.3) | copy-done | bytes 966680
  52.9 2.1 %shard_map.134 = (f32[59,4096]{1,0:T(8,128)S(1)}, f32[59,4096]{1,0:T(8,128)S(1)}, f32[59,4096]{1,0:T(8,128)S(1)}, f32[8,40,128]{2,1,0:T(8,128)S(1)}, f32[3,59,25...) custom-call(f32[304,128]{1,0:T(8,128)S(1)} %shard_map.133.refs_0_, f32[304,128]{1,0:T(8,128)S(1)} %collective-permute-done.refs_1_, ...), custom_call_target="tpu_custom_call" | custom-call | tf_op jit(solution)/shard_map/pallas_call | solution.py:855
  55.0 0.0 copy-start.11
  55.0 10.5 %all_to_all.27.refs_0_ = f32[8,40,128]{2,1,0:T(8,128)S(1)} all-to-all(f32[8,40,128]{2,1,0:T(8,128)S(1)} %get-tuple-element.22), channel_id=1, replica_groups=mesh['row'=8,'rep'=4] {'row'}, dimensions={0} | all-to-all | bytes 327680 | tf_op jit(solution)/shard_map/all_to_all | solution.py:754
  65.5 6.1 %shard_map.135 = (f32[2,1,3,4,256]{4,3,2,1,0:T(4,128)}, f32[8,72,128]{2,1,0:T(8,128)S(1)}) custom-call(f32[8,40,128]{2,1,0:T(8,128)S(1)} %all_to_all.27.refs_0_, f32[2,1,2,4]{3,2,1,0:T(2,128)S(1)} %bitcast.6, s32[2,1,4,4]{3,2,1,0:T(4,128)S(1)} %copy-done.7, s32[2,16]{1,0:T(2,128)S(1)} %get-tuple-element.20.refs_3_, s32[2,1,4,4]{3,2,1,0:T(4,128)S(1)} %copy-done.11, ...), custom_call_target="tpu_custom_call" | custom-call | tf_op jit(solution)/shard_map/pallas_call | solution.py:831
  71.5 12.9 %all_to_all.28.refs_0_ = f32[8,72,128]{2,1,0:T(8,128)S(1)} all-to-all(f32[8,72,128]{2,1,0:T(8,128)S(1)} %get-tuple-element.24), channel_id=1, replica_groups=mesh['row'=8,'rep'=4] {'row'}, dimensions={0} | all-to-all | bytes 589824 | tf_op jit(solution)/shard_map/all_to_all | solution.py:754
  84.4 0.9 shard_map.136.refs_0_
  85.3 1.6 %collective-permute-start.4 = (f32[304,128]{1,0:T(8,128)S(1)}, f32[304,128]{1,0:T(8,128)S(1)}, u32[]{:S(2)}, u32[]{:S(2)}) collective-permute-start(f32[304,128]{1,0:T(8,128)S(1)} %shard_map.136.refs_0_), channel_id=1, source_target_pairs={{0,2},{1,3},{2,0},{3,1},{4,6},{5,7},{6,4},{7,5},{8,10},{9,11},{10,... | collective-permute-start | bytes 466952 | tf_op jit(solution)/shard_map/ppermute | solution.py:738
  86.9 0.7 collective-permute-start.6
  87.6 4.0 %collective-permute-start.7 = (f32[3,59,256]{2,1,0:T(8,128)S(1)}, f32[3,59,256]{2,1,0:T(8,128)S(1)}, u32[]{:S(2)}, u32[]{:S(2)}) collective-permute-start(f32[3,59,256]{2,1,0:T(8,128)S(1)} %get-tuple-element.29), channel_id=1, source_target_pairs={{0,28},{4,0},{8,4},{12,8},{16,12},{20,16},{24,20},{28,24},{1,29},{... | collective-permute-start | bytes 543752 | tf_op jit(solution)/shard_map/ppermute | solution.py:743
  91.6 0.5 collective-permute-start.5
  92.1 3.2 %collective-permute-done.6.refs_7_ = f32[3,59,256]{2,1,0:T(8,128)S(1)} collective-permute-done((f32[3,59,256]{2,1,0:T(8,128)S(1)}, f32[3,59,256]{2,1,0:T(8,128)S(1)}, u32[]{:S(2)}, u32[]{:S(2)}) %collective-permute-start.6) | collective-permute-done | bytes 181280 | tf_op jit(solution)/shard_map/ppermute | solution.py:743
  95.3 0.5 collective-permute-done.7.refs_8_
  95.8 3.4 %shard_map.137 = (f32[59,4096]{1,0:T(8,128)}, f32[59,4096]{1,0:T(8,128)}, f32[59,4096]{1,0:T(8,128)}) custom-call(f32[304,128]{1,0:T(8,128)S(1)} %shard_map.136.refs_0_, f32[304,128]{1,0:T(8,128)S(1)} %collective-permute-done.3.refs_1_, f32[304,128]{1,0:T(8,128)S(1)} %collective-permute-done.4.refs_2_, f32[304,128]{1,0:T(8,128)S(1)} %collective-permute-done.5.refs_3_, ...), custom_call_target="tpu_custom_call" | custom-call | tf_op jit(solution)/shard_map/pallas_call | solution.py:872
  (27 shorter events, 0.1 us)
Async XLA Ops:
  0.6 0.7 copy-start.6
  1.3 0.7 copy-start.8
  2.0 0.7 copy-start.10
  4.3 7.3 %copy-start.12 = (f32[2,1,11]{2,1,0:T(1,128)S(1)}, f32[2,1,11]{2,1,0:T(1,128)}, u32[]{:S(2)}) copy-start(f32[2,1,11]{2,1,0:T(1,128)} %refs_3_.3) | copy-start | bytes 268
  4.3 13.7 %all-to-all-start = ((s32[8,1,128]{2,1,0:T(1,128)}), s32[8,1,128]{2,1,0:T(1,128)S(1)}, u32[]{:S(2)}, u32[]{:S(2)}) async-start(s32[8,1,128]{2,1,0:T(1,128)} %get-tuple-element.19), calls=%async_computation | async-start | bytes 8192 | tf_op jit(solution)/shard_map/all_to_all | solution.py:754
  11.6 1.2 %copy-start = (f32[59,4096]{1,0:T(8,128)S(1)}, f32[59,4096]{1,0:T(8,128)}, u32[]{:S(2)}) copy-start(f32[59,4096]{1,0:T(8,128)} %refs_4_.4) | copy-start | bytes 2899972
  12.8 15.8 %copy-start.4 = (f32[2,1,4,3,256]{4,2,3,1,0:T(4,128)S(1)}, f32[2,1,4,3,256]{4,2,3,1,0:T(4,128)}, u32[]{:S(2)}) copy-start(f32[2,1,4,3,256]{4,2,3,1,0:T(4,128)} %param.18) | copy-start | bytes 73732
  12.8 15.8 %copy-start.5 = (s32[2,1,4,512]{3,2,1,0:T(4,128)S(1)}, s32[2,1,4,512]{3,2,1,0:T(4,128)}, u32[]{:S(2)}) copy-start(s32[2,1,4,512]{3,2,1,0:T(4,128)} %refs_6_.3) | copy-start | bytes 49156
  12.8 15.8 %copy-start.7 = (s32[2,1,4,4]{3,2,1,0:T(4,128)S(1)}, s32[2,1,4,4]{3,2,1,0:T(4,128)}, u32[]{:S(2)}) copy-start(s32[2,1,4,4]{3,2,1,0:T(4,128)} %refs_2_.8) | copy-start | bytes 388
  12.8 15.8 %copy-start.13 = (f32[2,1,4,2]{2,3,1,0:T(2,128)S(1)}, f32[2,1,4,2]{2,3,1,0:T(2,128)}, u32[]{:S(2)}) copy-start(f32[2,1,4,2]{2,3,1,0:T(2,128)} %param.14) | copy-start | bytes 196
  12.8 38.8 %copy-start.2 = (f32[59,4096]{1,0:T(8,128)S(1)}, f32[59,4096]{1,0:T(8,128)}, u32[]{:S(2)}) copy-start(f32[59,4096]{1,0:T(8,128)} %refs_5_.1) | copy-start | bytes 2899972
  13.6 38.0 %copy-start.1 = (f32[59,4096]{1,0:T(8,128)S(1)}, f32[59,4096]{1,0:T(8,128)}, u32[]{:S(2)}) copy-start(f32[59,4096]{1,0:T(8,128)} %refs_4_.4) | copy-start | bytes 2899972
  34.0 10.1 %copy-start.9 = (s32[1,2,2]{2,1,0:T(2,128)S(1)}, s32[1,2,2]{2,1,0:T(2,128)}, u32[]{:S(2)}) copy-start(s32[1,2,2]{2,1,0:T(2,128)} %refs_9_.3) | copy-start | bytes 52
  44.9 5.3 %collective-permute-start.1 = (f32[304,128]{1,0:T(8,128)S(1)}, f32[304,128]{1,0:T(8,128)S(1)}, u32[]{:S(2)}, u32[]{:S(2)}) collective-permute-start(f32[304,128]{1,0:T(8,128)S(1)} %shard_map.133.refs_0_), channel_id=1, source_target_pairs={{0,2},{1,3},{2,0},{3,1},{4,6},{5,7},{6,4},{7,5},{8,10},{9,11},{10,... | collective-permute-start | bytes 466952 | tf_op jit(solution)/shard_map/ppermute | solution.py:738
  46.5 3.7 %collective-permute-start = (f32[304,128]{1,0:T(8,128)S(1)}, f32[304,128]{1,0:T(8,128)S(1)}, u32[]{:S(2)}, u32[]{:S(2)}) collective-permute-start(f32[304,128]{1,0:T(8,128)S(1)} %shard_map.133.refs_0_), channel_id=1, source_target_pairs={{0,1},{1,0},{2,3},{3,2},{4,5},{5,4},{6,7},{7,6},{8,9},{9,8},{10,11... | collective-permute-start | bytes 466952 | tf_op jit(solution)/shard_map/ppermute | solution.py:738
  50.2 1.4 %collective-permute-start.2 = (f32[304,128]{1,0:T(8,128)S(1)}, f32[304,128]{1,0:T(8,128)S(1)}, u32[]{:S(2)}, u32[]{:S(2)}) collective-permute-start(f32[304,128]{1,0:T(8,128)S(1)} %collective-permute-done.1.refs_2_), channel_id=1, source_target_pairs={{0,1},{1,0},{2,3},{3,2},{4,5},{5,4},{6,7},{7,6},{8,9},{9,8},{10,11... | collective-permute-start | bytes 466952 | tf_op jit(solution)/shard_map/ppermute | solution.py:738
  51.6 1.2 %copy-start.3 = (f32[59,4096]{1,0:T(8,128)S(1)}, f32[59,4096]{1,0:T(8,128)}, u32[]{:S(2)}) copy-start(f32[59,4096]{1,0:T(8,128)} %refs_6_.2) | copy-start | bytes 2899972
  55.0 10.5 %copy-start.11 = (s32[2,1,4,4]{3,2,1,0:T(4,128)S(1)}, s32[2,1,4,4]{3,2,1,0:T(4,128)}, u32[]{:S(2)}) copy-start(s32[2,1,4,4]{3,2,1,0:T(4,128)} %refs_4_.5) | copy-start | bytes 388
  85.3 6.3 %collective-permute-start.4 = (f32[304,128]{1,0:T(8,128)S(1)}, f32[304,128]{1,0:T(8,128)S(1)}, u32[]{:S(2)}, u32[]{:S(2)}) collective-permute-start(f32[304,128]{1,0:T(8,128)S(1)} %shard_map.136.refs_0_), channel_id=1, source_target_pairs={{0,2},{1,3},{2,0},{3,1},{4,6},{5,7},{6,4},{7,5},{8,10},{9,11},{10,... | collective-permute-start | bytes 466952 | tf_op jit(solution)/shard_map/ppermute | solution.py:738
  86.9 8.5 %collective-permute-start.6 = (f32[3,59,256]{2,1,0:T(8,128)S(1)}, f32[3,59,256]{2,1,0:T(8,128)S(1)}, u32[]{:S(2)}, u32[]{:S(2)}) collective-permute-start(f32[3,59,256]{2,1,0:T(8,128)S(1)} %get-tuple-element.28), channel_id=1, source_target_pairs={{0,4},{4,8},{8,12},{12,16},{16,20},{20,24},{24,28},{28,0},{1,5},{5... | collective-permute-start | bytes 543752 | tf_op jit(solution)/shard_map/ppermute | solution.py:743
  87.6 8.3 %collective-permute-start.7 = (f32[3,59,256]{2,1,0:T(8,128)S(1)}, f32[3,59,256]{2,1,0:T(8,128)S(1)}, u32[]{:S(2)}, u32[]{:S(2)}) collective-permute-start(f32[3,59,256]{2,1,0:T(8,128)S(1)} %get-tuple-element.29), channel_id=1, source_target_pairs={{0,28},{4,0},{8,4},{12,8},{16,12},{20,16},{24,20},{28,24},{1,29},{... | collective-permute-start | bytes 543752 | tf_op jit(solution)/shard_map/ppermute | solution.py:743
  91.6 4.2 %collective-permute-start.3 = (f32[304,128]{1,0:T(8,128)S(1)}, f32[304,128]{1,0:T(8,128)S(1)}, u32[]{:S(2)}, u32[]{:S(2)}) collective-permute-start(f32[304,128]{1,0:T(8,128)S(1)} %shard_map.136.refs_0_), channel_id=1, source_target_pairs={{0,1},{1,0},{2,3},{3,2},{4,5},{5,4},{6,7},{7,6},{8,9},{9,8},{10,11... | collective-permute-start | bytes 466952 | tf_op jit(solution)/shard_map/ppermute | solution.py:738
  91.6 4.2 %collective-permute-start.5 = (f32[304,128]{1,0:T(8,128)S(1)}, f32[304,128]{1,0:T(8,128)S(1)}, u32[]{:S(2)}, u32[]{:S(2)}) collective-permute-start(f32[304,128]{1,0:T(8,128)S(1)} %collective-permute-done.4.refs_2_), channel_id=1, source_target_pairs={{0,1},{1,0},{2,3},{3,2},{4,5},{5,4},{6,7},{7,6},{8,9},{9,8},{10,11... | collective-permute-start | bytes 466952 | tf_op jit(solution)/shard_map/ppermute | solution.py:738

commit v5 on v4

--- a/solution.py
+++ b/solution.py
@@ -15,6 +15,7 @@
 DEPTH = 512
 SIDE = 16
 MIG_LANE = 64
+PLAN_LANE = 72
 CAM_ROWS = 16
 LOG2E = 1.4426950408889634
 
@@ -43,6 +44,7 @@
 bf16 = jnp.bfloat16
 VM = pl.BlockSpec(memory_space=pltpu.VMEM)
 SM = pl.BlockSpec(memory_space=pltpu.SMEM)
+ANY = pl.BlockSpec(memory_space=pl.ANY)
 
 
 def pitch(blocks):
@@ -100,7 +102,7 @@
     return rank
 
 
-def request_kernel(capacity, owner_ref, block_ref, migration_ref, out_ref, ranks_ref):
+def request_kernel(capacity, blocks, owner_ref, block_ref, migration_ref, out_ref):
     owners = out_ref.shape[0]
     tiles = owner_ref.shape[2]
     lane = lax.broadcasted_iota(jnp.int32, (owners, BLOCK), 1)
@@ -111,10 +113,13 @@
         names = [owner_ref[step, 0, t, j] for t in range(tiles) for j in range(LISTB)]
         for index in range(tiles * LISTB):
             rank = rank_of(names, index)
-            ranks_ref[step, index] = rank
             target = names[index] * BLOCK + step * capacity + rank
             block = block_ref[step, 0, index // LISTB, index % LISTB]
             message = jnp.where(place == target, block, message)
+            plan = (names[index] * capacity + rank) * blocks + block
+            message = jnp.where(
+                lane == PLAN_LANE + step * tiles * LISTB + index, plan, message
+            )
     for side in range(2):
         for j in range(MIGH):
             message = jnp.where(
@@ -252,19 +257,22 @@
 COL_ROWS = {0: (0, 9, 15), 1: (3, 12), 2: (6,)}
 
 
-def render_kernel(step, capacity, slots, final, *refs):
+def render_kernel(step, capacity, slots, blocks, final, *refs):
     if final:
         (
-            arrived, corner_ref, owner_ref, ranks_ref, block_ref, asked_ref, order_ref, target_ref, earlier_ref,
-            picture_ref, out_ref, *scratch,
+            arrived, corner_ref, asked_ref, order_ref, target_ref, earlier_ref,
+            rendered_ref, out_ref, picture_ref, leaving, *scratch,
         ) = refs
-        for other in range(ITERS - 1):
-            picture_ref[other] = earlier_ref[other]
+        store = pltpu.make_async_copy(picture_ref, rendered_ref.at[step, 0], leaving)
     else:
-        arrived, corner_ref, owner_ref, ranks_ref, order_ref, target_ref, picture_ref, out_ref, *scratch = refs
+        (
+            arrived, corner_ref, asked_ref, order_ref, target_ref,
+            rendered_ref, out_ref, *scratch,
+        ) = refs
+        picture_ref = rendered_ref.at[step, 0]
     onehots, sorted_ref, coeffs, shades_ref, sums_ref, grads_ref, *per_tile = scratch
     owners = arrived.shape[0]
-    tiles = owner_ref.shape[2]
+    tiles = order_ref.shape[2]
     lists = DEPTH // BLOCK
     segments = 8
     steps = DEPTH // segments
@@ -273,8 +281,15 @@
     features = pixel_features(32, 3)
     flat = pixel_features(16, 1)
 
-    names = [owner_ref[step, 0, t, j] for t in range(tiles) for j in range(LISTB)]
-    ranks = [ranks_ref[step, index] for index in range(tiles * LISTB)]
+    mine = lax.axis_index("row")
+    plans = [
+        asked_ref[mine, 0, PLAN_LANE + step * tiles * LISTB + index]
+        for index in range(tiles * LISTB)
+    ]
+    numbers = [lax.rem(plan, blocks) for plan in plans]
+    places = [lax.div(plan, blocks) for plan in plans]
+    ranks = [lax.rem(place, capacity) for place in places]
+    names = [lax.div(place, capacity) for place in places]
 
     order = order_ref[step, 0]
     order = jnp.concatenate([order] * (8 // tiles), axis=0)
@@ -373,7 +388,7 @@
         shades = dot(col_left, weight_h[...]) + dot(col_left, weight_m[...])
         shades = shades[0:3] + shades[3:6] + shades[6:9]
         for k in range(3):
-            picture_ref[step, 0, k, one, :] = shades[k : k + 1]
+            picture_ref[k, one, :] = shades[k : k + 1]
         error = shades - jnp.concatenate(
             [target_ref[step, 0, k, one, :] for k in range(3)], axis=0
         )
@@ -457,7 +472,7 @@
         for j in range(LISTB):
             name, rank = names[tile * LISTB + j], ranks[tile * LISTB + j]
             if final:
-                block = block_ref[step, 0, tile, j]
+                block = numbers[tile * LISTB + j]
                 hop = jnp.int32(0)
                 for k in range(MIGH):
                     goes_left = asked_ref[name, 0, MIG_LANE + k] == block
@@ -483,12 +498,16 @@
         passes[tile] = opening(tile, *buffers(tile))
     for tile in range(tiles):
         errors[tile] = picture(tile, passes[tile], *buffers(tile))
+    if final:
+        store.start()
     for tile in range(tiles):
         unsort_matrix(tile)
     for tile in range(tiles):
         closing(tile, passes[tile], errors[tile], *buffers(tile))
         if tile % 2 == 1 or tile == tiles - 1:
             finish(tile - tile % 2, 1 + tile % 2)
+    if final:
+        store.wait()
 
 
 def gather_kernel(step, capacity, slots, returned, asked_ref, migration_ref, camera_ref, out_ref):
@@ -733,6 +752,10 @@
     return [pltpu.with_memory_space_constraint(value, pltpu.VMEM) for value in values]
 
 
+def in_hbm(*values):
+    return [pltpu.with_memory_space_constraint(value, pltpu.HBM) for value in values]
+
+
 def swap(value, axis, offset):
     count = lax.axis_size(axis)
     return lax.ppermute(value, axis, [(i, i ^ offset) for i in range(count)])
@@ -778,16 +801,13 @@
     payload = 9 * blocks + CAM_ROWS
     cams = pltpu.VMEM((replicas, payload, BLOCK), f32)
     state = [shape(params.shape)] * 3
-    kept = [pltpu.VMEM(params.shape, f32)] * 3
-
-    lists, ranks = pl.pallas_call(
-        bind(request_kernel, capacity),
-        out_shape=[
-            shape((owners, 1, BLOCK), jnp.int32), shape((ITERS, requests), jnp.int32)
-        ],
+    kept = [pltpu.VMEM(params.shape, f32)] * 2 + [pltpu.HBM(params.shape, f32)]
+
+    lists = pl.pallas_call(
+        bind(request_kernel, capacity, blocks),
+        out_shape=shape((owners, 1, BLOCK), jnp.int32),
         in_specs=[SM, SM, SM],
-        out_specs=[VM, SM],
-        compiler_params=grant(8),
+        out_specs=VM,
     )(tile_owner, tile_block, migration)
     asked = row_exchange(lists)
     projected = pl.pallas_call(
@@ -796,12 +816,12 @@
         in_specs=[VM, SM],
         out_specs=VM,
         scratch_shapes=[dense],
-        compiler_params=grant(8),
+        compiler_params=grant(4),
     )(params, camera)
     message = shape((owners, up8(9 * capacity), BLOCK))
     outgoing = pl.pallas_call(
         bind(serve_kernel, capacity), out_shape=message, in_specs=[VM, SM], out_specs=VM,
-        compiler_params=grant(8),
+        compiler_params=grant(4),
     )(projected, asked)
 
     deep = pltpu.VMEM((DEPTH, PIX), f32)
@@ -822,46 +842,47 @@
         return pl.pallas_call(
             bind(gather_kernel, step, capacity, count),
             out_shape=pltpu.VMEM((payload, BLOCK), f32),
-            compiler_params=grant(8),
+            compiler_params=grant(4),
             in_specs=[VM, SM, SM, SM],
             out_specs=VM,
         )(*near_core(returned), asked, migration, camera)
 
     def second(arrived, pictures):
         return pl.pallas_call(
-            bind(render_kernel, 1, capacity, slots, True),
+            bind(render_kernel, 1, capacity, slots, blocks, True),
             out_shape=[pictures_shape, shape((owners, up8(9 * slots), BLOCK))],
-            in_specs=[VM, SM, SM, SM, SM, SM, VM, VM, VM],
-            out_specs=[VM, VM],
-            scratch_shapes=render_scratch,
-            compiler_params=grant(24),
+            in_specs=[VM, SM, SM, VM, VM, ANY],
+            out_specs=[ANY, VM],
+            input_output_aliases={5: 0},
+            scratch_shapes=[
+                pltpu.VMEM(photos.shape[2:], f32), pltpu.SemaphoreType.DMA, *render_scratch
+            ],
+            compiler_params=grant(17),
         )(
-            *near_core(arrived), corners, tile_owner, ranks, tile_block, asked, depth_order, photos,
-            pictures,
+            *near_core(arrived), *in_hbm(corners), asked, depth_order, photos, pictures
         )
 
     arrived = row_exchange(outgoing)
     pictures, back = pl.pallas_call(
-        bind(render_kernel, 0, capacity, capacity, False),
+        bind(render_kernel, 0, capacity, capacity, blocks, False),
         out_shape=[pictures_shape, shape((owners, up8(9 * capacity), BLOCK))],
-        in_specs=[VM, SM, SM, SM, VM, VM],
+        in_specs=[VM, SM, SM, VM, VM],
         out_specs=[VM, VM],
         scratch_shapes=render_scratch,
-        compiler_params=grant(24),
-    )(*near_core(arrived), corners, tile_owner, ranks, depth_order, photos)
+        compiler_params=grant(17),
+    )(*near_core(arrived), corners, asked, depth_order, photos)
     own = gather(0, capacity, row_exchange(back))
     near, far, cross = exchange(own)
-    leaving = pltpu.VMEM((3, P_SIZE, MIGH * BLOCK), f32)
+    leaving = pltpu.HBM((3, P_SIZE, MIGH * BLOCK), f32)
     current, moment_one, moment_two, outgoing, left, right = pl.pallas_call(
         bind(update_kernel, capacity),
         out_shape=kept + [shape((owners, up8(9 * capacity), BLOCK)), leaving, leaving],
         in_specs=[VM] * 7 + [SM] * 3,
         out_specs=[VM] * 6,
         scratch_shapes=[cams, dense, dense, table],
-        compiler_params=grant(16),
+        compiler_params=grant(12),
     )(
-        *near_core(own, near, far, cross, params, first_moment, second_moment),
-        camera, asked, migration,
+        *near_core(own, near, far, cross, params), *in_hbm(first_moment, second_moment), camera, asked, migration,
     )
     arrived = row_exchange(outgoing)
     below = turn(right, "row", 1)
@@ -877,7 +898,8 @@
         scratch_shapes=[cams, dense, dense],
         compiler_params=grant(16),
     )(
-        *near_core(own, near, far, cross, current, moment_one, moment_two, below, above), migration
+        *near_core(own, near, far, cross, current, moment_one), *in_hbm(moment_two, below, above),
+        *in_hbm(migration),
     )
     return current, moment_one, moment_two, jnp.swapaxes(pictures, 2, 3)
 

time: 99.7 us -> 101 us (1.013)
  Pallas kernels: 21.6 us -> 25 us
  local copies, waits for them, and re-layouts: 4.54 us -> 1.93 us
    unnamed x28 -> x22, local copies, waits for them, and re-layouts: 4.54 us -> 1.93 us
    pallas_call x1, Pallas kernels: 2.12 us -> 4.03 us  [local(): pl.pallas_call(bind(update_kernel, capacity), out_shape=kept + [shape((ow...]
where the time goes in v5:
time: 101 us; the launch traced here: 100 us
  blocking collectives  43.4 us (43%)
  Pallas kernels  25 us (25%)
  starting transfers between devices  15.8 us (16%)
  waiting for transfers between devices  13.2 us (13%)
  local copies, waits for them, and re-layouts  1.93 us (2%)
    all_to_all x4, blocking collectives, row_exchange(): return lax.all_to_all(value, 'row', split_axis=0, concat_axis=0, tiled=True)  43.4 us
    all_to_all x1, starting transfers between devices, row_exchange(): return lax.all_to_all(value, 'row', split_axis=0, concat_axis=0, tiled=True)  7.44 us
    pallas_call x1, Pallas kernels, second(): pl.pallas_call(bind(render_kernel, 1, capacity, slots, blocks, True), out...  6.05 us
    pallas_call x1, Pallas kernels, local(): pl.pallas_call(bind(render_kernel, 0, capacity, capacity, blocks, False),...  5.87 us
    ppermute x6, waiting for transfers between devices, swap(): return lax.ppermute(value, axis, [(i, i ^ offset) for i in range(count)])  5.12 us
    ppermute x2, starting transfers between devices, turn(): lax.ppermute(value, axis, [(i, (i + offset) % count) for i in range(count)])  4.72 us
    all_to_all x1, waiting for transfers between devices, row_exchange(): return lax.all_to_all(value, 'row', split_axis=0, concat_axis=0, tiled=True)  4.4 us
    pallas_call x1, Pallas kernels, local(): pl.pallas_call(final_kernel, out_shape=state, in_specs=[VM] * 9 + [SM], o...  4.2 us
  transfers between devices with their start and end apart: 9, of which 5 were waited for; matrix products, arithmetic and copies ran while one was open for 0% of the time, Pallas kernels for 1%

profile of v5, /device:TPU:0, one launch (start us, length us, event | category | flops | bytes accessed | tf_op | source)
XLA Modules:
  0.0 100.1 jit_solution(11012977970427794642)
XLA Ops:
  0.6 1.8 %shard_map.130 = s32[8,1,128]{2,1,0:T(1,128)} custom-call(s32[2,1,4,4]{3,2,1,0:T(4,128)} %refs_0_.1, s32[2,1,4,4]{3,2,1,0:T(4,128)} %refs_1_.1, s32[1,2,2]{2,1,0:T(2,128)} %refs_9_.3), custom_call_target="tpu_custom_call" | custom-call | tf_op jit(solution)/shard_map/pallas_call | solution.py:806
  2.4 7.4 %all-to-all-start = ((s32[8,1,128]{2,1,0:T(1,128)}), s32[8,1,128]{2,1,0:T(1,128)S(1)}, u32[]{:S(2)}, u32[]{:S(2)}) async-start(s32[8,1,128]{2,1,0:T(1,128)} %shard_map.130), calls=%async_computation | async-start | bytes 8192 | tf_op jit(solution)/shard_map/all_to_all | solution.py:777
  9.9 0.0 copy-start
  9.9 1.2 %copy-done = f32[59,4096]{1,0:T(8,128)S(1)} copy-done((f32[59,4096]{1,0:T(8,128)S(1)}, f32[59,4096]{1,0:T(8,128)}, u32[]{:S(2)}) %copy-start) | copy-done | bytes 966680
  11.1 0.8 shard_map.129.refs_0_
  11.9 0.0 copy-start.1
  11.9 4.4 %all-to-all-done.refs_1_.refs_2_.refs_8_ = s32[8,1,128]{2,1,0:T(1,128)S(1)} async-done(((s32[8,1,128]{2,1,0:T(1,128)}), s32[8,1,128]{2,1,0:T(1,128)S(1)}, u32[]{:S(2)}, u32[]{:S(2)}) %all-to-all-start) | async-done | bytes 4128 | tf_op jit(solution)/shard_map/all_to_all | solution.py:777
  16.3 0.7 shard_map.131
  16.9 10.0 %all_to_all.25.refs_0_ = f32[8,40,128]{2,1,0:T(8,128)S(1)} all-to-all(f32[8,40,128]{2,1,0:T(8,128)S(1)} %shard_map.131), channel_id=1, replica_groups=mesh['row'=8,'rep'=4] {'row'}, dimensions={0} | all-to-all | bytes 327680 | tf_op jit(solution)/shard_map/all_to_all | solution.py:777
  26.9 5.9 %shard_map.132 = (f32[2,1,3,4,256]{4,3,2,1,0:T(4,128)}, f32[8,40,128]{2,1,0:T(8,128)S(1)}) custom-call(f32[8,40,128]{2,1,0:T(8,128)S(1)} %all_to_all.25.refs_0_, f32[2,1,2,4]{3,2,1,0:T(2,128)S(1)} %bitcast.6, s32[8,1,128]{2,1,0:T(1,128)S(1)} %all-to-all-done.refs_1_.refs_2_.refs_8_, s32[2,1,4,512]{3,2,1,0:T(4,128)S(1)} %copy-done.3, ...), custom_call_target="tpu_custom_call" | custom-call | tf_op jit(solution)/shard_map/pallas_call | solution.py:866
  32.8 10.1 %all_to_all.26.refs_0_ = f32[8,40,128]{2,1,0:T(8,128)S(1)} all-to-all(f32[8,40,128]{2,1,0:T(8,128)S(1)} %get-tuple-element.17), channel_id=1, replica_groups=mesh['row'=8,'rep'=4] {'row'}, dimensions={0} | all-to-all | bytes 327680 | tf_op jit(solution)/shard_map/all_to_all | solution.py:777
  42.9 0.8 shard_map.133.refs_0_
  43.7 1.6 %collective-permute-start.1 = (f32[304,128]{1,0:T(8,128)S(1)}, f32[304,128]{1,0:T(8,128)S(1)}, u32[]{:S(2)}, u32[]{:S(2)}) collective-permute-start(f32[304,128]{1,0:T(8,128)S(1)} %shard_map.133.refs_0_), channel_id=1, source_target_pairs={{0,2},{1,3},{2,0},{3,1},{4,6},{5,7},{6,4},{7,5},{8,10},{9,11},{10,... | collective-permute-start | bytes 466952 | tf_op jit(solution)/shard_map/ppermute | solution.py:761
  45.2 0.0 collective-permute-start
  45.2 3.7 %collective-permute-done.1.refs_2_ = f32[304,128]{1,0:T(8,128)S(1)} collective-permute-done((f32[304,128]{1,0:T(8,128)S(1)}, f32[304,128]{1,0:T(8,128)S(1)}, u32[]{:S(2)}, u32[]{:S(2)}) %collective-permute-start.1) | collective-permute-done | bytes 155680 | tf_op jit(solution)/shard_map/ppermute | solution.py:761
  49.0 1.4 %collective-permute-done.2.refs_3_ = f32[304,128]{1,0:T(8,128)S(1)} collective-permute-done((f32[304,128]{1,0:T(8,128)S(1)}, f32[304,128]{1,0:T(8,128)S(1)}, u32[]{:S(2)}, u32[]{:S(2)}) %collective-permute-start.2) | collective-permute-done | bytes 155680 | tf_op jit(solution)/shard_map/ppermute | solution.py:761
  50.4 4.0 %shard_map.134 = (f32[59,4096]{1,0:T(8,128)S(1)}, f32[59,4096]{1,0:T(8,128)S(1)}, f32[59,4096]{1,0:T(8,128)}, f32[8,40,128]{2,1,0:T(8,128)S(1)}, f32[3,59,256]{2,1,0:T(8,128)}, /*index=5*/f32[3,59,256]{2,1,0:T(8,128)}) custom-call(f32[304,128]{1,0:T(8,128)S(1)} %shard_map.133.refs_0_, f32[304,128]{1,0:T(8,128)S(1)} %collective-permute-done.refs_1_, ...), custom_call_target="tpu_custom_call" | custom-call | tf_op jit(solution)/shard_map/pallas_call | solution.py:877
  54.4 10.4 %all_to_all.27.refs_0_ = f32[8,40,128]{2,1,0:T(8,128)S(1)} all-to-all(f32[8,40,128]{2,1,0:T(8,128)S(1)} %get-tuple-element.18), channel_id=1, replica_groups=mesh['row'=8,'rep'=4] {'row'}, dimensions={0} | all-to-all | bytes 327680 | tf_op jit(solution)/shard_map/all_to_all | solution.py:777
  64.8 6.1 %shard_map.135 = (f32[2,1,3,4,256]{4,3,2,1,0:T(4,128)}, f32[8,72,128]{2,1,0:T(8,128)S(1)}) custom-call(f32[8,40,128]{2,1,0:T(8,128)S(1)} %all_to_all.27.refs_0_, f32[2,1,2,4]{3,2,1,0:T(2,128)} %bitcast.5, s32[8,1,128]{2,1,0:T(1,128)S(1)} %all-to-all-done.refs_1_.refs_2_.refs_8_, s32[2,1,4,512]{3,2,1,0:T(4,128)S(1)} %copy-done.3, ...), custom_call_target="tpu_custom_call", output_to_operand_aliasing={{0}: (5, {})} | custom-call | tf_op jit(solution)/shard_map/pallas_call | solution.py:851
  70.9 12.9 %all_to_all.28.refs_0_ = f32[8,72,128]{2,1,0:T(8,128)S(1)} all-to-all(f32[8,72,128]{2,1,0:T(8,128)S(1)} %get-tuple-element.20), channel_id=1, replica_groups=mesh['row'=8,'rep'=4] {'row'}, dimensions={0} | all-to-all | bytes 589824 | tf_op jit(solution)/shard_map/all_to_all | solution.py:777
  83.8 0.9 shard_map.136.refs_0_
  84.7 1.6 %collective-permute-start.4 = (f32[304,128]{1,0:T(8,128)S(1)}, f32[304,128]{1,0:T(8,128)S(1)}, u32[]{:S(2)}, u32[]{:S(2)}) collective-permute-start(f32[304,128]{1,0:T(8,128)S(1)} %shard_map.136.refs_0_), channel_id=1, source_target_pairs={{0,2},{1,3},{2,0},{3,1},{4,6},{5,7},{6,4},{7,5},{8,10},{9,11},{10,... | collective-permute-start | bytes 466952 | tf_op jit(solution)/shard_map/ppermute | solution.py:761
  86.2 0.7 collective-permute-start.6
  86.9 4.0 %collective-permute-start.7 = (f32[3,59,256]{2,1,0:T(8,128)S(1)}, f32[3,59,256]{2,1,0:T(8,128)S(1)}, u32[]{:S(2)}, u32[]{:S(2)}) collective-permute-start(f32[3,59,256]{2,1,0:T(8,128)S(1)} %copy-done.9), channel_id=1, source_target_pairs={{0,28},{4,0},{8,4},{12,8},{16,12},{20,16},{24,20},{28,24},{1,29},{... | collective-permute-start | bytes 543752 | tf_op jit(solution)/shard_map/ppermute | solution.py:766
  91.0 0.0 collective-permute-start.3
  91.0 0.5 collective-permute-start.5
  91.5 3.2 %collective-permute-done.6.refs_7_ = f32[3,59,256]{2,1,0:T(8,128)S(1)} collective-permute-done((f32[3,59,256]{2,1,0:T(8,128)S(1)}, f32[3,59,256]{2,1,0:T(8,128)S(1)}, u32[]{:S(2)}, u32[]{:S(2)}) %collective-permute-start.6) | collective-permute-done | bytes 181280 | tf_op jit(solution)/shard_map/ppermute | solution.py:766
  94.7 0.5 collective-permute-done.7.refs_8_
  95.2 0.0 collective-permute-done.3.refs_1_
  95.2 0.2 copy-done.7
  95.4 0.5 copy-done.8
  95.9 4.2 %shard_map.137 = (f32[59,4096]{1,0:T(8,128)}, f32[59,4096]{1,0:T(8,128)}, f32[59,4096]{1,0:T(8,128)}) custom-call(f32[304,128]{1,0:T(8,128)S(1)} %shard_map.136.refs_0_, f32[304,128]{1,0:T(8,128)S(1)} %collective-permute-done.3.refs_1_, f32[304,128]{1,0:T(8,128)S(1)} %collective-permute-done.4.refs_2_, f32[304,128]{1,0:T(8,128)S(1)} %collective-permute-done.5.refs_3_, ...), custom_call_target="tpu_custom_call" | custom-call | tf_op jit(solution)/shard_map/pallas_call | solution.py:893
  (21 shorter events, 0.0 us)
Async XLA Ops:
  2.4 7.4 %copy-start.5 = (f32[2,1,11]{2,1,0:T(1,128)S(1)}, f32[2,1,11]{2,1,0:T(1,128)}, u32[]{:S(2)}) copy-start(f32[2,1,11]{2,1,0:T(1,128)} %refs_3_.7) | copy-start | bytes 268
  2.4 13.9 %all-to-all-start = ((s32[8,1,128]{2,1,0:T(1,128)}), s32[8,1,128]{2,1,0:T(1,128)S(1)}, u32[]{:S(2)}, u32[]{:S(2)}) async-start(s32[8,1,128]{2,1,0:T(1,128)} %shard_map.130), calls=%async_computation | async-start | bytes 8192 | tf_op jit(solution)/shard_map/all_to_all | solution.py:777
  9.9 1.2 %copy-start = (f32[59,4096]{1,0:T(8,128)S(1)}, f32[59,4096]{1,0:T(8,128)}, u32[]{:S(2)}) copy-start(f32[59,4096]{1,0:T(8,128)} %refs_4_.1) | copy-start | bytes 2899972
  11.1 15.8 %copy-start.2 = (f32[2,1,4,3,256]{4,2,3,1,0:T(4,128)S(1)}, f32[2,1,4,3,256]{4,2,3,1,0:T(4,128)}, u32[]{:S(2)}) copy-start(f32[2,1,4,3,256]{4,2,3,1,0:T(4,128)} %param.18) | copy-start | bytes 73732
  11.1 15.8 %copy-start.3 = (s32[2,1,4,512]{3,2,1,0:T(4,128)S(1)}, s32[2,1,4,512]{3,2,1,0:T(4,128)}, u32[]{:S(2)}) copy-start(s32[2,1,4,512]{3,2,1,0:T(4,128)} %refs_3_.6) | copy-start | bytes 49156
  11.1 15.8 %copy-start.6 = (f32[2,1,4,2]{2,3,1,0:T(2,128)S(1)}, f32[2,1,4,2]{2,3,1,0:T(2,128)}, u32[]{:S(2)}) copy-start(f32[2,1,4,2]{2,3,1,0:T(2,128)} %param.14) | copy-start | bytes 196
  11.9 38.5 %copy-start.1 = (f32[59,4096]{1,0:T(8,128)S(1)}, f32[59,4096]{1,0:T(8,128)}, u32[]{:S(2)}) copy-start(f32[59,4096]{1,0:T(8,128)} %refs_4_.1) | copy-start | bytes 2899972
  32.8 10.1 %copy-start.4 = (s32[1,2,2]{2,1,0:T(2,128)S(1)}, s32[1,2,2]{2,1,0:T(2,128)}, u32[]{:S(2)}) copy-start(s32[1,2,2]{2,1,0:T(2,128)} %refs_9_.3) | copy-start | bytes 52
  43.7 5.3 %collective-permute-start.1 = (f32[304,128]{1,0:T(8,128)S(1)}, f32[304,128]{1,0:T(8,128)S(1)}, u32[]{:S(2)}, u32[]{:S(2)}) collective-permute-start(f32[304,128]{1,0:T(8,128)S(1)} %shard_map.133.refs_0_), channel_id=1, source_target_pairs={{0,2},{1,3},{2,0},{3,1},{4,6},{5,7},{6,4},{7,5},{8,10},{9,11},{10,... | collective-permute-start | bytes 466952 | tf_op jit(solution)/shard_map/ppermute | solution.py:761
  45.2 3.7 %collective-permute-start = (f32[304,128]{1,0:T(8,128)S(1)}, f32[304,128]{1,0:T(8,128)S(1)}, u32[]{:S(2)}, u32[]{:S(2)}) collective-permute-start(f32[304,128]{1,0:T(8,128)S(1)} %shard_map.133.refs_0_), channel_id=1, source_target_pairs={{0,1},{1,0},{2,3},{3,2},{4,5},{5,4},{6,7},{7,6},{8,9},{9,8},{10,11... | collective-permute-start | bytes 466952 | tf_op jit(solution)/shard_map/ppermute | solution.py:761
  49.0 1.4 %collective-permute-start.2 = (f32[304,128]{1,0:T(8,128)S(1)}, f32[304,128]{1,0:T(8,128)S(1)}, u32[]{:S(2)}, u32[]{:S(2)}) collective-permute-start(f32[304,128]{1,0:T(8,128)S(1)} %collective-permute-done.1.refs_2_), channel_id=1, source_target_pairs={{0,1},{1,0},{2,3},{3,2},{4,5},{5,4},{6,7},{7,6},{8,9},{9,8},{10,11... | collective-permute-start | bytes 466952 | tf_op jit(solution)/shard_map/ppermute | solution.py:761
  83.8 2.4 %copy-start.10 = (f32[3,59,256]{2,1,0:T(8,128)S(1)}, f32[3,59,256]{2,1,0:T(8,128)}, u32[]{:S(2)}) copy-start(f32[3,59,256]{2,1,0:T(8,128)} %get-tuple-element.24) | copy-start | bytes 543748
  83.8 3.1 %copy-start.9 = (f32[3,59,256]{2,1,0:T(8,128)S(1)}, f32[3,59,256]{2,1,0:T(8,128)}, u32[]{:S(2)}) copy-start(f32[3,59,256]{2,1,0:T(8,128)} %get-tuple-element.25) | copy-start | bytes 543748
  84.7 6.3 %collective-permute-start.4 = (f32[304,128]{1,0:T(8,128)S(1)}, f32[304,128]{1,0:T(8,128)S(1)}, u32[]{:S(2)}, u32[]{:S(2)}) collective-permute-start(f32[304,128]{1,0:T(8,128)S(1)} %shard_map.136.refs_0_), channel_id=1, source_target_pairs={{0,2},{1,3},{2,0},{3,1},{4,6},{5,7},{6,4},{7,5},{8,10},{9,11},{10,... | collective-permute-start | bytes 466952 | tf_op jit(solution)/shard_map/ppermute | solution.py:761
  86.2 8.5 %collective-permute-start.6 = (f32[3,59,256]{2,1,0:T(8,128)S(1)}, f32[3,59,256]{2,1,0:T(8,128)S(1)}, u32[]{:S(2)}, u32[]{:S(2)}) collective-permute-start(f32[3,59,256]{2,1,0:T(8,128)S(1)} %copy-done.10), channel_id=1, source_target_pairs={{0,4},{4,8},{8,12},{12,16},{16,20},{20,24},{24,28},{28,0},{1,5},{5... | collective-permute-start | bytes 543752 | tf_op jit(solution)/shard_map/ppermute | solution.py:766
  86.9 8.2 %collective-permute-start.7 = (f32[3,59,256]{2,1,0:T(8,128)S(1)}, f32[3,59,256]{2,1,0:T(8,128)S(1)}, u32[]{:S(2)}, u32[]{:S(2)}) collective-permute-start(f32[3,59,256]{2,1,0:T(8,128)S(1)} %copy-done.9), channel_id=1, source_target_pairs={{0,28},{4,0},{8,4},{12,8},{16,12},{20,16},{24,20},{28,24},{1,29},{... | collective-permute-start | bytes 543752 | tf_op jit(solution)/shard_map/ppermute | solution.py:766
  91.0 4.2 %collective-permute-start.3 = (f32[304,128]{1,0:T(8,128)S(1)}, f32[304,128]{1,0:T(8,128)S(1)}, u32[]{:S(2)}, u32[]{:S(2)}) collective-permute-start(f32[304,128]{1,0:T(8,128)S(1)} %shard_map.136.refs_0_), channel_id=1, source_target_pairs={{0,1},{1,0},{2,3},{3,2},{4,5},{5,4},{6,7},{7,6},{8,9},{9,8},{10,11... | collective-permute-start | bytes 466952 | tf_op jit(solution)/shard_map/ppermute | solution.py:761
  91.0 4.2 %collective-permute-start.5 = (f32[304,128]{1,0:T(8,128)S(1)}, f32[304,128]{1,0:T(8,128)S(1)}, u32[]{:S(2)}, u32[]{:S(2)}) collective-permute-start(f32[304,128]{1,0:T(8,128)S(1)} %collective-permute-done.4.refs_2_), channel_id=1, source_target_pairs={{0,1},{1,0},{2,3},{3,2},{4,5},{5,4},{6,7},{7,6},{8,9},{9,8},{10,11... | collective-permute-start | bytes 466952 | tf_op jit(solution)/shard_map/ppermute | solution.py:761
  94.7 0.7 copy-start.7
  95.2 0.7 copy-start.8
